TPU v7x, 32 devices: a whole 2x2x4 slice. The times are simulated.
32 devices in a mesh: dp: 8 (over z, x), seq: 4 (over y, core).
Axes of the slice: x: 2, y: 2, z: 4, core: 2. Of those that a mesh axis runs over, the one named last changes fastest.
Arguments:
- queries: bfloat16 [8, 512, 2048], P('dp', 'seq'), may hold values from -72 to 72
- hit_keys: bfloat16 [8, 512, 2048], P('dp', 'seq'), may hold values from -12 to 12
- hit_values: bfloat16 [8, 512, 2048], P('dp', 'seq'), may hold values from -6 to 6
- hit_counts: int32 [8], P('dp'), may hold values from 128 to 512, as said below
- master_weight: float32 [8, 256, 2048], P('dp', None, 'seq'), may hold values from -0.5 to 0.5
- first_moment: float32 [8, 256, 2048], P('dp', None, 'seq'), may hold values from -4 to 4
- second_moment: float32 [8, 256, 2048], P('dp', None, 'seq'), may hold values from 0.1 to 4
- gradient: float32 [8, 256, 2048], P('dp', None, 'seq'), may hold values from -6 to 6
- owner_bucket: int32 [8], replicated, may hold values from 0 to 7, each once
Outputs:
- projected: bfloat16 [8, 512, 2048], P('dp', 'seq')
- new_master: float32 [8, 256, 2048], P('dp', None, 'seq')
- new_first: float32 [8, 256, 2048], P('dp', None, 'seq')
- new_second: float32 [8, 256, 2048], P('dp', None, 'seq')
Inputs may be any that keep to these rules, and one draw needn't show every extreme that they name: The valid hits of event e are its first hit_counts[e] slots; some event is full. `owner_bucket`: each bucket is held by exactly one owner.
All inputs are finite; a program needn't handle non-finite values.
Results may differ from a plain program's by a relative error of at most 0.0063.
Values may be sent and summed in bfloat16 or wider, within the bound.
No kernel may reach another device: no remote copies, remote signals or barrier semaphores. Data moves between devices by JAX's collectives and lax.ppermute only.
A program may use at most 64 MiB of HBM per device.

v0:
```python
import jax
import jax.numpy as jnp
from jax import lax
from jax.sharding import PartitionSpec as P

HEAD_DIM = 128


beta_one = 0.9
beta_two = 0.999
learn_rate = 0.003
weight_decay = 0.1
epsilon = 1e-08
step_count = 10.0
block_rows = 512


def adam_update(master_weight, first_moment, second_moment, gradient):
    new_first = beta_one * first_moment + (1.0 - beta_one) * gradient
    new_second = beta_two * second_moment + (1.0 - beta_two) * gradient * gradient
    first_hat = new_first / (1.0 - beta_one**step_count)
    second_hat = new_second / (1.0 - beta_two**step_count)
    new_master = master_weight - learn_rate * (
        first_hat / (jnp.sqrt(second_hat) + epsilon) + weight_decay * master_weight
    )
    return (new_master, new_first, new_second)


def attend_head(head_query, head_keys, head_values, count):
    length = head_query.shape[0]
    block = min(block_rows, length)
    scale = head_query.shape[1] ** (-0.5)
    valid = lax.broadcasted_iota(jnp.int32, (1, length), 1) < count

    def one_block(rows):
        scores = (
            lax.dot_general(
                rows, head_keys, (((1,), (1,)), ((), ())), preferred_element_type=jnp.float32
            )
            * scale
        )
        scores = jnp.where(valid, scores, -jnp.inf)
        top = jnp.max(scores, axis=1, keepdims=True)
        expo = jnp.exp(scores - top)
        weights = (expo / jnp.sum(expo, axis=1, keepdims=True)).astype(jnp.bfloat16)
        return jnp.dot(weights, head_values, preferred_element_type=jnp.float32).astype(
            jnp.bfloat16
        )

    blocks = head_query.reshape(length // block, block, head_query.shape[1])
    return lax.map(one_block, blocks).reshape(length, head_query.shape[1])


def body(
    queries,
    hit_keys,
    hit_values,
    hit_counts,
    master_weight,
    first_moment,
    second_moment,
    gradient,
    owner_bucket,
):
    new_master, new_first, new_second = adam_update(
        master_weight, first_moment, second_moment, gradient
    )
    weight_half = new_master.astype(jnp.bfloat16)
    groups = lax.axis_size("seq")
    owners = lax.axis_size("dp")
    tok_rows = queries.shape[1]
    width = queries.shape[2]
    per_group = width // groups
    heads_here = per_group // HEAD_DIM
    count = hit_counts[0]
    matches = owner_bucket[:, None] == jnp.arange(owners, dtype=jnp.int32)[None, :]
    inverse = jnp.sum(jnp.where(matches, jnp.arange(owners, dtype=jnp.int32)[:, None], 0), axis=0)

    def split_heads(array):
        return array.reshape(1, tok_rows, groups, heads_here, HEAD_DIM)

    query_part = lax.all_to_all(
        split_heads(queries), "seq", split_axis=2, concat_axis=1, tiled=True
    )
    keys_part = lax.all_to_all(
        split_heads(hit_keys), "seq", split_axis=2, concat_axis=1, tiled=True
    )
    values_part = lax.all_to_all(
        split_heads(hit_values), "seq", split_axis=2, concat_axis=1, tiled=True
    )
    n_heads = query_part.shape[3]

    def one_head(index):
        head_query = lax.dynamic_index_in_dim(query_part, index, 3, keepdims=False)[0, :, 0, :]
        head_keys = lax.dynamic_index_in_dim(keys_part, index, 3, keepdims=False)[0, :, 0, :]
        head_values = lax.dynamic_index_in_dim(values_part, index, 3, keepdims=False)[0, :, 0, :]
        return attend_head(head_query, head_keys, head_values, count)

    outputs = lax.map(one_head, jnp.arange(n_heads, dtype=jnp.int32))
    attended = jnp.moveaxis(outputs, 0, 1)[None, :, None, :, :]
    returned = lax.all_to_all(attended, "seq", split_axis=1, concat_axis=2, tiled=True)
    rows_in = returned.reshape(tok_rows, width)
    owned = lax.all_gather(weight_half, "dp", axis=0, tiled=True)
    full = lax.all_gather(owned, "seq", axis=2, tiled=True)
    projection = jnp.take(full, inverse, axis=0).reshape(width, width)
    total = jnp.dot(rows_in, projection, preferred_element_type=jnp.float32)
    projected = total.astype(jnp.bfloat16)[None]
    return (projected, new_master, new_first, new_second)


def solution(mesh):
    return jax.shard_map(
        body,
        mesh=mesh,
        in_specs=(
            P("dp", "seq", None),
            P("dp", "seq", None),
            P("dp", "seq", None),
            P("dp"),
            P("dp", None, "seq"),
            P("dp", None, "seq"),
            P("dp", None, "seq"),
            P("dp", None, "seq"),
            P(),
        ),
        out_specs=(
            P("dp", "seq", None),
            P("dp", None, "seq"),
            P("dp", None, "seq"),
            P("dp", None, "seq"),
        ),
        check_vma=False,
    )
```

profile of v0, /device:TPU:0, one launch (start us, length us, event | category | flops | bytes accessed | tf_op | source)
XLA Modules:
  0.0 175.6 jit_solution(9775890406966182870)
XLA Ops:
  7.2 3.1 %fusion.15 = (bf16[1,256,512]{2,1,0:T(8,128)(2,1)}, f32[1,256,512]{2,1,0:T(8,128)}, f32[1,256,512]{2,1,0:T(8,128)}, f32[1,256,512]{2,1,0:T(8,128)}) fusion(f32[1,256,512]{2,1,0:T(8,128)} %param.15, f32[1,256,512]{2,1,0:T(8,128)} %param.18, f32[1,256,512]{2,1,0:T(8,128)} %param.16, f32[1,256,512]{2,1,0:T(8,128)} %param.17), kind=kLoop, calls=%fused_computation.33 | loop fusion | flops 2097152 | bytes 3932160 | tf_op jit(solution)/shard_map/convert_element_type | solution.py:68
  10.4 52.3 %all-gather.3.cloned.1.call-done = bf16[8,256,512]{2,1,0:T(8,128)(2,1)} async-done(((bf16[1,256,512]{2,1,0:T(8,128)(2,1)}), bf16[8,256,512]{2,1,0:T(8,128)(2,1)}) %all-gather.3.cloned.1.call-update) | async-done | bytes 2097168 | tf_op jit(solution)/shard_map/all_gather | solution.py:103
  62.8 1.3 copy.41
  64.1 1.0 copy.42
  65.1 3.5 %all-to-all-start.1 = ((bf16[1,128,4,4,128]{4,1,3,0,2:T(8,128)(2,1)}), bf16[1,128,4,4,128]{4,1,3,0,2:T(8,128)(2,1)S(1)}, u32[]{:S(2)}, u32[]{:S(2)}) async-start(bf16[1,128,4,4,128]{4,1,3,0,2:T(8,128)(2,1)} %copy.42), calls=%async_computation.1 | async-start | bytes 1048576 | tf_op jit(solution)/shard_map/all_to_all | solution.py:85
  68.9 1.0 copy.45
  69.9 10.8 %all-to-all-done.1 = bf16[1,128,4,4,128]{4,1,3,0,2:T(8,128)(2,1)S(1)} async-done(((bf16[1,128,4,4,128]{4,1,3,0,2:T(8,128)(2,1)}), bf16[1,128,4,4,128]{4,1,3,0,2:T(8,128)(2,1)S(1)}, u32[]{:S(2)}, u32[]{:S(2)}) %all-to-all-start.1) | async-done | bytes 524320 | tf_op jit(solution)/shard_map/all_to_all | solution.py:85
  80.7 3.5 %all-to-all-start.2 = ((bf16[1,128,4,4,128]{4,1,3,0,2:T(8,128)(2,1)}), bf16[1,128,4,4,128]{4,1,3,0,2:T(8,128)(2,1)S(1)}, u32[]{:S(2)}, u32[]{:S(2)}) async-start(bf16[1,128,4,4,128]{4,1,3,0,2:T(8,128)(2,1)} %copy.45), calls=%async_computation.2 | async-start | bytes 1048576 | tf_op jit(solution)/shard_map/all_to_all | solution.py:88
  84.5 1.0 copy.39
  85.5 13.4 %all-to-all-done.2 = bf16[1,128,4,4,128]{4,1,3,0,2:T(8,128)(2,1)S(1)} async-done(((bf16[1,128,4,4,128]{4,1,3,0,2:T(8,128)(2,1)}), bf16[1,128,4,4,128]{4,1,3,0,2:T(8,128)(2,1)S(1)}, u32[]{:S(2)}, u32[]{:S(2)}) %all-to-all-start.2) | async-done | bytes 524320 | tf_op jit(solution)/shard_map/all_to_all | solution.py:88
  99.0 3.5 %all-to-all-start = ((bf16[1,128,4,4,128]{4,1,3,0,2:T(8,128)(2,1)}), bf16[1,128,4,4,128]{4,1,3,0,2:T(8,128)(2,1)S(1)}, u32[]{:S(2)}, u32[]{:S(2)}) async-start(bf16[1,128,4,4,128]{4,1,3,0,2:T(8,128)(2,1)} %copy.39), calls=%async_computation | async-start | bytes 1048576 | tf_op jit(solution)/shard_map/all_to_all | solution.py:82
  102.6 14.5 %all-to-all-done = bf16[1,128,4,4,128]{4,1,3,0,2:T(8,128)(2,1)S(1)} async-done(((bf16[1,128,4,4,128]{4,1,3,0,2:T(8,128)(2,1)}), bf16[1,128,4,4,128]{4,1,3,0,2:T(8,128)(2,1)S(1)}, u32[]{:S(2)}, u32[]{:S(2)}) %all-to-all-start) | async-done | bytes 524320 | tf_op jit(solution)/shard_map/all_to_all | solution.py:82
  117.2 16.6 %while.10 = (s32[]{:T(128)}, bf16[4,512,128]{2,1,0:T(8,128)(2,1)S(1)}, s32[]{:T(128)}, s32[4]{0:T(128)S(1)}, bf16[1,512,1,4,128]{4,1,3,2,0:T(8,128)(2,1)S(1)}, /...) while((s32[]{:T(128)}, ...), condition=%wide.region_3.4_spmd, body=%wide.region_0.3_spmd.sunk | while | flops 136379904 | bytes 3682463 | solution.py:99
  117.3 0.6 dynamic_slice.40
  119.8 0.7 iota_compare_fusion.3
  121.0 0.4 fusion.27
  121.4 0.6 dynamic_slice.40
  123.9 0.7 iota_compare_fusion.3
  125.1 0.4 fusion.27
  125.6 0.6 dynamic_slice.40
  128.1 0.7 iota_compare_fusion.3
  128.8 0.3 fusion.25
  129.3 0.4 fusion.27
  129.7 0.6 dynamic_slice.40
  132.3 0.7 iota_compare_fusion.3
  133.4 0.4 fusion.27
  133.9 1.2 copy.51
  135.1 3.5 %all-to-all-start.3 = ((bf16[1,512,1,4,128]{4,3,2,0,1:T(4,128)(2,1)}), bf16[1,512,1,4,128]{4,3,2,0,1:T(4,128)(2,1)S(1)}, u32[]{:S(2)}, u32[]{:S(2)}) async-start(bf16[1,512,1,4,128]{4,3,2,0,1:T(4,128)(2,1)} %bitcast.54), calls=%async_computation.3 | async-start | bytes 1048576 | tf_op jit(solution)/shard_map/all_to_all | solution.py:101
  138.6 8.8 %all-to-all-done.3 = bf16[1,512,1,4,128]{4,3,2,0,1:T(4,128)(2,1)S(1)} async-done(((bf16[1,512,1,4,128]{4,3,2,0,1:T(4,128)(2,1)}), bf16[1,512,1,4,128]{4,3,2,0,1:T(4,128)(2,1)S(1)}, u32[]{:S(2)}, u32[]{:S(2)}) %all-to-all-start.3) | async-done | bytes 524320 | tf_op jit(solution)/shard_map/all_to_all | solution.py:101
  147.8 8.1 %gather_fusion = bf16[8,256,2048]{2,1,0:T(8,128)(2,1)} fusion(bf16[8,256,2048]{2,1,0:T(8,128)(2,1)} %all-gather.5.cloned.1.call-done, s32[1024]{0:T(1024)S(1)} %pad_clamp_fusion), kind=kCustom, calls=%fused_computation | custom fusion | bytes 16777248 | tf_op jit(solution)/shard_map/jit(_take)/gather | solution.py:105
  155.8 7.5 %broadcast_select_fusion = bf16[8,256,2048]{2,1,0:T(8,128)(2,1)} fusion(bf16[8,256,2048]{2,1,0:T(8,128)(2,1)} %gather_fusion, pred[8]{0:T(512)(128)(4,1)S(1)} %compare_and_fusion), kind=kLoop, calls=%fused_computation.18 | loop fusion | flops 4194304 | bytes 16777224 | tf_op jit(solution)/shard_map/jit(_take)/select_n | solution.py:105
  163.3 5.5 %fusion.12 = bf16[1,128,2048]{2,1,0:T(8,128)(2,1)} fusion(bf16[128,2048]{0,1:T(8,128)(2,1)S(1)} %bitcast.66, bf16[2048,2048]{1,0:T(8,128)(2,1)} %bitcast.65), kind=kOutput, calls=%fused_computation.20 | convolution fusion | flops 1074003968 | bytes 9437184 | tf_op jit(solution)/shard_map/dot_general | solution.py:106
  (31 shorter events, 3.0 us)
Async XLA Ops:
  7.2 61.4 %copy-start = (bf16[1,128,2048]{2,1,0:T(8,128)(2,1)S(1)}, bf16[1,128,2048]{2,1,0:T(8,128)(2,1)}, u32[]{:S(2)}) copy-start(bf16[1,128,2048]{2,1,0:T(8,128)(2,1)} %param.13) | copy-start | bytes 1572868
  7.2 77.0 %copy-start.1 = (bf16[1,128,2048]{2,1,0:T(8,128)(2,1)S(1)}, bf16[1,128,2048]{2,1,0:T(8,128)(2,1)}, u32[]{:S(2)}) copy-start(bf16[1,128,2048]{2,1,0:T(8,128)(2,1)} %param.11) | copy-start | bytes 1572868
  7.2 95.3 %copy-start.2 = (s32[8]{0:T(128)S(1)}, s32[8]{0:T(128)}, u32[]{:S(2)}) copy-start(s32[8]{0:T(128)} %param.19) | copy-start | bytes 100
  7.2 55.6 %all-gather.3.cloned.1.call-start = ((), (), s32[]{:S(2)}) async-start(), calls=%async_computation.4 | async-start | bytes 2359296 | tf_op jit(solution)/shard_map/all_gather | solution.py:103
  10.4 137.4 %all-gather.5.cloned.1.call-start = ((), (), s32[]{:S(2)}) async-start(), calls=%async_computation.5 | async-start | bytes 10485760 | tf_op jit(solution)/shard_map/all_gather | solution.py:104
  65.1 15.6 %all-to-all-start.1 = ((bf16[1,128,4,4,128]{4,1,3,0,2:T(8,128)(2,1)}), bf16[1,128,4,4,128]{4,1,3,0,2:T(8,128)(2,1)S(1)}, u32[]{:S(2)}, u32[]{:S(2)}) async-start(bf16[1,128,4,4,128]{4,1,3,0,2:T(8,128)(2,1)} %copy.42), calls=%async_computation.1 | async-start | bytes 1048576 | tf_op jit(solution)/shard_map/all_to_all | solution.py:85
  80.7 18.2 %all-to-all-start.2 = ((bf16[1,128,4,4,128]{4,1,3,0,2:T(8,128)(2,1)}), bf16[1,128,4,4,128]{4,1,3,0,2:T(8,128)(2,1)S(1)}, u32[]{:S(2)}, u32[]{:S(2)}) async-start(bf16[1,128,4,4,128]{4,1,3,0,2:T(8,128)(2,1)} %copy.45), calls=%async_computation.2 | async-start | bytes 1048576 | tf_op jit(solution)/shard_map/all_to_all | solution.py:88
  99.0 18.2 %all-to-all-start = ((bf16[1,128,4,4,128]{4,1,3,0,2:T(8,128)(2,1)}), bf16[1,128,4,4,128]{4,1,3,0,2:T(8,128)(2,1)S(1)}, u32[]{:S(2)}, u32[]{:S(2)}) async-start(bf16[1,128,4,4,128]{4,1,3,0,2:T(8,128)(2,1)} %copy.39), calls=%async_computation | async-start | bytes 1048576 | tf_op jit(solution)/shard_map/all_to_all | solution.py:82
  135.1 12.3 %all-to-all-start.3 = ((bf16[1,512,1,4,128]{4,3,2,0,1:T(4,128)(2,1)}), bf16[1,512,1,4,128]{4,3,2,0,1:T(4,128)(2,1)S(1)}, u32[]{:S(2)}, u32[]{:S(2)}) async-start(bf16[1,512,1,4,128]{4,3,2,0,1:T(4,128)(2,1)} %bitcast.54), calls=%async_computation.3 | async-start | bytes 1048576 | tf_op jit(solution)/shard_map/all_to_all | solution.py:101
Sparse Core Ops, SparseCore 0:
  10.7 51.9 all-gather.2
  64.3 71.0 all-gather.4
where the time goes:
time: 176 us
  waiting for transfers between devices  100 us (57%)
  local copies, waits for them, and re-layouts  17 us (10%)
  between operations  14.2 us (8%)
  other arithmetic  14.1 us (8%)
  starting transfers between devices  14 us (8%)
  matrix products  8.47 us (5%)
  loops' own time  7.88 us (4%)
    all_gather x1, waiting for transfers between devices, body(): owned = lax.all_gather(weight_half, 'dp', axis=0, tiled=True)  52.3 us
    all_to_all x1, waiting for transfers between devices, body(): lax.all_to_all(split_heads(queries), 'seq', split_axis=2, concat_axis=1,...  14.5 us
    all_to_all x1, waiting for transfers between devices, body(): lax.all_to_all(split_heads(hit_values), 'seq', split_axis=2, concat_axis=...  13.4 us
    all_to_all x1, waiting for transfers between devices, body(): lax.all_to_all(split_heads(hit_keys), 'seq', split_axis=2, concat_axis=1,...  10.8 us
    all_to_all x1, waiting for transfers between devices, body(): lax.all_to_all(attended, 'seq', split_axis=1, concat_axis=2, tiled=True)  8.77 us
    gather x1, local copies, waits for them, and re-layouts, body(): projection = jnp.take(full, inverse, axis=0).reshape(width, width)  8.08 us
    another operation x1, loops' own time, body(): outputs = lax.map(one_head, jnp.arange(n_heads, dtype=jnp.int32))  7.88 us
    select_n x2, other arithmetic, body(): projection = jnp.take(full, inverse, axis=0).reshape(width, width)  7.49 us
  transfers between devices with their start and end apart: 6, of which 5 were waited for; matrix products, arithmetic and copies ran while one was open for 9% of the time, Pallas kernels for 0%

commit v1 on v0

v1 whole, which is shorter than its diff:
```python
import functools
import math

import jax
import jax.numpy as jnp
from jax import lax
from jax.experimental import pallas as pl
from jax.experimental.pallas import tpu as pltpu
from jax.sharding import PartitionSpec as P

HEAD_DIM = 128

beta_one = 0.9
beta_two = 0.999
learn_rate = 0.003
weight_decay = 0.1
epsilon = 1e-08
step_count = 10.0


def adam_update(master_weight, first_moment, second_moment, gradient):
    new_first = beta_one * first_moment + (1.0 - beta_one) * gradient
    new_second = beta_two * second_moment + (1.0 - beta_two) * gradient * gradient
    first_hat = new_first / (1.0 - beta_one**step_count)
    second_hat = new_second / (1.0 - beta_two**step_count)
    new_master = master_weight - learn_rate * (
        first_hat / (jnp.sqrt(second_hat) + epsilon) + weight_decay * master_weight
    )
    return (new_master, new_first, new_second)


def attend_kernel(n_keys, info_ref, *refs):
    query_refs, pair_refs = refs[:2], refs[2 : 2 + n_keys]
    out_ref, keys, values = refs[2 + n_keys :]
    rows, wide = query_refs[0].shape
    count = info_ref[0]
    columns = []
    for i, ref in enumerate(pair_refs):
        keys[i * rows : (i + 1) * rows, :] = ref[0]
        values[i * rows : (i + 1) * rows, :] = ref[1]
        base = info_ref[1 + i] * rows
        columns.append(base + lax.broadcasted_iota(jnp.int32, (1, rows), 1))
    valid = jnp.concatenate(columns, axis=1) < count
    factor = HEAD_DIM ** (-0.5) * math.log2(math.e)
    for block, query_ref in enumerate(query_refs):
        for head in range(wide // HEAD_DIM):
            lanes = slice(head * HEAD_DIM, (head + 1) * HEAD_DIM)
            scores = lax.dot_general(
                query_ref[:, lanes],
                keys[:, lanes],
                (((1,), (1,)), ((), ())),
                preferred_element_type=jnp.float32,
            )
            scores = jnp.where(valid, scores, -1e30)
            top = jnp.max(scores, axis=1, keepdims=True)
            expo = jnp.exp2((scores - top) * factor)
            total = jnp.sum(expo, axis=1, keepdims=True)
            weights = (expo * (1.0 / total)).astype(jnp.bfloat16)
            out_ref[block, :, lanes] = jnp.dot(
                weights, values[:, lanes], preferred_element_type=jnp.float32
            ).astype(jnp.bfloat16)


def attend(info, query_blocks, pairs):
    rows, wide = query_blocks[0].shape
    n_keys = len(pairs)
    work = 4 * 2 * rows * n_keys * rows * wide
    moved = 2 * (4 * rows * wide + 2 * n_keys * rows * wide)
    return pl.pallas_call(
        functools.partial(attend_kernel, n_keys),
        out_shape=jax.ShapeDtypeStruct((2, rows, wide), jnp.bfloat16),
        in_specs=[pl.BlockSpec(memory_space=pltpu.SMEM)]
        + [pl.BlockSpec(memory_space=pltpu.VMEM)] * (2 + n_keys),
        out_specs=pl.BlockSpec(memory_space=pltpu.VMEM),
        scratch_shapes=[pltpu.VMEM((n_keys * rows, wide), jnp.bfloat16)] * 2,
        cost_estimate=pl.CostEstimate(flops=work, bytes_accessed=moved, transcendentals=0),
        name="attend",
    )(info, *query_blocks, *pairs)


def project_kernel(n_att, n_weights, info_ref, *refs):
    att_refs, weight_refs = refs[:n_att], refs[n_att : n_att + n_weights]
    out_ref, held = refs[n_att + n_weights :]
    _, rows, wide = att_refs[0].shape
    depth = weight_refs[0].shape[0]
    parts = wide // depth
    for slot, ref in enumerate(att_refs):
        flip = slot % 2
        for block in range(2):
            for part in range(parts):
                held[slot * parts + part, block * rows : (block + 1) * rows, :] = ref[
                    block ^ flip, :, part * depth : (part + 1) * depth
                ]
    total = None
    for i, ref in enumerate(weight_refs):
        term = jnp.dot(held[info_ref[i]], ref[...], preferred_element_type=jnp.float32)
        total = term if total is None else total + term
    total = total.astype(jnp.bfloat16)
    out_ref[0] = total[:rows]
    out_ref[1] = total[rows:]


def project(info, att, weights):
    _, rows, wide = att[0].shape
    depth, columns = weights[0].shape
    work = 2 * 2 * rows * len(att) * wide * columns
    moved = 2 * (2 * rows * len(att) * wide + len(weights) * depth * columns)
    return pl.pallas_call(
        functools.partial(project_kernel, len(att), len(weights)),
        out_shape=jax.ShapeDtypeStruct((2, rows, columns), jnp.bfloat16),
        in_specs=[pl.BlockSpec(memory_space=pltpu.SMEM)]
        + [pl.BlockSpec(memory_space=pltpu.VMEM)] * (len(att) + len(weights)),
        out_specs=pl.BlockSpec(memory_space=pltpu.VMEM),
        scratch_shapes=[pltpu.VMEM((len(att) * wide // depth, 2 * rows, depth), jnp.bfloat16)],
        cost_estimate=pl.CostEstimate(flops=work, bytes_accessed=moved, transcendentals=0),
        name="project",
    )(info, *att, *weights)


def place_kernel(n, info_ref, *refs):
    out_ref = refs[n]
    columns = refs[0].shape[1]
    for i in range(n):
        start = pl.multiple_of(info_ref[i] * columns, columns)
        out_ref[:, pl.ds(start, columns)] = refs[i][...]


def place(info, blocks):
    rows, columns = blocks[0].shape
    return pl.pallas_call(
        functools.partial(place_kernel, len(blocks)),
        out_shape=jax.ShapeDtypeStruct((rows, columns * len(blocks)), jnp.bfloat16),
        in_specs=[pl.BlockSpec(memory_space=pltpu.SMEM)]
        + [pl.BlockSpec(memory_space=pltpu.VMEM)] * len(blocks),
        out_specs=pl.BlockSpec(memory_space=pltpu.VMEM),
        cost_estimate=pl.CostEstimate(
            flops=0, bytes_accessed=4 * rows * columns * len(blocks), transcendentals=0
        ),
        name="place",
    )(info, *blocks)


def gather_weights(shard):
    owners = lax.axis_size("dp")
    me = lax.axis_index("dp")
    ring = owners // 2
    place_, side = me // 2, me % 2

    def moved(block, step):
        perm = [(o, (o // 2 + step) % ring * 2 + o % 2) for o in range(owners)]
        return lax.ppermute(block, "dp", perm)

    def swapped(block):
        return lax.ppermute(block, "dp", [(o, o ^ 1) for o in range(owners)])

    held = [(place_, shard)]
    ahead, back = shard, shard
    for step in range(1, ring // 2 + 1):
        ahead = moved(ahead, 1)
        held.append(((place_ - step) % ring, ahead))
        if step <= (ring - 1) // 2:
            back = moved(back, -1)
            held.append(((place_ + step) % ring, back))
    blocks = []
    for where, block in held:
        blocks.append((where * 2 + side, block))
        blocks.append((where * 2 + 1 - side, swapped(block)))
    return blocks


def body(
    queries,
    hit_keys,
    hit_values,
    hit_counts,
    master_weight,
    first_moment,
    second_moment,
    gradient,
    owner_bucket,
):
    groups = lax.axis_size("seq")
    chips = groups // 2
    me = lax.axis_index("seq")
    chip, core = me // 2, me % 2
    query, key, value = queries[0], hit_keys[0], hit_values[0]
    rows, width = query.shape
    wide = width // groups

    def to_same(array, step):
        perm = [(s, (s // 2 + step) % chips * 2 + s % 2) for s in range(groups)]
        return lax.ppermute(array, "seq", perm)

    def to_cross(array, step):
        perm = [(s, (s // 2 + step) % chips * 2 + 1 - s % 2) for s in range(groups)]
        return lax.ppermute(array, "seq", perm)

    def to_sibling(array):
        return lax.ppermute(array, "seq", [(s, s ^ 1) for s in range(groups)])

    def cut(array, group):
        return lax.dynamic_slice_in_dim(array, group * wide, wide, 1)

    def pair(group):
        return jnp.stack([cut(key, group), cut(value, group)])

    sibling = me ^ 1
    pairs, sources = [pair(me), to_sibling(pair(sibling))], [me, sibling]
    asked = [[cut(query, me), to_sibling(cut(query, sibling))]]
    for step in range(1, chips):
        target, source = (chip + step) % chips, (chip - step) % chips
        pairs.append(to_same(pair(target * 2 + core), step))
        pairs.append(to_cross(pair(target * 2 + 1 - core), step))
        sources += [source * 2 + core, source * 2 + 1 - core]
        asked.append(
            [
                to_same(cut(query, target * 2 + core), step),
                to_cross(cut(query, target * 2 + 1 - core), step),
            ]
        )
    new_master, new_first, new_second = adam_update(
        master_weight, first_moment, second_moment, gradient
    )
    weights = gather_weights(new_master[0].astype(jnp.bfloat16))

    info = jnp.stack([hit_counts[0]] + sources).astype(jnp.int32)
    attended = [attend(info, blocks, pairs) for blocks in asked]
    spread = [attended] + [[to_same(a, step) for a in attended] for step in range(1, chips)]
    beside = [[to_sibling(a) for a in row] for row in spread]

    owner_ids = jnp.stack([owner for owner, _ in weights])
    bucket = jnp.take(owner_bucket, owner_ids)
    depth = weights[0][1].shape[0]
    parts = wide // depth if wide >= depth else 1
    group, part = bucket // parts, bucket % parts
    slot = (chip - group // 2) % chips * 2 + (group % 2 - core) % 2
    where = (slot * parts + part).astype(jnp.int32)
    blocks = [block for _, block in weights]

    columns = [None] * groups
    for e in list(range(1, chips)) + [0]:
        att = []
        for d in range(chips):
            att += [spread[d][(e - d) % chips], beside[d][(e - d) % chips]]
        out = project(where, att, blocks)
        if e == 0:
            columns[0], columns[1] = out[0], to_sibling(out[1])
        else:
            columns[2 * e] = to_same(out[0], chips - e)
            columns[2 * e + 1] = to_cross(out[1], chips - e)
    order = []
    for e in range(chips):
        other = (chip + e) % chips
        order += [other * 2 + core, other * 2 + 1 - core]
    projected = place(jnp.stack(order).astype(jnp.int32), columns)[None]
    return (projected, new_master, new_first, new_second)


def solution(mesh):
    return jax.shard_map(
        body,
        mesh=mesh,
        in_specs=(
            P("dp", "seq", None),
            P("dp", "seq", None),
            P("dp", "seq", None),
            P("dp"),
            P("dp", None, "seq"),
            P("dp", None, "seq"),
            P("dp", None, "seq"),
            P("dp", None, "seq"),
            P(),
        ),
        out_specs=(
            P("dp", "seq", None),
            P("dp", None, "seq"),
            P("dp", None, "seq"),
            P("dp", None, "seq"),
        ),
        check_vma=False,
    )
```

time: 176 us -> 78.2 us (0.44)
  waiting for transfers between devices: 100 us -> 23.4 us
  Pallas kernels: 0 us -> 18.3 us
  between operations: 14.2 us -> 1.68 us
  other arithmetic: 14.1 us -> 3.39 us
  matrix products: 8.47 us -> 0 us
  loops' own time: 7.88 us -> 0 us
  starting transfers between devices: 14 us -> 21.5 us
  local copies, waits for them, and re-layouts: 17 us -> 9.58 us
    all_gather x2 -> x0, waiting for transfers between devices: 52.4 us -> none  [the longest x1 52.3 us: body(): owned = lax.all_gather(weight_half, 'dp', axis=0, tiled=True)]
    all_to_all x4 -> x0, waiting for transfers between devices: 47.6 us -> none  [the longest x1 14.5 us: body(): lax.all_to_all(split_heads(queries), 'seq', split_axis=2, concat_axis=1,...]
    ppermute x0 -> x22, waiting for transfers between devices: none -> 23.4 us  [the longest x5 9.1 us: to_same(): return lax.ppermute(array, 'seq', perm)]
    ppermute x0 -> x22, starting transfers between devices: none -> 21.5 us  [the longest x5 8.06 us: to_same(): return lax.ppermute(array, 'seq', perm)]
    pallas_call x0 -> x5, Pallas kernels: none -> 18.3 us  [the longest x2 9.82 us: attend(): pl.pallas_call(functools.partial(attend_kernel, n_keys), out_shape=jax.Sh...]
    all_to_all x4 -> x0, starting transfers between devices: 13.9 us -> none  [the longest x1 3.47 us: body(): lax.all_to_all(split_heads(queries), 'seq', split_axis=2, concat_axis=1,...]
    dot_general x9 -> x0, matrix products: 8.47 us -> none  [the longest x1 5.45 us: body(): total = jnp.dot(rows_in, projection, preferred_element_type=jnp.float32)]
    another operation x1 -> x0, loops' own time: 7.88 us -> none  [body(): outputs = lax.map(one_head, jnp.arange(n_heads, dtype=jnp.int32))]
  transfers between devices with their start and end apart: 6 -> 22, of which waited for: 5 -> 8; matrix products, arithmetic and copies ran while one was open for 9% -> 10% of each run, Pallas kernels for 0% -> 21%
where the time goes in v1:
time: 78.2 us; the launch traced here: 77.9 us
  waiting for transfers between devices  23.4 us (30%)
  starting transfers between devices  21.5 us (27%)
  Pallas kernels  18.3 us (23%)
  local copies, waits for them, and re-layouts  9.58 us (12%)
  other arithmetic  3.39 us (4%)
  between operations  1.68 us (2%)
    pallas_call x2, Pallas kernels, attend(): pl.pallas_call(functools.partial(attend_kernel, n_keys), out_shape=jax.Sh...  9.82 us
    ppermute x5, waiting for transfers between devices, to_same(): return lax.ppermute(array, 'seq', perm)  9.1 us
    ppermute x5, starting transfers between devices, to_same(): return lax.ppermute(array, 'seq', perm)  8.06 us
    pallas_call x2, Pallas kernels, project(): pl.pallas_call(functools.partial(project_kernel, len(att), len(weights)),...  6.58 us
    ppermute x4, waiting for transfers between devices, swapped(): return lax.ppermute(block, 'dp', [(o, o ^ 1) for o in range(owners)])  6.51 us
    ppermute x4, starting transfers between devices, swapped(): return lax.ppermute(block, 'dp', [(o, o ^ 1) for o in range(owners)])  5.55 us
    ppermute x3, starting transfers between devices, moved(): return lax.ppermute(block, 'dp', perm)  5.21 us
    ppermute x3, waiting for transfers between devices, to_cross(): return lax.ppermute(array, 'seq', perm)  5.2 us
  transfers between devices with their start and end apart: 22, of which 8 were waited for; matrix products, arithmetic and copies ran while one was open for 10% of the time, Pallas kernels for 21%

profile of v1, /device:TPU:0, one launch (start us, length us, event | category | flops | bytes accessed | tf_op | source)
XLA Modules:
  0.0 77.9 jit_solution(7761737652104545888)
XLA Ops:
  0.7 1.9 %dynamic-slice_bitcast_fusion = (bf16[128,512]{1,0:T(8,128)(2,1)S(1)}, bf16[128,512]{1,0:T(8,128)(2,1)S(1)}, bf16[128,512]{1,0:T(8,128)(2,1)}, bf16[128,512]{1,0:T(8,128)(2,1)S(1)}) fusion(bf16[1,128,2048]{2,1,0:T(8,128)(2,1)} %param.9, s32[]{:T(128)S(6)} %select_n.131, s32[]{:T(128)S(6)} %select_n.129, s32[]{:T(128)S(6)} %select_n.128, s32[]{:T(128)S(6)} %select_n.130), kind=kLoop, calls=%fused_computation.14 | loop fusion | bytes 1048592 | tf_op jit(solution)/shard_map/dynamic_slice | solution.py:202
  3.4 3.0 %collective-permute-start.2 = (bf16[2,128,512]{2,1,0:T(8,128)(2,1)S(1)}, bf16[2,128,512]{2,1,0:T(8,128)(2,1)S(1)}, u32[]{:S(2)}, u32[]{:S(2)}) collective-permute-start(bf16[2,128,512]{2,1,0:T(8,128)(2,1)S(1)} %pad_maximum_fusion.2), channel_id=1, source_target_pairs={{0,2},{1,3},{2,0},{3,1},{4,6},{5,7},{6,4},{7,5},{8,10},{9,11},{10,... | collective-permute-start | bytes 786440 | tf_op jit(solution)/shard_map/ppermute | solution.py:192
  6.6 1.4 %convert_bitcast_fusion = (bf16[256,512]{1,0:T(8,128)(2,1)S(1)}, f32[1,256,512]{2,1,0:T(8,128)}, f32[1,256,512]{2,1,0:T(8,128)}, f32[1,256,512]{2,1,0:T(8,128)}) fusion(f32[1,256,512]{2,1,0:T(8,128)S(1)} %copy-done.16, f32[1,256,512]{2,1,0:T(8,128)S(1)} %copy-done.17, f32[1,256,512]{2,1,0:T(8,128)S(1)} %copy-done.18, f32[1,256,512]{2,1,0:T(8,128)S(1)} %copy-done.19), kind=kLoop, calls=%fused_computation.9 | loop fusion | flops 2097152 | bytes 3932160 | tf_op jit(solution)/shard_map/convert_element_type | solution.py:224
  8.0 1.6 %collective-permute-start.10 = (bf16[256,512]{1,0:T(8,128)(2,1)S(1)}, bf16[256,512]{1,0:T(8,128)(2,1)S(1)}, u32[]{:S(2)}, u32[]{:S(2)}) collective-permute-start(bf16[256,512]{1,0:T(8,128)(2,1)S(1)} %get-tuple-element.4.refs_4_), channel_id=1, source_target_pairs={{0,8},{4,12},{8,16},{12,20},{16,24},{20,28},{24,0},{28,4},{1,9},{5... | collective-permute-start | bytes 786440 | tf_op jit(solution)/shard_map/ppermute | solution.py:151
  10.9 1.3 %collective-permute-start.5 = (bf16[128,512]{1,0:T(8,128)(2,1)S(1)}, bf16[128,512]{1,0:T(8,128)(2,1)S(1)}, u32[]{:S(2)}, u32[]{:S(2)}) collective-permute-start(bf16[128,512]{1,0:T(8,128)(2,1)S(1)} %get-tuple-element.11), channel_id=1, source_target_pairs={{0,2},{1,3},{2,0},{3,1},{4,6},{5,7},{6,4},{7,5},{8,10},{9,11},{10,... | collective-permute-start | bytes 393224 | tf_op jit(solution)/shard_map/ppermute | solution.py:192
  12.5 0.7 pad_maximum_fusion.refs_2_
  13.5 2.0 %collective-permute-start.9 = (bf16[256,512]{1,0:T(8,128)(2,1)S(1)}, bf16[256,512]{1,0:T(8,128)(2,1)S(1)}, u32[]{:S(2)}, u32[]{:S(2)}) collective-permute-start(bf16[256,512]{1,0:T(8,128)(2,1)S(1)} %get-tuple-element.4.refs_4_), channel_id=1, source_target_pairs={{0,4},{4,0},{8,12},{12,8},{16,20},{20,16},{24,28},{28,24},{1,5},{5... | collective-permute-start | bytes 786440 | tf_op jit(solution)/shard_map/ppermute | solution.py:154
  15.6 3.2 %collective-permute-done.3.refs_5_ = bf16[2,128,512]{2,1,0:T(8,128)(2,1)S(1)} collective-permute-done((bf16[2,128,512]{2,1,0:T(8,128)(2,1)S(1)}, bf16[2,128,512]{2,1,0:T(8,128)(2,1)S(1)}, u32[]{:S(2)}, u32[]{:S(2)}) %collective-permute-start.3) | collective-permute-done | bytes 262176 | tf_op jit(solution)/shard_map/ppermute | solution.py:196
  18.7 3.6 %collective-permute-start.12 = (bf16[256,512]{1,0:T(8,128)(2,1)S(1)}, bf16[256,512]{1,0:T(8,128)(2,1)S(1)}, u32[]{:S(2)}, u32[]{:S(2)}) collective-permute-start(bf16[256,512]{1,0:T(8,128)(2,1)S(1)} %get-tuple-element.4.refs_4_), channel_id=1, source_target_pairs={{0,24},{4,28},{8,0},{12,4},{16,8},{20,12},{24,16},{28,20},{1,25},{... | collective-permute-start | bytes 786440 | tf_op jit(solution)/shard_map/ppermute | solution.py:151
  22.4 4.9 %attend.2.refs_0_ = bf16[2,128,512]{2,1,0:T(8,128)(2,1)} custom-call(s32[5]{0:T(128)} %stack.122.info_ref, bf16[128,512]{1,0:T(8,128)(2,1)} %get-tuple-element.10.refs_0_, bf16[128,512]{1,0:T(8,128)(2,1)} %copy-done.26, bf16[2,128,512]{2,1,0:T(8,128)(2,1)} %pad_maximum_fusion.refs_2_, bf16[2,128,512]{2,1,0:T(8,128)(2,1)} %copy-done.11, ...), custom_call_target="tpu_custom_call" | custom-call | flops 268435456 | bytes 1572864 | tf_op jit(solution)/shard_map/attend/pallas_call | solution.py:69
  27.3 0.8 %collective-permute-start.4 = (bf16[2,128,512]{2,1,0:T(8,128)(2,1)}, bf16[2,128,512]{2,1,0:T(8,128)(2,1)S(1)}, u32[]{:S(2)}, u32[]{:S(2)}) collective-permute-start(bf16[2,128,512]{2,1,0:T(8,128)(2,1)} %attend.2.refs_0_), channel_id=1, source_target_pairs={{0,1},{1,0},{2,3},{3,2},{4,5},{5,4},{6,7},{7,6},{8,9},{9,8},{10,11... | collective-permute-start | bytes 786440 | tf_op jit(solution)/shard_map/ppermute | solution.py:199
  28.1 0.7 copy-done.28
  28.8 4.9 %attend.3.refs_0_ = bf16[2,128,512]{2,1,0:T(8,128)(2,1)} custom-call(s32[5]{0:T(128)} %stack.122.info_ref, bf16[128,512]{1,0:T(8,128)(2,1)} %copy-done.27, bf16[128,512]{1,0:T(8,128)(2,1)} %copy-done.28, bf16[2,128,512]{2,1,0:T(8,128)(2,1)} %pad_maximum_fusion.refs_2_, bf16[2,128,512]{2,1,0:T(8,128)(2,1)} %copy-done.11, bf16[2,128,512]{2,1,0:T(8,128)(2,1)} %copy-done.12, ...), custom_call_target="tpu_custom_call" | custom-call | flops 268435456 | bytes 1572864 | tf_op jit(solution)/shard_map/attend/pallas_call | solution.py:69
  33.7 1.5 %collective-permute-start.7 = (bf16[2,128,512]{2,1,0:T(8,128)(2,1)}, bf16[2,128,512]{2,1,0:T(8,128)(2,1)S(1)}, u32[]{:S(2)}, u32[]{:S(2)}) collective-permute-start(bf16[2,128,512]{2,1,0:T(8,128)(2,1)} %attend.3.refs_0_), channel_id=1, source_target_pairs={{0,2},{1,3},{2,0},{3,1},{4,6},{5,7},{6,4},{7,5},{8,10},{9,11},{10,... | collective-permute-start | bytes 786440 | tf_op jit(solution)/shard_map/ppermute | solution.py:192
  36.0 1.5 %collective-permute-start.11 = (bf16[256,512]{1,0:T(8,128)(2,1)S(1)}, bf16[256,512]{1,0:T(8,128)(2,1)S(1)}, u32[]{:S(2)}, u32[]{:S(2)}) collective-permute-start(bf16[256,512]{1,0:T(8,128)(2,1)S(1)} %collective-permute-done.10.refs_6_), channel_id=1, source_target_pairs={{0,4},{4,0},{8,12},{12,8},{16,20},{20,16},{24,28},{28,24},{1,5},{5... | collective-permute-start | bytes 786440 | tf_op jit(solution)/shard_map/ppermute | solution.py:154
  38.1 4.9 %collective-permute-done.7.refs_2_ = bf16[2,128,512]{2,1,0:T(8,128)(2,1)S(1)} collective-permute-done((bf16[2,128,512]{2,1,0:T(8,128)(2,1)}, bf16[2,128,512]{2,1,0:T(8,128)(2,1)S(1)}, u32[]{:S(2)}, u32[]{:S(2)}) %collective-permute-start.7) | collective-permute-done | bytes 262176 | tf_op jit(solution)/shard_map/ppermute | solution.py:192
  43.0 2.6 %collective-permute-done.14.refs_10_ = bf16[256,512]{1,0:T(8,128)(2,1)S(1)} collective-permute-done((bf16[256,512]{1,0:T(8,128)(2,1)S(1)}, bf16[256,512]{1,0:T(8,128)(2,1)S(1)}, u32[]{:S(2)}, u32[]{:S(2)}) %collective-permute-start.14) | collective-permute-done | bytes 262176 | tf_op jit(solution)/shard_map/ppermute | solution.py:151
  45.6 1.5 %collective-permute-start.15 = (bf16[256,512]{1,0:T(8,128)(2,1)S(1)}, bf16[256,512]{1,0:T(8,128)(2,1)S(1)}, u32[]{:S(2)}, u32[]{:S(2)}) collective-permute-start(bf16[256,512]{1,0:T(8,128)(2,1)S(1)} %collective-permute-done.14.refs_10_), channel_id=1, source_target_pairs={{0,4},{4,0},{8,12},{12,8},{16,20},{20,16},{24,28},{28,24},{1,5},{5... | collective-permute-start | bytes 786440 | tf_op jit(solution)/shard_map/ppermute | solution.py:154
  49.0 1.8 %collective-permute-done.13.refs_9_ = bf16[256,512]{1,0:T(8,128)(2,1)S(1)} collective-permute-done((bf16[256,512]{1,0:T(8,128)(2,1)S(1)}, bf16[256,512]{1,0:T(8,128)(2,1)S(1)}, u32[]{:S(2)}, u32[]{:S(2)}) %collective-permute-start.13) | collective-permute-done | bytes 262176 | tf_op jit(solution)/shard_map/ppermute | solution.py:154
  50.8 4.7 %collective-permute-done.15.refs_11_ = bf16[256,512]{1,0:T(8,128)(2,1)S(1)} collective-permute-done((bf16[256,512]{1,0:T(8,128)(2,1)S(1)}, bf16[256,512]{1,0:T(8,128)(2,1)S(1)}, u32[]{:S(2)}, u32[]{:S(2)}) %collective-permute-start.15) | collective-permute-done | bytes 262176 | tf_op jit(solution)/shard_map/ppermute | solution.py:154
  55.6 0.7 copy-done.8
  56.2 3.3 %project.2 = bf16[2,128,512]{2,1,0:T(8,128)(2,1)} custom-call(s32[8]{0:T(128)} %fusion.2.info_ref, bf16[2,128,512]{2,1,0:T(8,128)(2,1)} %attend.2.refs_0_, bf16[2,128,512]{2,1,0:T(8,128)(2,1)} %copy-done.20, bf16[2,128,512]{2,1,0:T(8,128)(2,1)} %copy-done.21, bf16[2,128,512]{2,1,0:T(8,128)(2,1)} %copy-done.23, bf16[256,512]{1,0:T(8,128)(2,1)} %copy-done.1, ...), custom_call_target="tpu_custom_call" | custom-call | flops 536870912 | bytes 3145728 | tf_op jit(solution)/shard_map/project/pallas_call | solution.py:108
  59.5 1.6 %slice_bitcast_fusion.2 = (bf16[128,512]{1,0:T(8,128)(2,1)S(1)}, bf16[128,512]{1,0:T(8,128)(2,1)}) fusion(bf16[2,128,512]{2,1,0:T(8,128)(2,1)} %project.2), kind=kLoop, calls=%fused_computation.12 | loop fusion | bytes 524288 | tf_op jit(solution)/shard_map/squeeze | solution.py:247
  61.2 0.7 copy-done.24
  61.9 0.7 copy-done.25
  62.6 3.3 %project.3 = bf16[2,128,512]{2,1,0:T(8,128)(2,1)} custom-call(s32[8]{0:T(128)} %fusion.2.info_ref, bf16[2,128,512]{2,1,0:T(8,128)(2,1)} %attend.3.refs_0_, bf16[2,128,512]{2,1,0:T(8,128)(2,1)} %copy-done.24, bf16[2,128,512]{2,1,0:T(8,128)(2,1)} %copy-done.22, bf16[2,128,512]{2,1,0:T(8,128)(2,1)} %copy-done.25, bf16[256,512]{1,0:T(8,128)(2,1)} %copy-done.1, ...), custom_call_target="tpu_custom_call" | custom-call | flops 536870912 | bytes 3145728 | tf_op jit(solution)/shard_map/project/pallas_call | solution.py:108
  65.9 1.0 %slice_bitcast_fusion = (bf16[128,512]{1,0:T(8,128)(2,1)S(1)}, bf16[128,512]{1,0:T(8,128)(2,1)S(1)}) fusion(bf16[2,128,512]{2,1,0:T(8,128)(2,1)} %project.3), kind=kLoop, calls=%fused_computation.10 | loop fusion | bytes 524288 | tf_op jit(solution)/shard_map/squeeze | solution.py:250
  66.9 1.6 %collective-permute-start.20 = (bf16[128,512]{1,0:T(8,128)(2,1)S(1)}, bf16[128,512]{1,0:T(8,128)(2,1)S(1)}, u32[]{:S(2)}, u32[]{:S(2)}) collective-permute-start(bf16[128,512]{1,0:T(8,128)(2,1)S(1)} %get-tuple-element.21), channel_id=1, source_target_pairs={{0,2},{1,3},{2,0},{3,1},{4,6},{5,7},{6,4},{7,5},{8,10},{9,11},{10,... | collective-permute-start | bytes 393224 | tf_op jit(solution)/shard_map/ppermute | solution.py:192
  69.4 3.9 %collective-permute-done.20.refs_2_ = bf16[128,512]{1,0:T(8,128)(2,1)S(1)} collective-permute-done((bf16[128,512]{1,0:T(8,128)(2,1)S(1)}, bf16[128,512]{1,0:T(8,128)(2,1)S(1)}, u32[]{:S(2)}, u32[]{:S(2)}) %collective-permute-start.20) | collective-permute-done | bytes 131104 | tf_op jit(solution)/shard_map/ppermute | solution.py:192
  73.2 2.0 %collective-permute-done.21.refs_3_ = bf16[128,512]{1,0:T(8,128)(2,1)S(1)} collective-permute-done((bf16[128,512]{1,0:T(8,128)(2,1)S(1)}, bf16[128,512]{1,0:T(8,128)(2,1)S(1)}, u32[]{:S(2)}, u32[]{:S(2)}) %collective-permute-start.21) | collective-permute-done | bytes 131104 | tf_op jit(solution)/shard_map/ppermute | solution.py:196
  75.3 0.6 copy-done.31
  75.9 1.9 %place.1 = bf16[128,2048]{1,0:T(8,128)(2,1)} custom-call(s32[4]{0:T(128)} %pad_add_fusion.info_ref, bf16[128,512]{1,0:T(8,128)(2,1)} %get-tuple-element.23.refs_0_, bf16[128,512]{1,0:T(8,128)(2,1)} %copy-done.29, bf16[128,512]{1,0:T(8,128)(2,1)} %copy-done.30, bf16[128,512]{1,0:T(8,128)(2,1)} %copy-done.31), custom_call_target="tpu_custom_call" | custom-call | bytes 1048576 | tf_op jit(solution)/shard_map/place/pallas_call | solution.py:130
  (98 shorter events, 6.1 us)
Async XLA Ops:
  0.6 46.4 %copy-start = (s32[8]{0:T(128)S(1)}, s32[8]{0:T(128)}, u32[]{:S(2)}) copy-start(s32[8]{0:T(128)} %param.17) | copy-start | bytes 100
  2.6 8.2 %collective-permute-start = (bf16[128,512]{1,0:T(8,128)(2,1)S(1)}, bf16[128,512]{1,0:T(8,128)(2,1)S(1)}, u32[]{:S(2)}, u32[]{:S(2)}) collective-permute-start(bf16[128,512]{1,0:T(8,128)(2,1)S(1)} %get-tuple-element.9), channel_id=1, source_target_pairs={{0,1},{1,0},{2,3},{3,2},{4,5},{5,4},{6,7},{7,6},{8,9},{9,8},{10,11... | collective-permute-start | bytes 393224 | tf_op jit(solution)/shard_map/ppermute | solution.py:199
  3.2 9.0 %collective-permute-start.1 = (bf16[2,128,512]{2,1,0:T(8,128)(2,1)S(1)}, bf16[2,128,512]{2,1,0:T(8,128)(2,1)S(1)}, u32[]{:S(2)}, u32[]{:S(2)}) collective-permute-start(bf16[2,128,512]{2,1,0:T(8,128)(2,1)S(1)} %pad_maximum_fusion.1), channel_id=1, source_target_pairs={{0,1},{1,0},{2,3},{3,2},{4,5},{5,4},{6,7},{7,6},{8,9},{9,8},{10,11... | collective-permute-start | bytes 786440 | tf_op jit(solution)/shard_map/ppermute | solution.py:199
  3.4 10.1 %collective-permute-start.2 = (bf16[2,128,512]{2,1,0:T(8,128)(2,1)S(1)}, bf16[2,128,512]{2,1,0:T(8,128)(2,1)S(1)}, u32[]{:S(2)}, u32[]{:S(2)}) collective-permute-start(bf16[2,128,512]{2,1,0:T(8,128)(2,1)S(1)} %pad_maximum_fusion.2), channel_id=1, source_target_pairs={{0,2},{1,3},{2,0},{3,1},{4,6},{5,7},{6,4},{7,5},{8,10},{9,11},{10,... | collective-permute-start | bytes 786440 | tf_op jit(solution)/shard_map/ppermute | solution.py:192
  6.4 12.3 %collective-permute-start.3 = (bf16[2,128,512]{2,1,0:T(8,128)(2,1)S(1)}, bf16[2,128,512]{2,1,0:T(8,128)(2,1)S(1)}, u32[]{:S(2)}, u32[]{:S(2)}) collective-permute-start(bf16[2,128,512]{2,1,0:T(8,128)(2,1)S(1)} %pad_maximum_fusion.3), channel_id=1, source_target_pairs={{0,3},{1,2},{2,1},{3,0},{4,7},{5,6},{6,5},{7,4},{8,11},{9,10},{10,... | collective-permute-start | bytes 786440 | tf_op jit(solution)/shard_map/ppermute | solution.py:196
  8.0 10.7 %copy-start.1 = (bf16[256,512]{1,0:T(8,128)(2,1)}, bf16[256,512]{1,0:T(8,128)(2,1)S(1)}, u32[]{:S(2)}) copy-start(bf16[256,512]{1,0:T(8,128)(2,1)S(1)} %get-tuple-element.4.refs_4_) | copy-start | bytes 786436
  8.0 27.2 %collective-permute-start.10 = (bf16[256,512]{1,0:T(8,128)(2,1)S(1)}, bf16[256,512]{1,0:T(8,128)(2,1)S(1)}, u32[]{:S(2)}, u32[]{:S(2)}) collective-permute-start(bf16[256,512]{1,0:T(8,128)(2,1)S(1)} %get-tuple-element.4.refs_4_), channel_id=1, source_target_pairs={{0,8},{4,12},{8,16},{12,20},{16,24},{20,28},{24,0},{28,4},{1,9},{5... | collective-permute-start | bytes 786440 | tf_op jit(solution)/shard_map/ppermute | solution.py:151
  10.9 11.5 %copy-start.26 = (bf16[128,512]{1,0:T(8,128)(2,1)}, bf16[128,512]{1,0:T(8,128)(2,1)S(1)}, u32[]{:S(2)}) copy-start(bf16[128,512]{1,0:T(8,128)(2,1)S(1)} %collective-permute-done.refs_1_) | copy-start | bytes 393220
  10.9 16.4 %collective-permute-start.5 = (bf16[128,512]{1,0:T(8,128)(2,1)S(1)}, bf16[128,512]{1,0:T(8,128)(2,1)S(1)}, u32[]{:S(2)}, u32[]{:S(2)}) collective-permute-start(bf16[128,512]{1,0:T(8,128)(2,1)S(1)} %get-tuple-element.11), channel_id=1, source_target_pairs={{0,2},{1,3},{2,0},{3,1},{4,6},{5,7},{6,4},{7,5},{8,10},{9,11},{10,... | collective-permute-start | bytes 393224 | tf_op jit(solution)/shard_map/ppermute | solution.py:192
  12.2 15.9 %collective-permute-start.6 = (bf16[128,512]{1,0:T(8,128)(2,1)S(1)}, bf16[128,512]{1,0:T(8,128)(2,1)S(1)}, u32[]{:S(2)}, u32[]{:S(2)}) collective-permute-start(bf16[128,512]{1,0:T(8,128)(2,1)S(1)} %get-tuple-element.8), channel_id=1, source_target_pairs={{0,3},{1,2},{2,1},{3,0},{4,7},{5,6},{6,5},{7,4},{8,11},{9,10},{10,... | collective-permute-start | bytes 393224 | tf_op jit(solution)/shard_map/ppermute | solution.py:196
  13.5 21.9 %collective-permute-start.9 = (bf16[256,512]{1,0:T(8,128)(2,1)S(1)}, bf16[256,512]{1,0:T(8,128)(2,1)S(1)}, u32[]{:S(2)}, u32[]{:S(2)}) collective-permute-start(bf16[256,512]{1,0:T(8,128)(2,1)S(1)} %get-tuple-element.4.refs_4_), channel_id=1, source_target_pairs={{0,4},{4,0},{8,12},{12,8},{16,20},{20,16},{24,28},{28,24},{1,5},{5... | collective-permute-start | bytes 786440 | tf_op jit(solution)/shard_map/ppermute | solution.py:154
  18.7 17.3 %collective-permute-start.12 = (bf16[256,512]{1,0:T(8,128)(2,1)S(1)}, bf16[256,512]{1,0:T(8,128)(2,1)S(1)}, u32[]{:S(2)}, u32[]{:S(2)}) collective-permute-start(bf16[256,512]{1,0:T(8,128)(2,1)S(1)} %get-tuple-element.4.refs_4_), channel_id=1, source_target_pairs={{0,24},{4,28},{8,0},{12,4},{16,8},{20,12},{24,16},{28,20},{1,25},{... | collective-permute-start | bytes 786440 | tf_op jit(solution)/shard_map/ppermute | solution.py:151
  27.3 10.2 %collective-permute-start.4 = (bf16[2,128,512]{2,1,0:T(8,128)(2,1)}, bf16[2,128,512]{2,1,0:T(8,128)(2,1)S(1)}, u32[]{:S(2)}, u32[]{:S(2)}) collective-permute-start(bf16[2,128,512]{2,1,0:T(8,128)(2,1)} %attend.2.refs_0_), channel_id=1, source_target_pairs={{0,1},{1,0},{2,3},{3,2},{4,5},{5,4},{6,7},{7,6},{8,9},{9,8},{10,11... | collective-permute-start | bytes 786440 | tf_op jit(solution)/shard_map/ppermute | solution.py:199
  33.7 9.3 %collective-permute-start.7 = (bf16[2,128,512]{2,1,0:T(8,128)(2,1)}, bf16[2,128,512]{2,1,0:T(8,128)(2,1)S(1)}, u32[]{:S(2)}, u32[]{:S(2)}) collective-permute-start(bf16[2,128,512]{2,1,0:T(8,128)(2,1)} %attend.3.refs_0_), channel_id=1, source_target_pairs={{0,2},{1,3},{2,0},{3,1},{4,6},{5,7},{6,4},{7,5},{8,10},{9,11},{10,... | collective-permute-start | bytes 786440 | tf_op jit(solution)/shard_map/ppermute | solution.py:192
  35.2 12.5 %copy-start.2 = (bf16[256,512]{1,0:T(8,128)(2,1)}, bf16[256,512]{1,0:T(8,128)(2,1)S(1)}, u32[]{:S(2)}) copy-start(bf16[256,512]{1,0:T(8,128)(2,1)S(1)} %collective-permute-done.10.refs_6_) | copy-start | bytes 786436
  35.2 10.3 %collective-permute-start.14 = (bf16[256,512]{1,0:T(8,128)(2,1)S(1)}, bf16[256,512]{1,0:T(8,128)(2,1)S(1)}, u32[]{:S(2)}, u32[]{:S(2)}) collective-permute-start(bf16[256,512]{1,0:T(8,128)(2,1)S(1)} %collective-permute-done.10.refs_6_), channel_id=1, source_target_pairs={{0,8},{4,12},{8,16},{12,20},{16,24},{20,28},{24,0},{28,4},{1,9},{5... | collective-permute-start | bytes 786440 | tf_op jit(solution)/shard_map/ppermute | solution.py:151
  35.5 12.3 %copy-start.3 = (bf16[256,512]{1,0:T(8,128)(2,1)}, bf16[256,512]{1,0:T(8,128)(2,1)S(1)}, u32[]{:S(2)}) copy-start(bf16[256,512]{1,0:T(8,128)(2,1)S(1)} %collective-permute-done.9.refs_5_) | copy-start | bytes 786436
  35.5 13.0 %collective-permute-start.18 = (bf16[2,128,512]{2,1,0:T(8,128)(2,1)S(1)}, bf16[2,128,512]{2,1,0:T(8,128)(2,1)S(1)}, u32[]{:S(2)}, u32[]{:S(2)}) collective-permute-start(bf16[2,128,512]{2,1,0:T(8,128)(2,1)S(1)} %copy-done.10), channel_id=1, source_target_pairs={{0,2},{1,3},{2,0},{3,1},{4,6},{5,7},{6,4},{7,5},{8,10},{9,11},{10,... | collective-permute-start | bytes 786440 | tf_op jit(solution)/shard_map/ppermute | solution.py:192
  36.0 19.5 %copy-start.4 = (bf16[256,512]{1,0:T(8,128)(2,1)}, bf16[256,512]{1,0:T(8,128)(2,1)S(1)}, u32[]{:S(2)}) copy-start(bf16[256,512]{1,0:T(8,128)(2,1)S(1)} %collective-permute-done.12.refs_8_) | copy-start | bytes 786436
  36.0 12.4 %collective-permute-start.11 = (bf16[256,512]{1,0:T(8,128)(2,1)S(1)}, bf16[256,512]{1,0:T(8,128)(2,1)S(1)}, u32[]{:S(2)}, u32[]{:S(2)}) collective-permute-start(bf16[256,512]{1,0:T(8,128)(2,1)S(1)} %collective-permute-done.10.refs_6_), channel_id=1, source_target_pairs={{0,4},{4,0},{8,12},{12,8},{16,20},{20,16},{24,28},{28,24},{1,5},{5... | collective-permute-start | bytes 786440 | tf_op jit(solution)/shard_map/ppermute | solution.py:154
  37.5 18.0 %copy-start.20 = (bf16[2,128,512]{2,1,0:T(8,128)(2,1)}, bf16[2,128,512]{2,1,0:T(8,128)(2,1)S(1)}, u32[]{:S(2)}) copy-start(bf16[2,128,512]{2,1,0:T(8,128)(2,1)S(1)} %collective-permute-done.4.refs_1_) | copy-start | bytes 786436
  37.5 13.3 %collective-permute-start.13 = (bf16[256,512]{1,0:T(8,128)(2,1)S(1)}, bf16[256,512]{1,0:T(8,128)(2,1)S(1)}, u32[]{:S(2)}, u32[]{:S(2)}) collective-permute-start(bf16[256,512]{1,0:T(8,128)(2,1)S(1)} %collective-permute-done.12.refs_8_), channel_id=1, source_target_pairs={{0,4},{4,0},{8,12},{12,8},{16,20},{20,16},{24,28},{28,24},{1,5},{5... | collective-permute-start | bytes 786440 | tf_op jit(solution)/shard_map/ppermute | solution.py:154
  43.0 12.5 %copy-start.21 = (bf16[2,128,512]{2,1,0:T(8,128)(2,1)}, bf16[2,128,512]{2,1,0:T(8,128)(2,1)S(1)}, u32[]{:S(2)}) copy-start(bf16[2,128,512]{2,1,0:T(8,128)(2,1)S(1)} %collective-permute-done.7.refs_2_) | copy-start | bytes 786436
  43.0 7.8 %collective-permute-start.8 = (bf16[2,128,512]{2,1,0:T(8,128)(2,1)S(1)}, bf16[2,128,512]{2,1,0:T(8,128)(2,1)S(1)}, u32[]{:S(2)}, u32[]{:S(2)}) collective-permute-start(bf16[2,128,512]{2,1,0:T(8,128)(2,1)S(1)} %collective-permute-done.7.refs_2_), channel_id=1, source_target_pairs={{0,1},{1,0},{2,3},{3,2},{4,5},{5,4},{6,7},{7,6},{8,9},{9,8},{10,11... | collective-permute-start | bytes 786440 | tf_op jit(solution)/shard_map/ppermute | solution.py:199
  45.6 9.9 %copy-start.5 = (bf16[256,512]{1,0:T(8,128)(2,1)}, bf16[256,512]{1,0:T(8,128)(2,1)S(1)}, u32[]{:S(2)}) copy-start(bf16[256,512]{1,0:T(8,128)(2,1)S(1)} %collective-permute-done.14.refs_10_) | copy-start | bytes 786436
  45.6 9.9 %collective-permute-start.15 = (bf16[256,512]{1,0:T(8,128)(2,1)S(1)}, bf16[256,512]{1,0:T(8,128)(2,1)S(1)}, u32[]{:S(2)}, u32[]{:S(2)}) collective-permute-start(bf16[256,512]{1,0:T(8,128)(2,1)S(1)} %collective-permute-done.14.refs_10_), channel_id=1, source_target_pairs={{0,4},{4,0},{8,12},{12,8},{16,20},{20,16},{24,28},{28,24},{1,5},{5... | collective-permute-start | bytes 786440 | tf_op jit(solution)/shard_map/ppermute | solution.py:154
  48.4 12.8 %collective-permute-start.17 = (bf16[2,128,512]{2,1,0:T(8,128)(2,1)S(1)}, bf16[2,128,512]{2,1,0:T(8,128)(2,1)S(1)}, u32[]{:S(2)}, u32[]{:S(2)}) collective-permute-start(bf16[2,128,512]{2,1,0:T(8,128)(2,1)S(1)} %copy-done.9), channel_id=1, source_target_pairs={{0,1},{1,0},{2,3},{3,2},{4,5},{5,4},{6,7},{7,6},{8,9},{9,8},{10,11... | collective-permute-start | bytes 786440 | tf_op jit(solution)/shard_map/ppermute | solution.py:199
  48.5 11.0 %copy-start.22 = (bf16[2,128,512]{2,1,0:T(8,128)(2,1)}, bf16[2,128,512]{2,1,0:T(8,128)(2,1)S(1)}, u32[]{:S(2)}) copy-start(bf16[2,128,512]{2,1,0:T(8,128)(2,1)S(1)} %collective-permute-done.18.refs_2_) | copy-start | bytes 786436
  48.5 12.7 %collective-permute-start.19 = (bf16[2,128,512]{2,1,0:T(8,128)(2,1)S(1)}, bf16[2,128,512]{2,1,0:T(8,128)(2,1)S(1)}, u32[]{:S(2)}, u32[]{:S(2)}) collective-permute-start(bf16[2,128,512]{2,1,0:T(8,128)(2,1)S(1)} %collective-permute-done.18.refs_2_), channel_id=1, source_target_pairs={{0,1},{1,0},{2,3},{3,2},{4,5},{5,4},{6,7},{7,6},{8,9},{9,8},{10,11... | collective-permute-start | bytes 786440 | tf_op jit(solution)/shard_map/ppermute | solution.py:199
  61.2 8.2 %collective-permute-start.16 = (bf16[128,512]{1,0:T(8,128)(2,1)S(1)}, bf16[128,512]{1,0:T(8,128)(2,1)S(1)}, u32[]{:S(2)}, u32[]{:S(2)}) collective-permute-start(bf16[128,512]{1,0:T(8,128)(2,1)S(1)} %get-tuple-element.22), channel_id=1, source_target_pairs={{0,1},{1,0},{2,3},{3,2},{4,5},{5,4},{6,7},{7,6},{8,9},{9,8},{10,11... | collective-permute-start | bytes 393224 | tf_op jit(solution)/shard_map/ppermute | solution.py:199
  66.9 6.4 %collective-permute-start.20 = (bf16[128,512]{1,0:T(8,128)(2,1)S(1)}, bf16[128,512]{1,0:T(8,128)(2,1)S(1)}, u32[]{:S(2)}, u32[]{:S(2)}) collective-permute-start(bf16[128,512]{1,0:T(8,128)(2,1)S(1)} %get-tuple-element.21), channel_id=1, source_target_pairs={{0,2},{1,3},{2,0},{3,1},{4,6},{5,7},{6,4},{7,5},{8,10},{9,11},{10,... | collective-permute-start | bytes 393224 | tf_op jit(solution)/shard_map/ppermute | solution.py:192
  68.5 6.8 %collective-permute-start.21 = (bf16[128,512]{1,0:T(8,128)(2,1)S(1)}, bf16[128,512]{1,0:T(8,128)(2,1)S(1)}, u32[]{:S(2)}, u32[]{:S(2)}) collective-permute-start(bf16[128,512]{1,0:T(8,128)(2,1)S(1)} %get-tuple-element.20), channel_id=1, source_target_pairs={{0,3},{1,2},{2,1},{3,0},{4,7},{5,6},{6,5},{7,4},{8,11},{9,10},{10,... | collective-permute-start | bytes 393224 | tf_op jit(solution)/shard_map/ppermute | solution.py:196
  (22 other events, 69.7 us)

commit v2 on v1

v2 whole, which is shorter than its diff:
```python
import functools
import math

import jax
import jax.numpy as jnp
from jax import lax
from jax.experimental import pallas as pl
from jax.experimental.pallas import tpu as pltpu
from jax.sharding import PartitionSpec as P

HEAD_DIM = 128

beta_one = 0.9
beta_two = 0.999
learn_rate = 0.003
weight_decay = 0.1
epsilon = 1e-08
step_count = 10.0


def adam_update(master_weight, first_moment, second_moment, gradient):
    new_first = beta_one * first_moment + (1.0 - beta_one) * gradient
    new_second = beta_two * second_moment + (1.0 - beta_two) * gradient * gradient
    first_hat = new_first / (1.0 - beta_one**step_count)
    second_hat = new_second / (1.0 - beta_two**step_count)
    new_master = master_weight - learn_rate * (
        first_hat / (jnp.sqrt(second_hat) + epsilon) + weight_decay * master_weight
    )
    return (new_master, new_first, new_second)


ATTEND_US = 3
PROJECT_US = 2

SMALL = pltpu.CompilerParams(vmem_limit_bytes=16 * 1024 * 1024)
IN_VMEM = pl.BlockSpec(memory_space=pltpu.VMEM)
IN_SMEM = pl.BlockSpec(memory_space=pltpu.SMEM)


def estimate(micros):
    return pl.CostEstimate(flops=0, bytes_accessed=int(micros * 3.69e6), transcendentals=0)


def chip_and_core():
    me = lax.axis_index("seq")
    return lax.shift_right_logical(me, 1), lax.bitwise_and(me, 1)


def turned(position, step, size):
    moved = position + step
    return jnp.where(moved >= size, moved - size, moved)


def cut_kernel(n_arrays, *refs):
    arrays, blocks, sems = refs[:n_arrays], refs[n_arrays:-1], refs[-1]
    chips = len(blocks) // 2
    chip, core = chip_and_core()
    copies = []
    for i, block in enumerate(blocks):
        group = 2 * turned(chip, i // 2, chips) + (core if i % 2 == 0 else 1 - core)
        wide = block.shape[-1]
        lanes = pl.ds(pl.multiple_of(group * wide, wide), wide)
        for j, array in enumerate(arrays):
            target = block if n_arrays == 1 else block.at[j]
            copies.append(pltpu.make_async_copy(array.at[:, lanes], target, sems.at[i, j]))
    for copy in copies:
        copy.start()
    for copy in copies:
        copy.wait()


def cut(*arrays):
    groups = lax.axis_size("seq")
    rows, width = arrays[0].shape
    shape = (rows, width // groups)
    if len(arrays) > 1:
        shape = (len(arrays),) + shape
    return pl.pallas_call(
        functools.partial(cut_kernel, len(arrays)),
        out_shape=[jax.ShapeDtypeStruct(shape, jnp.bfloat16)] * groups,
        in_specs=[pl.BlockSpec(memory_space=pl.ANY)] * len(arrays),
        out_specs=[pl.BlockSpec(memory_space=pl.ANY)] * groups,
        scratch_shapes=[pltpu.SemaphoreType.DMA((groups, len(arrays)))],
        compiler_params=SMALL,
        cost_estimate=estimate(1),
        name="cut",
    )(*arrays)


def attend_kernel(n_keys, count_ref, *refs):
    query_refs, pair_refs = refs[:2], refs[2 : 2 + n_keys]
    out_ref, keys, values = refs[2 + n_keys :]
    rows, wide = query_refs[0].shape
    chips = n_keys // 2
    chip, core = chip_and_core()
    columns = []
    for i, ref in enumerate(pair_refs):
        keys[i * rows : (i + 1) * rows, :] = ref[0]
        values[i * rows : (i + 1) * rows, :] = ref[1]
        source = 2 * turned(chip, (chips - i // 2) % chips, chips) + (core if i % 2 == 0 else 1 - core)
        columns.append(source * rows + lax.broadcasted_iota(jnp.int32, (1, rows), 1))
    valid = jnp.concatenate(columns, axis=1) < count_ref[0]
    factor = HEAD_DIM ** (-0.5) * math.log2(math.e)
    for block, query_ref in enumerate(query_refs):
        for head in range(wide // HEAD_DIM):
            lanes = slice(head * HEAD_DIM, (head + 1) * HEAD_DIM)
            scores = lax.dot_general(
                query_ref[:, lanes],
                keys[:, lanes],
                (((1,), (1,)), ((), ())),
                preferred_element_type=jnp.float32,
            )
            scores = jnp.where(valid, scores, -1e30)
            top = jnp.max(scores, axis=1, keepdims=True)
            expo = jnp.exp2((scores - top) * factor)
            total = jnp.sum(expo, axis=1, keepdims=True)
            weights = (expo * (1.0 / total)).astype(jnp.bfloat16)
            out_ref[block, :, lanes] = jnp.dot(
                weights, values[:, lanes], preferred_element_type=jnp.float32
            ).astype(jnp.bfloat16)


def attend(counts, query_blocks, pairs):
    rows, wide = query_blocks[0].shape
    n_keys = len(pairs)
    return pl.pallas_call(
        functools.partial(attend_kernel, n_keys),
        out_shape=jax.ShapeDtypeStruct((2, rows, wide), jnp.bfloat16),
        in_specs=[IN_SMEM] + [IN_VMEM] * (2 + n_keys),
        out_specs=IN_VMEM,
        scratch_shapes=[pltpu.VMEM((n_keys * rows, wide), jnp.bfloat16)] * 2,
        compiler_params=SMALL,
        cost_estimate=estimate(ATTEND_US),
        name="attend",
    )(counts, *query_blocks, *pairs)


def project_kernel(n_att, steps, bucket_ref, *refs):
    att_refs, weight_refs = refs[:n_att], refs[n_att : n_att + 2 * len(steps)]
    out_ref, other_ref, held = refs[n_att + 2 * len(steps) :]
    _, rows, wide = att_refs[0].shape
    depth = weight_refs[0].shape[0]
    parts = wide // depth
    chip, core = chip_and_core()
    owner = lax.axis_index("dp")
    ring = lax.axis_size("dp") // 2
    spot, side = lax.shift_right_logical(owner, 1), lax.bitwise_and(owner, 1)
    for slot, ref in enumerate(att_refs):
        for block in range(2):
            for part in range(parts):
                held[slot * parts + part, block * rows : (block + 1) * rows, :] = ref[
                    block ^ (slot % 2), :, part * depth : (part + 1) * depth
                ]
    total = None
    for i, ref in enumerate(weight_refs):
        from_owner = 2 * turned(spot, steps[i // 2], ring) + (side if i % 2 == 0 else 1 - side)
        bucket = bucket_ref[from_owner]
        group, part = lax.div(bucket, parts), lax.rem(bucket, parts)
        group_chip, group_core = lax.shift_right_logical(group, 1), lax.bitwise_and(group, 1)
        back = chip - group_chip
        back = jnp.where(back < 0, back + n_att // 2, back)
        slot = 2 * back + lax.bitwise_xor(group_core, core)
        term = jnp.dot(held[slot * parts + part], ref[...], preferred_element_type=jnp.float32)
        total = term if total is None else total + term
    total = total.astype(jnp.bfloat16)
    out_ref[...] = total[:rows]
    other_ref[...] = total[rows:]


def project(owner_bucket, att, steps, weights):
    _, rows, wide = att[0].shape
    depth, columns = weights[0].shape
    return pl.pallas_call(
        functools.partial(project_kernel, len(att), steps),
        out_shape=[jax.ShapeDtypeStruct((rows, columns), jnp.bfloat16)] * 2,
        in_specs=[IN_SMEM] + [IN_VMEM] * (len(att) + len(weights)),
        out_specs=[IN_VMEM] * 2,
        scratch_shapes=[pltpu.VMEM((len(att) * wide // depth, 2 * rows, depth), jnp.bfloat16)],
        compiler_params=SMALL,
        cost_estimate=estimate(PROJECT_US),
        name="project",
    )(owner_bucket, *att, *weights)


def place_kernel(n, *refs):
    out_ref = refs[n]
    columns = refs[0].shape[1]
    chip, core = chip_and_core()
    for i in range(n):
        group = 2 * turned(chip, i // 2, n // 2) + (core if i % 2 == 0 else 1 - core)
        out_ref[:, pl.ds(pl.multiple_of(group * columns, columns), columns)] = refs[i][...]


def place(blocks):
    rows, columns = blocks[0].shape
    return pl.pallas_call(
        functools.partial(place_kernel, len(blocks)),
        out_shape=jax.ShapeDtypeStruct((rows, columns * len(blocks)), jnp.bfloat16),
        in_specs=[IN_VMEM] * len(blocks),
        out_specs=IN_VMEM,
        compiler_params=SMALL,
        cost_estimate=estimate(1),
        name="place",
    )(*blocks)


def gather_weights(shard):
    owners = lax.axis_size("dp")
    ring = owners // 2

    def moved(block, step):
        perm = [(o, (o // 2 + step) % ring * 2 + o % 2) for o in range(owners)]
        return lax.ppermute(block, "dp", perm)

    def swapped(block):
        return lax.ppermute(block, "dp", [(o, o ^ 1) for o in range(owners)])

    steps, held = [0], [shard]
    ahead, back = shard, shard
    for step in range(1, ring // 2 + 1):
        ahead = moved(ahead, 1)
        held.append(ahead)
        steps.append((-step) % ring)
        if step <= (ring - 1) // 2:
            back = moved(back, -1)
            held.append(back)
            steps.append(step)
    blocks = []
    for block in held:
        blocks += [block, swapped(block)]
    return steps, blocks


def body(
    queries,
    hit_keys,
    hit_values,
    hit_counts,
    master_weight,
    first_moment,
    second_moment,
    gradient,
    owner_bucket,
):
    groups = lax.axis_size("seq")
    chips = groups // 2

    def to_same(array, step):
        perm = [(s, (s // 2 + step) % chips * 2 + s % 2) for s in range(groups)]
        return lax.ppermute(array, "seq", perm)

    def to_cross(array, step):
        perm = [(s, (s // 2 + step) % chips * 2 + 1 - s % 2) for s in range(groups)]
        return lax.ppermute(array, "seq", perm)

    def to_sibling(array):
        return lax.ppermute(array, "seq", [(s, s ^ 1) for s in range(groups)])

    def exchanged(blocks):
        got = [blocks[0], to_sibling(blocks[1])]
        for step in range(1, chips):
            got += [to_same(blocks[2 * step], step), to_cross(blocks[2 * step + 1], step)]
        return got

    pairs = exchanged(cut(hit_keys[0], hit_values[0]))
    new_master, new_first, new_second = adam_update(
        master_weight, first_moment, second_moment, gradient
    )
    steps, weights = gather_weights(new_master[0].astype(jnp.bfloat16))
    asked = exchanged(cut(queries[0]))

    attended = [attend(hit_counts, asked[2 * e : 2 * e + 2], pairs) for e in range(chips)]
    spread = [attended] + [[to_same(a, step) for a in attended] for step in range(1, chips)]
    beside = [[to_sibling(a) for a in row] for row in spread]

    columns = [None] * groups
    for e in list(range(1, chips)) + [0]:
        att = []
        for d in range(chips):
            att += [spread[d][(e - d) % chips], beside[d][(e - d) % chips]]
        out, other = project(owner_bucket, att, steps, weights)
        if e == 0:
            columns[0], columns[1] = out, to_sibling(other)
        else:
            columns[2 * e] = to_same(out, chips - e)
            columns[2 * e + 1] = to_cross(other, chips - e)
    projected = place(columns)[None]
    return (projected, new_master, new_first, new_second)


def solution(mesh):
    return jax.shard_map(
        body,
        mesh=mesh,
        in_specs=(
            P("dp", "seq", None),
            P("dp", "seq", None),
            P("dp", "seq", None),
            P("dp"),
            P("dp", None, "seq"),
            P("dp", None, "seq"),
            P("dp", None, "seq"),
            P("dp", None, "seq"),
            P(),
        ),
        out_specs=(
            P("dp", "seq", None),
            P("dp", None, "seq"),
            P("dp", None, "seq"),
            P("dp", None, "seq"),
        ),
        check_vma=False,
    )
```

time: 78.2 us -> 58.6 us (0.75)
  Pallas kernels: 18.3 us -> 9.54 us
  local copies, waits for them, and re-layouts: 9.58 us -> 2.1 us
  waiting for transfers between devices: 23.4 us -> 19.4 us
  starting transfers between devices: 21.5 us -> 23.4 us
    ppermute x5, waiting for transfers between devices: 9.1 us -> 1.93 us  [to_same(): return lax.ppermute(array, 'seq', perm)]
    pallas_call x2, Pallas kernels: 9.82 us -> 5.76 us  [attend(): pl.pallas_call(functools.partial(attend_kernel, n_keys), out_shape=jax.Sh...]
    pallas_call x2 -> x4, Pallas kernels: 6.58 us -> 2.94 us  [the longest x2 2.58 us: project(): pl.pallas_call(functools.partial(project_kernel, len(att), steps), out_sh...]
    squeeze x2 -> x0, local copies, waits for them, and re-layouts: 2.63 us -> none  [the longest x1 1.64 us: body(): columns[0], columns[1] = (out[0], to_sibling(out[1]))]
    ppermute x3, waiting for transfers between devices: 2.56 us -> 4.84 us  [moved(): return lax.ppermute(block, 'dp', perm)]
    ppermute x4, waiting for transfers between devices: 6.51 us -> 8.67 us  [swapped(): return lax.ppermute(block, 'dp', [(o, o ^ 1) for o in range(owners)])]
    dynamic_slice x2 -> x0, local copies, waits for them, and re-layouts: 1.99 us -> none  [cut(): return lax.dynamic_slice_in_dim(array, group * wide, wide, 1)]
    ppermute x3, starting transfers between devices: 0.7 us -> 2.26 us  [to_cross(): return lax.ppermute(array, 'seq', perm)]
  transfers between devices with their start and end apart: 22 -> 22, of which waited for: 8 -> 7; matrix products, arithmetic and copies ran while one was open for 10% -> 5% of each run, Pallas kernels for 21% -> 14%
where the time goes in v2:
time: 58.6 us; the launch traced here: 58.4 us
  starting transfers between devices  23.4 us (40%)
  waiting for transfers between devices  19.4 us (33%)
  Pallas kernels  9.54 us (16%)
  other arithmetic  2.64 us (5%)
  local copies, waits for them, and re-layouts  2.1 us (4%)
  between operations  1.39 us (2%)
    ppermute x4, waiting for transfers between devices, swapped(): return lax.ppermute(block, 'dp', [(o, o ^ 1) for o in range(owners)])  8.67 us
    ppermute x5, starting transfers between devices, to_same(): return lax.ppermute(array, 'seq', perm)  7.32 us
    pallas_call x2, Pallas kernels, attend(): pl.pallas_call(functools.partial(attend_kernel, n_keys), out_shape=jax.Sh...  5.76 us
    ppermute x4, starting transfers between devices, swapped(): return lax.ppermute(block, 'dp', [(o, o ^ 1) for o in range(owners)])  5.72 us
    ppermute x3, starting transfers between devices, moved(): return lax.ppermute(block, 'dp', perm)  5.68 us
    ppermute x3, waiting for transfers between devices, moved(): return lax.ppermute(block, 'dp', perm)  4.84 us
    ppermute x3, waiting for transfers between devices, to_cross(): return lax.ppermute(array, 'seq', perm)  3.9 us
    convert_element_type x1, other arithmetic, body(): steps, weights = gather_weights(new_master[0].astype(jnp.bfloat16))  2.64 us
  transfers between devices with their start and end apart: 22, of which 7 were waited for; matrix products, arithmetic and copies ran while one was open for 5% of the time, Pallas kernels for 14%

profile of v2, /device:TPU:0, one launch (start us, length us, event | category | flops | bytes accessed | tf_op | source)
XLA Modules:
  0.0 58.4 jit_solution(12122334968816414235)
XLA Ops:
  0.6 1.0 %copy-done = bf16[1,128,2048]{2,1,0:T(8,128)(2,1)S(1)} copy-done((bf16[1,128,2048]{2,1,0:T(8,128)(2,1)S(1)}, bf16[1,128,2048]{2,1,0:T(8,128)(2,1)}, u32[]{:S(2)}) %copy-start) | copy-done | bytes 524312
  1.7 1.0 %copy-done.1 = bf16[1,128,2048]{2,1,0:T(8,128)(2,1)S(1)} copy-done((bf16[1,128,2048]{2,1,0:T(8,128)(2,1)S(1)}, bf16[1,128,2048]{2,1,0:T(8,128)(2,1)}, u32[]{:S(2)}) %copy-start.1) | copy-done | bytes 524312
  2.7 0.2 cut.3
  3.0 0.5 collective-permute-start.1
  3.5 2.6 %collective-permute-start.2 = (bf16[2,128,512]{2,1,0:T(8,128)(2,1)S(1)}, bf16[2,128,512]{2,1,0:T(8,128)(2,1)S(1)}, u32[]{:S(2)}, u32[]{:S(2)}) collective-permute-start(bf16[2,128,512]{2,1,0:T(8,128)(2,1)S(1)} %get-tuple-element.20), channel_id=1, source_target_pairs={{0,2},{1,3},{2,0},{3,1},{4,6},{5,7},{6,4},{7,5},{8,10},{9,11},{10,... | collective-permute-start | bytes 786440 | tf_op jit(solution)/shard_map/ppermute | solution.py:250
  6.3 0.2 collective-permute-start
  6.5 2.6 %convert_bitcast_fusion = (bf16[256,512]{1,0:T(8,128)(2,1)S(1)}, f32[1,256,512]{2,1,0:T(8,128)}, f32[1,256,512]{2,1,0:T(8,128)}, f32[1,256,512]{2,1,0:T(8,128)}) fusion(f32[1,256,512]{2,1,0:T(8,128)S(1)} %copy-done.4, f32[1,256,512]{2,1,0:T(8,128)S(1)} %copy-done.5, f32[1,256,512]{2,1,0:T(8,128)} %param.14, f32[1,256,512]{2,1,0:T(8,128)} %param.15), kind=kLoop, calls=%fused_computation.4 | loop fusion | flops 2097152 | bytes 3932160 | tf_op jit(solution)/shard_map/convert_element_type | solution.py:269
  9.1 2.0 %collective-permute-start.10 = (bf16[256,512]{1,0:T(8,128)(2,1)S(1)}, bf16[256,512]{1,0:T(8,128)(2,1)S(1)}, u32[]{:S(2)}, u32[]{:S(2)}) collective-permute-start(bf16[256,512]{1,0:T(8,128)(2,1)S(1)} %get-tuple-element.28.refs_4_), channel_id=1, source_target_pairs={{0,8},{4,12},{8,16},{12,20},{16,24},{20,28},{24,0},{28,4},{1,9},{5... | collective-permute-start | bytes 786440 | tf_op jit(solution)/shard_map/ppermute | solution.py:213
  11.1 2.1 %collective-permute-start.12 = (bf16[256,512]{1,0:T(8,128)(2,1)S(1)}, bf16[256,512]{1,0:T(8,128)(2,1)S(1)}, u32[]{:S(2)}, u32[]{:S(2)}) collective-permute-start(bf16[256,512]{1,0:T(8,128)(2,1)S(1)} %get-tuple-element.28.refs_4_), channel_id=1, source_target_pairs={{0,24},{4,28},{8,0},{12,4},{16,8},{20,12},{24,16},{28,20},{1,25},{... | collective-permute-start | bytes 786440 | tf_op jit(solution)/shard_map/ppermute | solution.py:213
  13.2 1.7 %collective-permute-start.9 = (bf16[256,512]{1,0:T(8,128)(2,1)S(1)}, bf16[256,512]{1,0:T(8,128)(2,1)S(1)}, u32[]{:S(2)}, u32[]{:S(2)}) collective-permute-start(bf16[256,512]{1,0:T(8,128)(2,1)S(1)} %get-tuple-element.28.refs_4_), channel_id=1, source_target_pairs={{0,4},{4,0},{8,12},{12,8},{16,20},{20,16},{24,28},{28,24},{1,5},{5... | collective-permute-start | bytes 786440 | tf_op jit(solution)/shard_map/ppermute | solution.py:216
  14.9 1.5 %collective-permute-start.5 = (bf16[128,512]{1,0:T(8,128)(2,1)S(1)}, bf16[128,512]{1,0:T(8,128)(2,1)S(1)}, u32[]{:S(2)}, u32[]{:S(2)}) collective-permute-start(bf16[128,512]{1,0:T(8,128)(2,1)S(1)} %get-tuple-element.22), channel_id=1, source_target_pairs={{0,2},{1,3},{2,0},{3,1},{4,6},{5,7},{6,4},{7,5},{8,10},{9,11},{10,... | collective-permute-start | bytes 393224 | tf_op jit(solution)/shard_map/ppermute | solution.py:250
  16.4 1.9 %collective-permute-done.3.refs_5_ = bf16[2,128,512]{2,1,0:T(8,128)(2,1)S(1)} collective-permute-done((bf16[2,128,512]{2,1,0:T(8,128)(2,1)S(1)}, bf16[2,128,512]{2,1,0:T(8,128)(2,1)S(1)}, u32[]{:S(2)}, u32[]{:S(2)}) %collective-permute-start.3) | collective-permute-done | bytes 262176 | tf_op jit(solution)/shard_map/ppermute | solution.py:254
  18.3 2.2 %collective-permute-start.6 = (bf16[128,512]{1,0:T(8,128)(2,1)S(1)}, bf16[128,512]{1,0:T(8,128)(2,1)S(1)}, u32[]{:S(2)}, u32[]{:S(2)}) collective-permute-start(bf16[128,512]{1,0:T(8,128)(2,1)S(1)} %get-tuple-element.23), channel_id=1, source_target_pairs={{0,3},{1,2},{2,1},{3,0},{4,7},{5,6},{6,5},{7,4},{8,11},{9,10},{10,... | collective-permute-start | bytes 393224 | tf_op jit(solution)/shard_map/ppermute | solution.py:254
  21.2 2.9 %attend.2.refs_0_ = bf16[2,128,512]{2,1,0:T(8,128)(2,1)S(1)} custom-call(s32[1]{0:T(128)S(6)} %copy.13.count_ref, bf16[128,512]{1,0:T(8,128)(2,1)S(1)} %get-tuple-element.16.refs_0_, bf16[128,512]{1,0:T(8,128)(2,1)S(1)} %collective-permute-done.refs_1_, bf16[2,128,512]{2,1,0:T(8,128)(2,1)S(1)} %get-tuple-element.18.refs_2_, ...), custom_call_target="tpu_custom_call" | custom-call | bytes 11070000 | tf_op jit(solution)/shard_map/attend/pallas_call | solution.py:126
  24.3 2.9 %attend.3.refs_0_ = bf16[2,128,512]{2,1,0:T(8,128)(2,1)S(1)} custom-call(s32[1]{0:T(128)S(6)} %copy.13.count_ref, bf16[128,512]{1,0:T(8,128)(2,1)S(1)} %collective-permute-done.5.refs_0_, bf16[128,512]{1,0:T(8,128)(2,1)S(1)} %collective-permute-done.6.refs_1_, bf16[2,128,512]{2,1,0:T(8,128)(2,1)S(1)} %get-tuple-element.18.refs_2_, ...), custom_call_target="tpu_custom_call" | custom-call | bytes 11070000 | tf_op jit(solution)/shard_map/attend/pallas_call | solution.py:126
  27.2 0.5 collective-permute-start.17
  27.6 1.6 %collective-permute-start.14 = (bf16[256,512]{1,0:T(8,128)(2,1)S(1)}, bf16[256,512]{1,0:T(8,128)(2,1)S(1)}, u32[]{:S(2)}, u32[]{:S(2)}) collective-permute-start(bf16[256,512]{1,0:T(8,128)(2,1)S(1)} %collective-permute-done.10.refs_6_), channel_id=1, source_target_pairs={{0,8},{4,12},{8,16},{12,20},{16,24},{20,28},{24,0},{28,4},{1,9},{5... | collective-permute-start | bytes 786440 | tf_op jit(solution)/shard_map/ppermute | solution.py:213
  29.3 1.5 %collective-permute-start.11 = (bf16[256,512]{1,0:T(8,128)(2,1)S(1)}, bf16[256,512]{1,0:T(8,128)(2,1)S(1)}, u32[]{:S(2)}, u32[]{:S(2)}) collective-permute-start(bf16[256,512]{1,0:T(8,128)(2,1)S(1)} %collective-permute-done.10.refs_6_), channel_id=1, source_target_pairs={{0,4},{4,0},{8,12},{12,8},{16,20},{20,16},{24,28},{28,24},{1,5},{5... | collective-permute-start | bytes 786440 | tf_op jit(solution)/shard_map/ppermute | solution.py:216
  30.8 1.5 %collective-permute-start.7 = (bf16[2,128,512]{2,1,0:T(8,128)(2,1)S(1)}, bf16[2,128,512]{2,1,0:T(8,128)(2,1)S(1)}, u32[]{:S(2)}, u32[]{:S(2)}) collective-permute-start(bf16[2,128,512]{2,1,0:T(8,128)(2,1)S(1)} %attend.3.refs_0_), channel_id=1, source_target_pairs={{0,2},{1,3},{2,0},{3,1},{4,6},{5,7},{6,4},{7,5},{8,10},{9,11},{10,... | collective-permute-start | bytes 786440 | tf_op jit(solution)/shard_map/ppermute | solution.py:250
  32.3 1.1 %collective-permute-start.13 = (bf16[256,512]{1,0:T(8,128)(2,1)S(1)}, bf16[256,512]{1,0:T(8,128)(2,1)S(1)}, u32[]{:S(2)}, u32[]{:S(2)}) collective-permute-start(bf16[256,512]{1,0:T(8,128)(2,1)S(1)} %collective-permute-done.12.refs_8_), channel_id=1, source_target_pairs={{0,4},{4,0},{8,12},{12,8},{16,20},{20,16},{24,28},{28,24},{1,5},{5... | collective-permute-start | bytes 786440 | tf_op jit(solution)/shard_map/ppermute | solution.py:216
  33.4 4.8 %collective-permute-done.14.refs_10_ = bf16[256,512]{1,0:T(8,128)(2,1)S(1)} collective-permute-done((bf16[256,512]{1,0:T(8,128)(2,1)S(1)}, bf16[256,512]{1,0:T(8,128)(2,1)S(1)}, u32[]{:S(2)}, u32[]{:S(2)}) %collective-permute-start.14) | collective-permute-done | bytes 262176 | tf_op jit(solution)/shard_map/ppermute | solution.py:213
  38.2 1.5 %collective-permute-start.15 = (bf16[256,512]{1,0:T(8,128)(2,1)S(1)}, bf16[256,512]{1,0:T(8,128)(2,1)S(1)}, u32[]{:S(2)}, u32[]{:S(2)}) collective-permute-start(bf16[256,512]{1,0:T(8,128)(2,1)S(1)} %collective-permute-done.14.refs_10_), channel_id=1, source_target_pairs={{0,4},{4,0},{8,12},{12,8},{16,20},{20,16},{24,28},{28,24},{1,5},{5... | collective-permute-start | bytes 786440 | tf_op jit(solution)/shard_map/ppermute | solution.py:216
  39.7 0.5 collective-permute-start.8
  40.2 3.8 %collective-permute-done.13.refs_9_ = bf16[256,512]{1,0:T(8,128)(2,1)S(1)} collective-permute-done((bf16[256,512]{1,0:T(8,128)(2,1)S(1)}, bf16[256,512]{1,0:T(8,128)(2,1)S(1)}, u32[]{:S(2)}, u32[]{:S(2)}) %collective-permute-start.13) | collective-permute-done | bytes 262176 | tf_op jit(solution)/shard_map/ppermute | solution.py:216
  44.0 4.8 %collective-permute-done.15.refs_11_ = bf16[256,512]{1,0:T(8,128)(2,1)S(1)} collective-permute-done((bf16[256,512]{1,0:T(8,128)(2,1)S(1)}, bf16[256,512]{1,0:T(8,128)(2,1)S(1)}, u32[]{:S(2)}, u32[]{:S(2)}) %collective-permute-start.15) | collective-permute-done | bytes 262176 | tf_op jit(solution)/shard_map/ppermute | solution.py:216
  48.9 1.3 %project.3 = (bf16[128,512]{1,0:T(8,128)(2,1)S(1)}, bf16[128,512]{1,0:T(8,128)(2,1)S(1)}) custom-call(s32[8]{0:T(128)S(1)} %copy-done.3, bf16[2,128,512]{2,1,0:T(8,128)(2,1)S(1)} %attend.3.refs_0_, bf16[2,128,512]{2,1,0:T(8,128)(2,1)S(1)} %collective-permute-done.17.refs_1_, bf16[2,128,512]{2,1,0:T(8,128)(2,1)S(1)} %collective-permute-done.18.refs_2_, ...), custom_call_target="tpu_custom_call" | custom-call | bytes 7380000 | tf_op jit(solution)/shard_map/project/pallas_call | solution.py:173
  50.2 1.6 %collective-permute-start.20 = (bf16[128,512]{1,0:T(8,128)(2,1)S(1)}, bf16[128,512]{1,0:T(8,128)(2,1)S(1)}, u32[]{:S(2)}, u32[]{:S(2)}) collective-permute-start(bf16[128,512]{1,0:T(8,128)(2,1)S(1)} %get-tuple-element.26), channel_id=1, source_target_pairs={{0,2},{1,3},{2,0},{3,1},{4,6},{5,7},{6,4},{7,5},{8,10},{9,11},{10,... | collective-permute-start | bytes 393224 | tf_op jit(solution)/shard_map/ppermute | solution.py:250
  51.8 1.3 %project.2 = (bf16[128,512]{1,0:T(8,128)(2,1)S(1)}, bf16[128,512]{1,0:T(8,128)(2,1)S(1)}) custom-call(s32[8]{0:T(128)S(1)} %copy-done.3, bf16[2,128,512]{2,1,0:T(8,128)(2,1)S(1)} %attend.2.refs_0_, bf16[2,128,512]{2,1,0:T(8,128)(2,1)S(1)} %collective-permute-done.4.refs_1_, bf16[2,128,512]{2,1,0:T(8,128)(2,1)S(1)} %collective-permute-done.7.refs_2_, ...), custom_call_target="tpu_custom_call" | custom-call | bytes 7380000 | tf_op jit(solution)/shard_map/project/pallas_call | solution.py:173
  53.1 0.7 %collective-permute-start.16 = (bf16[128,512]{1,0:T(8,128)(2,1)S(1)}, bf16[128,512]{1,0:T(8,128)(2,1)S(1)}, u32[]{:S(2)}, u32[]{:S(2)}) collective-permute-start(bf16[128,512]{1,0:T(8,128)(2,1)S(1)} %get-tuple-element.25), channel_id=1, source_target_pairs={{0,1},{1,0},{2,3},{3,2},{4,5},{5,4},{6,7},{7,6},{8,9},{9,8},{10,11... | collective-permute-start | bytes 393224 | tf_op jit(solution)/shard_map/ppermute | solution.py:257
  53.7 1.9 %collective-permute-done.20.refs_2_ = bf16[128,512]{1,0:T(8,128)(2,1)S(1)} collective-permute-done((bf16[128,512]{1,0:T(8,128)(2,1)S(1)}, bf16[128,512]{1,0:T(8,128)(2,1)S(1)}, u32[]{:S(2)}, u32[]{:S(2)}) %collective-permute-start.20) | collective-permute-done | bytes 131104 | tf_op jit(solution)/shard_map/ppermute | solution.py:250
  55.7 1.9 %collective-permute-done.21.refs_3_ = bf16[128,512]{1,0:T(8,128)(2,1)S(1)} collective-permute-done((bf16[128,512]{1,0:T(8,128)(2,1)S(1)}, bf16[128,512]{1,0:T(8,128)(2,1)S(1)}, u32[]{:S(2)}, u32[]{:S(2)}) %collective-permute-start.21) | collective-permute-done | bytes 131104 | tf_op jit(solution)/shard_map/ppermute | solution.py:254
  57.5 0.8 %place.1 = bf16[128,2048]{1,0:T(8,128)(2,1)} custom-call(bf16[128,512]{1,0:T(8,128)(2,1)S(1)} %get-tuple-element.24.refs_0_, bf16[128,512]{1,0:T(8,128)(2,1)S(1)} %collective-permute-done.16.refs_1_, bf16[128,512]{1,0:T(8,128)(2,1)S(1)} %collective-permute-done.20.refs_2_, bf16[128,512]{1,0:T(8,128)(2,1)S(1)} %collective-permute-done.21.refs_3_), custom_call_target="tpu_custom_call" | custom-call | bytes 3690000 | tf_op jit(solution)/shard_map/place/pallas_call | solution.py:196
  (32 shorter events, 0.5 us)
Async XLA Ops:
  0.6 1.0 %copy-start = (bf16[1,128,2048]{2,1,0:T(8,128)(2,1)S(1)}, bf16[1,128,2048]{2,1,0:T(8,128)(2,1)}, u32[]{:S(2)}) copy-start(bf16[1,128,2048]{2,1,0:T(8,128)(2,1)} %param.10) | copy-start | bytes 1572868
  1.7 1.0 %copy-start.1 = (bf16[1,128,2048]{2,1,0:T(8,128)(2,1)S(1)}, bf16[1,128,2048]{2,1,0:T(8,128)(2,1)}, u32[]{:S(2)}) copy-start(bf16[1,128,2048]{2,1,0:T(8,128)(2,1)} %param.11) | copy-start | bytes 1572868
  2.7 3.4 %copy-start.2 = (bf16[1,128,2048]{2,1,0:T(8,128)(2,1)S(1)}, bf16[1,128,2048]{2,1,0:T(8,128)(2,1)}, u32[]{:S(2)}) copy-start(bf16[1,128,2048]{2,1,0:T(8,128)(2,1)} %param.9) | copy-start | bytes 1572868
  2.7 3.8 %copy-start.5 = (f32[1,256,512]{2,1,0:T(8,128)S(1)}, f32[1,256,512]{2,1,0:T(8,128)}, u32[]{:S(2)}) copy-start(f32[1,256,512]{2,1,0:T(8,128)} %param.16) | copy-start | bytes 1572868
  3.0 3.5 %copy-start.4 = (f32[1,256,512]{2,1,0:T(8,128)S(1)}, f32[1,256,512]{2,1,0:T(8,128)}, u32[]{:S(2)}) copy-start(f32[1,256,512]{2,1,0:T(8,128)} %param.13) | copy-start | bytes 1572868
  3.0 10.2 %collective-permute-start.1 = (bf16[2,128,512]{2,1,0:T(8,128)(2,1)S(1)}, bf16[2,128,512]{2,1,0:T(8,128)(2,1)S(1)}, u32[]{:S(2)}, u32[]{:S(2)}) collective-permute-start(bf16[2,128,512]{2,1,0:T(8,128)(2,1)S(1)} %get-tuple-element.19), channel_id=1, source_target_pairs={{0,1},{1,0},{2,3},{3,2},{4,5},{5,4},{6,7},{7,6},{8,9},{9,8},{10,11... | collective-permute-start | bytes 786440 | tf_op jit(solution)/shard_map/ppermute | solution.py:257
  3.5 11.4 %collective-permute-start.2 = (bf16[2,128,512]{2,1,0:T(8,128)(2,1)S(1)}, bf16[2,128,512]{2,1,0:T(8,128)(2,1)S(1)}, u32[]{:S(2)}, u32[]{:S(2)}) collective-permute-start(bf16[2,128,512]{2,1,0:T(8,128)(2,1)S(1)} %get-tuple-element.20), channel_id=1, source_target_pairs={{0,2},{1,3},{2,0},{3,1},{4,6},{5,7},{6,4},{7,5},{8,10},{9,11},{10,... | collective-permute-start | bytes 786440 | tf_op jit(solution)/shard_map/ppermute | solution.py:250
  6.1 12.3 %collective-permute-start.3 = (bf16[2,128,512]{2,1,0:T(8,128)(2,1)S(1)}, bf16[2,128,512]{2,1,0:T(8,128)(2,1)S(1)}, u32[]{:S(2)}, u32[]{:S(2)}) collective-permute-start(bf16[2,128,512]{2,1,0:T(8,128)(2,1)S(1)} %get-tuple-element.21), channel_id=1, source_target_pairs={{0,3},{1,2},{2,1},{3,0},{4,7},{5,6},{6,5},{7,4},{8,11},{9,10},{10,... | collective-permute-start | bytes 786440 | tf_op jit(solution)/shard_map/ppermute | solution.py:254
  6.3 4.8 %collective-permute-start = (bf16[128,512]{1,0:T(8,128)(2,1)S(1)}, bf16[128,512]{1,0:T(8,128)(2,1)S(1)}, u32[]{:S(2)}, u32[]{:S(2)}) collective-permute-start(bf16[128,512]{1,0:T(8,128)(2,1)S(1)} %get-tuple-element.17), channel_id=1, source_target_pairs={{0,1},{1,0},{2,3},{3,2},{4,5},{5,4},{6,7},{7,6},{8,9},{9,8},{10,11... | collective-permute-start | bytes 393224 | tf_op jit(solution)/shard_map/ppermute | solution.py:257
  9.1 18.5 %collective-permute-start.10 = (bf16[256,512]{1,0:T(8,128)(2,1)S(1)}, bf16[256,512]{1,0:T(8,128)(2,1)S(1)}, u32[]{:S(2)}, u32[]{:S(2)}) collective-permute-start(bf16[256,512]{1,0:T(8,128)(2,1)S(1)} %get-tuple-element.28.refs_4_), channel_id=1, source_target_pairs={{0,8},{4,12},{8,16},{12,20},{16,24},{20,28},{24,0},{28,4},{1,9},{5... | collective-permute-start | bytes 786440 | tf_op jit(solution)/shard_map/ppermute | solution.py:213
  11.1 18.1 %collective-permute-start.12 = (bf16[256,512]{1,0:T(8,128)(2,1)S(1)}, bf16[256,512]{1,0:T(8,128)(2,1)S(1)}, u32[]{:S(2)}, u32[]{:S(2)}) collective-permute-start(bf16[256,512]{1,0:T(8,128)(2,1)S(1)} %get-tuple-element.28.refs_4_), channel_id=1, source_target_pairs={{0,24},{4,28},{8,0},{12,4},{16,8},{20,12},{24,16},{28,20},{1,25},{... | collective-permute-start | bytes 786440 | tf_op jit(solution)/shard_map/ppermute | solution.py:213
  13.2 17.6 %collective-permute-start.9 = (bf16[256,512]{1,0:T(8,128)(2,1)S(1)}, bf16[256,512]{1,0:T(8,128)(2,1)S(1)}, u32[]{:S(2)}, u32[]{:S(2)}) collective-permute-start(bf16[256,512]{1,0:T(8,128)(2,1)S(1)} %get-tuple-element.28.refs_4_), channel_id=1, source_target_pairs={{0,4},{4,0},{8,12},{12,8},{16,20},{20,16},{24,28},{28,24},{1,5},{5... | collective-permute-start | bytes 786440 | tf_op jit(solution)/shard_map/ppermute | solution.py:216
  14.9 9.2 %collective-permute-start.5 = (bf16[128,512]{1,0:T(8,128)(2,1)S(1)}, bf16[128,512]{1,0:T(8,128)(2,1)S(1)}, u32[]{:S(2)}, u32[]{:S(2)}) collective-permute-start(bf16[128,512]{1,0:T(8,128)(2,1)S(1)} %get-tuple-element.22), channel_id=1, source_target_pairs={{0,2},{1,3},{2,0},{3,1},{4,6},{5,7},{6,4},{7,5},{8,10},{9,11},{10,... | collective-permute-start | bytes 393224 | tf_op jit(solution)/shard_map/ppermute | solution.py:250
  18.3 6.0 %collective-permute-start.6 = (bf16[128,512]{1,0:T(8,128)(2,1)S(1)}, bf16[128,512]{1,0:T(8,128)(2,1)S(1)}, u32[]{:S(2)}, u32[]{:S(2)}) collective-permute-start(bf16[128,512]{1,0:T(8,128)(2,1)S(1)} %get-tuple-element.23), channel_id=1, source_target_pairs={{0,3},{1,2},{2,1},{3,0},{4,7},{5,6},{6,5},{7,4},{8,11},{9,10},{10,... | collective-permute-start | bytes 393224 | tf_op jit(solution)/shard_map/ppermute | solution.py:254
  24.1 24.8 %copy-start.3 = (s32[8]{0:T(128)S(1)}, s32[8]{0:T(128)}, u32[]{:S(2)}) copy-start(s32[8]{0:T(128)} %bucket_ref.3) | copy-start | bytes 100
  24.1 8.2 %collective-permute-start.18 = (bf16[2,128,512]{2,1,0:T(8,128)(2,1)S(1)}, bf16[2,128,512]{2,1,0:T(8,128)(2,1)S(1)}, u32[]{:S(2)}, u32[]{:S(2)}) collective-permute-start(bf16[2,128,512]{2,1,0:T(8,128)(2,1)S(1)} %attend.2.refs_0_), channel_id=1, source_target_pairs={{0,2},{1,3},{2,0},{3,1},{4,6},{5,7},{6,4},{7,5},{8,10},{9,11},{10,... | collective-permute-start | bytes 786440 | tf_op jit(solution)/shard_map/ppermute | solution.py:250
  27.2 6.2 %collective-permute-start.17 = (bf16[2,128,512]{2,1,0:T(8,128)(2,1)S(1)}, bf16[2,128,512]{2,1,0:T(8,128)(2,1)S(1)}, u32[]{:S(2)}, u32[]{:S(2)}) collective-permute-start(bf16[2,128,512]{2,1,0:T(8,128)(2,1)S(1)} %attend.3.refs_0_), channel_id=1, source_target_pairs={{0,1},{1,0},{2,3},{3,2},{4,5},{5,4},{6,7},{7,6},{8,9},{9,8},{10,11... | collective-permute-start | bytes 786440 | tf_op jit(solution)/shard_map/ppermute | solution.py:257
  27.6 10.5 %collective-permute-start.14 = (bf16[256,512]{1,0:T(8,128)(2,1)S(1)}, bf16[256,512]{1,0:T(8,128)(2,1)S(1)}, u32[]{:S(2)}, u32[]{:S(2)}) collective-permute-start(bf16[256,512]{1,0:T(8,128)(2,1)S(1)} %collective-permute-done.10.refs_6_), channel_id=1, source_target_pairs={{0,8},{4,12},{8,16},{12,20},{16,24},{20,28},{24,0},{28,4},{1,9},{5... | collective-permute-start | bytes 786440 | tf_op jit(solution)/shard_map/ppermute | solution.py:213
  29.3 10.4 %collective-permute-start.11 = (bf16[256,512]{1,0:T(8,128)(2,1)S(1)}, bf16[256,512]{1,0:T(8,128)(2,1)S(1)}, u32[]{:S(2)}, u32[]{:S(2)}) collective-permute-start(bf16[256,512]{1,0:T(8,128)(2,1)S(1)} %collective-permute-done.10.refs_6_), channel_id=1, source_target_pairs={{0,4},{4,0},{8,12},{12,8},{16,20},{20,16},{24,28},{28,24},{1,5},{5... | collective-permute-start | bytes 786440 | tf_op jit(solution)/shard_map/ppermute | solution.py:216
  30.8 8.9 %collective-permute-start.7 = (bf16[2,128,512]{2,1,0:T(8,128)(2,1)S(1)}, bf16[2,128,512]{2,1,0:T(8,128)(2,1)S(1)}, u32[]{:S(2)}, u32[]{:S(2)}) collective-permute-start(bf16[2,128,512]{2,1,0:T(8,128)(2,1)S(1)} %attend.3.refs_0_), channel_id=1, source_target_pairs={{0,2},{1,3},{2,0},{3,1},{4,6},{5,7},{6,4},{7,5},{8,10},{9,11},{10,... | collective-permute-start | bytes 786440 | tf_op jit(solution)/shard_map/ppermute | solution.py:250
  32.3 11.8 %collective-permute-start.13 = (bf16[256,512]{1,0:T(8,128)(2,1)S(1)}, bf16[256,512]{1,0:T(8,128)(2,1)S(1)}, u32[]{:S(2)}, u32[]{:S(2)}) collective-permute-start(bf16[256,512]{1,0:T(8,128)(2,1)S(1)} %collective-permute-done.12.refs_8_), channel_id=1, source_target_pairs={{0,4},{4,0},{8,12},{12,8},{16,20},{20,16},{24,28},{28,24},{1,5},{5... | collective-permute-start | bytes 786440 | tf_op jit(solution)/shard_map/ppermute | solution.py:216
  33.3 10.7 %collective-permute-start.19 = (bf16[2,128,512]{2,1,0:T(8,128)(2,1)S(1)}, bf16[2,128,512]{2,1,0:T(8,128)(2,1)S(1)}, u32[]{:S(2)}, u32[]{:S(2)}) collective-permute-start(bf16[2,128,512]{2,1,0:T(8,128)(2,1)S(1)} %collective-permute-done.18.refs_2_), channel_id=1, source_target_pairs={{0,1},{1,0},{2,3},{3,2},{4,5},{5,4},{6,7},{7,6},{8,9},{9,8},{10,11... | collective-permute-start | bytes 786440 | tf_op jit(solution)/shard_map/ppermute | solution.py:257
  38.2 10.7 %collective-permute-start.15 = (bf16[256,512]{1,0:T(8,128)(2,1)S(1)}, bf16[256,512]{1,0:T(8,128)(2,1)S(1)}, u32[]{:S(2)}, u32[]{:S(2)}) collective-permute-start(bf16[256,512]{1,0:T(8,128)(2,1)S(1)} %collective-permute-done.14.refs_10_), channel_id=1, source_target_pairs={{0,4},{4,0},{8,12},{12,8},{16,20},{20,16},{24,28},{28,24},{1,5},{5... | collective-permute-start | bytes 786440 | tf_op jit(solution)/shard_map/ppermute | solution.py:216
  39.7 12.1 %collective-permute-start.4 = (bf16[2,128,512]{2,1,0:T(8,128)(2,1)S(1)}, bf16[2,128,512]{2,1,0:T(8,128)(2,1)S(1)}, u32[]{:S(2)}, u32[]{:S(2)}) collective-permute-start(bf16[2,128,512]{2,1,0:T(8,128)(2,1)S(1)} %attend.2.refs_0_), channel_id=1, source_target_pairs={{0,1},{1,0},{2,3},{3,2},{4,5},{5,4},{6,7},{7,6},{8,9},{9,8},{10,11... | collective-permute-start | bytes 786440 | tf_op jit(solution)/shard_map/ppermute | solution.py:257
  39.7 12.1 %collective-permute-start.8 = (bf16[2,128,512]{2,1,0:T(8,128)(2,1)S(1)}, bf16[2,128,512]{2,1,0:T(8,128)(2,1)S(1)}, u32[]{:S(2)}, u32[]{:S(2)}) collective-permute-start(bf16[2,128,512]{2,1,0:T(8,128)(2,1)S(1)} %collective-permute-done.7.refs_2_), channel_id=1, source_target_pairs={{0,1},{1,0},{2,3},{3,2},{4,5},{5,4},{6,7},{7,6},{8,9},{9,8},{10,11... | collective-permute-start | bytes 786440 | tf_op jit(solution)/shard_map/ppermute | solution.py:257
  50.2 5.5 %collective-permute-start.20 = (bf16[128,512]{1,0:T(8,128)(2,1)S(1)}, bf16[128,512]{1,0:T(8,128)(2,1)S(1)}, u32[]{:S(2)}, u32[]{:S(2)}) collective-permute-start(bf16[128,512]{1,0:T(8,128)(2,1)S(1)} %get-tuple-element.26), channel_id=1, source_target_pairs={{0,2},{1,3},{2,0},{3,1},{4,6},{5,7},{6,4},{7,5},{8,10},{9,11},{10,... | collective-permute-start | bytes 393224 | tf_op jit(solution)/shard_map/ppermute | solution.py:250
  51.8 5.8 %collective-permute-start.21 = (bf16[128,512]{1,0:T(8,128)(2,1)S(1)}, bf16[128,512]{1,0:T(8,128)(2,1)S(1)}, u32[]{:S(2)}, u32[]{:S(2)}) collective-permute-start(bf16[128,512]{1,0:T(8,128)(2,1)S(1)} %get-tuple-element.27), channel_id=1, source_target_pairs={{0,3},{1,2},{2,1},{3,0},{4,7},{5,6},{6,5},{7,4},{8,11},{9,10},{10,... | collective-permute-start | bytes 393224 | tf_op jit(solution)/shard_map/ppermute | solution.py:254
  53.1 4.5 %collective-permute-start.16 = (bf16[128,512]{1,0:T(8,128)(2,1)S(1)}, bf16[128,512]{1,0:T(8,128)(2,1)S(1)}, u32[]{:S(2)}, u32[]{:S(2)}) collective-permute-start(bf16[128,512]{1,0:T(8,128)(2,1)S(1)} %get-tuple-element.25), channel_id=1, source_target_pairs={{0,1},{1,0},{2,3},{3,2},{4,5},{5,4},{6,7},{7,6},{8,9},{9,8},{10,11... | collective-permute-start | bytes 393224 | tf_op jit(solution)/shard_map/ppermute | solution.py:257

commit v3 on v2

--- a/solution.py
+++ b/solution.py
@@ -30,6 +30,7 @@
 
 
 ATTEND_US = 3
+HALF_STEPS = 2
 PROJECT_US = 2
 
 SMALL = pltpu.CompilerParams(vmem_limit_bytes=16 * 1024 * 1024)
@@ -51,61 +52,101 @@
     return jnp.where(moved >= size, moved - size, moved)
 
 
-def cut_kernel(n_arrays, *refs):
-    arrays, blocks, sems = refs[:n_arrays], refs[n_arrays:-1], refs[-1]
-    chips = len(blocks) // 2
+def after(value, *others):
+    return lax.optimization_barrier((value,) + others)[0]
+
+
+def half_kernel(master_ref, first_ref, second_ref, gradient_ref, half_ref):
+    new_master, _, _ = adam_update(
+        master_ref[...], first_ref[...], second_ref[...], gradient_ref[...]
+    )
+    half_ref[...] = new_master.astype(jnp.bfloat16)
+
+
+def half(master_weight, first_moment, second_moment, gradient):
+    depth, columns = master_weight.shape
+    rows = depth // HALF_STEPS
+    spec = pl.BlockSpec((rows, columns), lambda i: (i, 0))
+    return pl.pallas_call(
+        half_kernel,
+        grid=(HALF_STEPS,),
+        out_shape=jax.ShapeDtypeStruct((depth, columns), jnp.bfloat16),
+        in_specs=[spec] * 4,
+        out_specs=spec,
+        compiler_params=SMALL,
+        cost_estimate=estimate(1),
+        name="half",
+    )(*[
+        pltpu.with_memory_space_constraint(array, pltpu.HBM)
+        for array in (master_weight, first_moment, second_moment, gradient)
+    ])
+
+
+def cut_kernel(query, key, value, *refs):
+    blocks, sems = refs[:-1], refs[-1]
+    chips = (len(blocks) - 2) // 3 + 1
+    wide = blocks[0].shape[-1]
     chip, core = chip_and_core()
     copies = []
-    for i, block in enumerate(blocks):
-        group = 2 * turned(chip, i // 2, chips) + (core if i % 2 == 0 else 1 - core)
-        wide = block.shape[-1]
+
+    def copy(array, step, crossed, target):
+        group = 2 * turned(chip, step, chips) + (1 - core if crossed else core)
         lanes = pl.ds(pl.multiple_of(group * wide, wide), wide)
-        for j, array in enumerate(arrays):
-            target = block if n_arrays == 1 else block.at[j]
-            copies.append(pltpu.make_async_copy(array.at[:, lanes], target, sems.at[i, j]))
-    for copy in copies:
-        copy.start()
-    for copy in copies:
-        copy.wait()
+        copies.append(pltpu.make_async_copy(array.at[:, lanes], target, sems.at[len(copies)]))
+
+    for step in range(1, chips):
+        for crossed in range(2):
+            for i, array in enumerate((key, value)):
+                copy(array, step, crossed, blocks[3 * step - 1 + crossed].at[i])
+    for crossed in (1, 0):
+        for i, array in enumerate((query, key, value)):
+            copy(array, 0, crossed, blocks[crossed].at[i])
+    for step in range(1, chips):
+        for crossed in range(2):
+            copy(query, step, crossed, blocks[3 * step + 1].at[crossed])
+    for one in copies:
+        one.start()
+    for one in copies:
+        one.wait()
 
 
 def cut(*arrays):
     groups = lax.axis_size("seq")
     rows, width = arrays[0].shape
-    shape = (rows, width // groups)
-    if len(arrays) > 1:
-        shape = (len(arrays),) + shape
-    return pl.pallas_call(
-        functools.partial(cut_kernel, len(arrays)),
-        out_shape=[jax.ShapeDtypeStruct(shape, jnp.bfloat16)] * groups,
-        in_specs=[pl.BlockSpec(memory_space=pl.ANY)] * len(arrays),
-        out_specs=[pl.BlockSpec(memory_space=pl.ANY)] * groups,
-        scratch_shapes=[pltpu.SemaphoreType.DMA((groups, len(arrays)))],
+    counts = [3, 3] + [2] * (3 * (groups // 2 - 1))
+    return pl.pallas_call(
+        cut_kernel,
+        out_shape=[
+            jax.ShapeDtypeStruct((n, rows, width // groups), jnp.bfloat16) for n in counts
+        ],
+        in_specs=[pl.BlockSpec(memory_space=pl.ANY)] * 3,
+        out_specs=[IN_VMEM] * len(counts),
+        scratch_shapes=[pltpu.SemaphoreType.DMA((3 * groups,))],
         compiler_params=SMALL,
         cost_estimate=estimate(1),
         name="cut",
-    )(*arrays)
-
-
-def attend_kernel(n_keys, count_ref, *refs):
-    query_refs, pair_refs = refs[:2], refs[2 : 2 + n_keys]
-    out_ref, keys, values = refs[2 + n_keys :]
-    rows, wide = query_refs[0].shape
-    chips = n_keys // 2
+    )(*[pltpu.with_memory_space_constraint(array, pltpu.HBM) for array in arrays])
+
+
+def attend_kernel(n_pairs, picks, count_ref, *refs):
+    pair_refs = refs[:n_pairs]
+    out_ref, keys, values = refs[-3:]
+    _, rows, wide = out_ref.shape
+    chips = n_pairs // 2
     chip, core = chip_and_core()
     columns = []
     for i, ref in enumerate(pair_refs):
-        keys[i * rows : (i + 1) * rows, :] = ref[0]
-        values[i * rows : (i + 1) * rows, :] = ref[1]
+        keys[i * rows : (i + 1) * rows, :] = ref[ref.shape[0] - 2]
+        values[i * rows : (i + 1) * rows, :] = ref[ref.shape[0] - 1]
         source = 2 * turned(chip, (chips - i // 2) % chips, chips) + (core if i % 2 == 0 else 1 - core)
         columns.append(source * rows + lax.broadcasted_iota(jnp.int32, (1, rows), 1))
     valid = jnp.concatenate(columns, axis=1) < count_ref[0]
     factor = HEAD_DIM ** (-0.5) * math.log2(math.e)
-    for block, query_ref in enumerate(query_refs):
+    for block, (at, index) in enumerate(picks):
         for head in range(wide // HEAD_DIM):
             lanes = slice(head * HEAD_DIM, (head + 1) * HEAD_DIM)
             scores = lax.dot_general(
-                query_ref[:, lanes],
+                refs[at][index, :, lanes],
                 keys[:, lanes],
                 (((1,), (1,)), ((), ())),
                 preferred_element_type=jnp.float32,
@@ -114,25 +155,26 @@
             top = jnp.max(scores, axis=1, keepdims=True)
             expo = jnp.exp2((scores - top) * factor)
             total = jnp.sum(expo, axis=1, keepdims=True)
-            weights = (expo * (1.0 / total)).astype(jnp.bfloat16)
-            out_ref[block, :, lanes] = jnp.dot(
-                weights, values[:, lanes], preferred_element_type=jnp.float32
-            ).astype(jnp.bfloat16)
-
-
-def attend(counts, query_blocks, pairs):
-    rows, wide = query_blocks[0].shape
-    n_keys = len(pairs)
-    return pl.pallas_call(
-        functools.partial(attend_kernel, n_keys),
+            mixed = jnp.dot(
+                expo.astype(jnp.bfloat16), values[:, lanes], preferred_element_type=jnp.float32
+            )
+            out_ref[block, :, lanes] = (mixed * (1.0 / total)).astype(jnp.bfloat16)
+
+
+def attend(counts, pairs, queries=()):
+    _, rows, wide = pairs[0].shape
+    n_pairs = len(pairs)
+    picks = ((n_pairs, 0), (n_pairs + 1, 1)) if queries else ((0, 0), (1, 0))
+    return pl.pallas_call(
+        functools.partial(attend_kernel, n_pairs, picks),
         out_shape=jax.ShapeDtypeStruct((2, rows, wide), jnp.bfloat16),
-        in_specs=[IN_SMEM] + [IN_VMEM] * (2 + n_keys),
+        in_specs=[IN_SMEM] + [IN_VMEM] * (n_pairs + len(queries)),
         out_specs=IN_VMEM,
-        scratch_shapes=[pltpu.VMEM((n_keys * rows, wide), jnp.bfloat16)] * 2,
+        scratch_shapes=[pltpu.VMEM((n_pairs * rows, wide), jnp.bfloat16)] * 2,
         compiler_params=SMALL,
         cost_estimate=estimate(ATTEND_US),
         name="attend",
-    )(counts, *query_blocks, *pairs)
+    )(counts, *pairs, *queries)
 
 
 def project_kernel(n_att, steps, bucket_ref, *refs):
@@ -204,31 +246,35 @@
     )(*blocks)
 
 
-def gather_weights(shard):
+def gather_weights(shard, first):
     owners = lax.axis_size("dp")
     ring = owners // 2
 
-    def moved(block, step):
+    def moved(block, step, name):
         perm = [(o, (o // 2 + step) % ring * 2 + o % 2) for o in range(owners)]
-        return lax.ppermute(block, "dp", perm)
-
-    def swapped(block):
-        return lax.ppermute(block, "dp", [(o, o ^ 1) for o in range(owners)])
-
-    steps, held = [0], [shard]
+        with jax.named_scope(name):
+            return lax.ppermute(block, "dp", perm)
+
+    def swapped(block, name):
+        with jax.named_scope(name):
+            return lax.ppermute(block, "dp", [(o, o ^ 1) for o in range(owners)])
+
+    steps, held, names = [0], [shard], ["swap_own"]
     ahead, back = shard, shard
     for step in range(1, ring // 2 + 1):
-        ahead = moved(ahead, 1)
+        ahead = moved(ahead, 1, f"ahead{step}")
         held.append(ahead)
+        names.append(f"swap_ahead{step}")
         steps.append((-step) % ring)
         if step <= (ring - 1) // 2:
-            back = moved(back, -1)
+            back = moved(back, -1, f"back{step}")
             held.append(back)
+            names.append(f"swap_back{step}")
             steps.append(step)
-    blocks = []
-    for block in held:
-        blocks += [block, swapped(block)]
-    return steps, blocks
+    blocks = [shard, swapped(after(shard, first), names[0])]
+    for block, name in zip(held[1:], names[1:]):
+        blocks += [block, swapped(block, name)]
+    return steps, blocks, held[1:]
 
 
 def body(
@@ -245,46 +291,66 @@
     groups = lax.axis_size("seq")
     chips = groups // 2
 
-    def to_same(array, step):
+    def to_same(array, step, name):
         perm = [(s, (s // 2 + step) % chips * 2 + s % 2) for s in range(groups)]
-        return lax.ppermute(array, "seq", perm)
-
-    def to_cross(array, step):
+        with jax.named_scope(name):
+            return lax.ppermute(array, "seq", perm)
+
+    def to_cross(array, step, name):
         perm = [(s, (s // 2 + step) % chips * 2 + 1 - s % 2) for s in range(groups)]
-        return lax.ppermute(array, "seq", perm)
-
-    def to_sibling(array):
-        return lax.ppermute(array, "seq", [(s, s ^ 1) for s in range(groups)])
-
-    def exchanged(blocks):
-        got = [blocks[0], to_sibling(blocks[1])]
-        for step in range(1, chips):
-            got += [to_same(blocks[2 * step], step), to_cross(blocks[2 * step + 1], step)]
-        return got
-
-    pairs = exchanged(cut(hit_keys[0], hit_values[0]))
-    new_master, new_first, new_second = adam_update(
-        master_weight, first_moment, second_moment, gradient
-    )
-    steps, weights = gather_weights(new_master[0].astype(jnp.bfloat16))
-    asked = exchanged(cut(queries[0]))
-
-    attended = [attend(hit_counts, asked[2 * e : 2 * e + 2], pairs) for e in range(chips)]
-    spread = [attended] + [[to_same(a, step) for a in attended] for step in range(1, chips)]
-    beside = [[to_sibling(a) for a in row] for row in spread]
+        with jax.named_scope(name):
+            return lax.ppermute(array, "seq", perm)
+
+    def to_sibling(array, name):
+        with jax.named_scope(name):
+            return lax.ppermute(array, "seq", [(s, s ^ 1) for s in range(groups)])
+
+    master, first = master_weight[0], first_moment[0]
+    second, grad = second_moment[0], gradient[0]
+
+    own, other, *rest = cut(queries[0], hit_keys[0], hit_values[0])
+    rounded = half(master, first, second, grad)
+    sibling = to_sibling(other, "sibling")
+    steps, weights, ring = gather_weights(rounded, sibling)
+    pairs, asked = [own, sibling], [()]
+    for step in range(1, chips):
+        same, cross, queries_for = rest[3 * step - 3 : 3 * step]
+        pairs += [
+            to_same(same, step, "pairs_same"),
+            to_cross(after(cross, sibling), step, "pairs_cross"),
+        ]
+        here = to_same(after(queries_for, pairs[-2], rounded), step, "queries")
+        asked.append((here, to_sibling(here, "queries_sibling")))
+
+    attended = [attend(hit_counts, [after(own, ring[0], ring[1], weights[1])] + pairs[1:])]
+    for here, beside in asked[1:]:
+        attended.append(attend(hit_counts, pairs, (after(here, attended[-1], ring[2], weights[3]), beside)))
+    pass
+    spread = [attended] + [
+        [to_same(a, step, f"attended{e}_same") for e, a in enumerate(attended)]
+        for step in range(1, chips)
+    ]
+    beside = [
+        [to_sibling(after(a, spread[1][0], weights[5]), f"spread{d}_{e}_sibling") for e, a in enumerate(row)]
+        for d, row in enumerate(spread)
+    ]
 
     columns = [None] * groups
     for e in list(range(1, chips)) + [0]:
         att = []
         for d in range(chips):
             att += [spread[d][(e - d) % chips], beside[d][(e - d) % chips]]
+        if e == 0:
+            att[0] = after(att[0], out)
         out, other = project(owner_bucket, att, steps, weights)
         if e == 0:
-            columns[0], columns[1] = out, to_sibling(other)
+            columns[0], columns[1] = out, to_sibling(other, "out_sibling")
         else:
-            columns[2 * e] = to_same(out, chips - e)
-            columns[2 * e + 1] = to_cross(other, chips - e)
+            columns[2 * e] = to_same(out, chips - e, "out_same")
+            columns[2 * e + 1] = to_cross(other, chips - e, "out_cross")
     projected = place(columns)[None]
+    new_master, new_first, new_second = adam_update(*lax.optimization_barrier(
+        (master_weight, first_moment, second_moment, gradient, columns[0]))[:4])
     return (projected, new_master, new_first, new_second)
 
 

time: 58.6 us -> 52.6 us (0.90)
  starting transfers between devices: 23.4 us -> 17.7 us
  local copies, waits for them, and re-layouts: 2.1 us -> 0.02 us
  Pallas kernels: 9.54 us -> 11.3 us
  other arithmetic: 2.64 us -> 1.43 us
  waiting for transfers between devices: 19.4 us -> 20.6 us
    ppermute x4, waiting for transfers between devices: 8.67 us -> 4.08 us  [swapped(): return lax.ppermute(block, 'dp', [(o, o ^ 1) for o in range(owners)])]
    ppermute x3, waiting for transfers between devices: 4.84 us -> 8.7 us  [moved(): return lax.ppermute(block, 'dp', perm)]
    ppermute x5, waiting for transfers between devices: 1.93 us -> 5.73 us  [to_same(): return lax.ppermute(array, 'seq', perm)]
    convert_element_type x1 -> x0, other arithmetic: 2.64 us -> none  [body(): steps, weights = gather_weights(new_master[0].astype(jnp.bfloat16))]
    unnamed x12 -> x10, local copies, waits for them, and re-layouts: 2.1 us -> 0.02 us
    ppermute x3 -> x2, waiting for transfers between devices: 3.9 us -> 2.03 us  [to_cross(): return lax.ppermute(array, 'seq', perm)]
    ppermute x3, starting transfers between devices: 5.68 us -> 3.88 us  [moved(): return lax.ppermute(block, 'dp', perm)]
    pallas_call x4, Pallas kernels: 6.12 us -> 7.82 us  [the longest x2 4.52 us: attend(): pl.pallas_call(functools.partial(attend_kernel, n_pairs, picks), out_shap...]
  transfers between devices with their start and end apart: 22 -> 21, of which waited for: 7 -> 9; matrix products, arithmetic and copies ran while one was open for 5% -> 3% of each run, Pallas kernels for 14% -> 17%
where the time goes in v3:
time: 52.6 us; the launch traced here: 52.4 us
  waiting for transfers between devices  20.6 us (39%)
  starting transfers between devices  17.7 us (34%)
  Pallas kernels  11.3 us (21%)
  other arithmetic  1.43 us (3%)
  between operations  1.39 us (3%)
    ppermute x3, waiting for transfers between devices, moved(): return lax.ppermute(block, 'dp', perm)  8.7 us
    ppermute x5, starting transfers between devices, to_same(): return lax.ppermute(array, 'seq', perm)  6.77 us
    ppermute x5, waiting for transfers between devices, to_same(): return lax.ppermute(array, 'seq', perm)  5.73 us
    ppermute x4, starting transfers between devices, swapped(): return lax.ppermute(block, 'dp', [(o, o ^ 1) for o in range(owners)])  5.08 us
    pallas_call x2, Pallas kernels, attend(): pl.pallas_call(functools.partial(attend_kernel, n_pairs, picks), out_shap...  4.52 us
    ppermute x4, waiting for transfers between devices, swapped(): return lax.ppermute(block, 'dp', [(o, o ^ 1) for o in range(owners)])  4.08 us
    ppermute x3, starting transfers between devices, moved(): return lax.ppermute(block, 'dp', perm)  3.88 us
    pallas_call x2, Pallas kernels, project(): pl.pallas_call(functools.partial(project_kernel, len(att), steps), out_sh...  2.59 us
  transfers between devices with their start and end apart: 21, of which 9 were waited for; matrix products, arithmetic and copies ran while one was open for 3% of the time, Pallas kernels for 17%

profile of v3, /device:TPU:0, one launch (start us, length us, event | category | flops | bytes accessed | tf_op | source)
XLA Modules:
  0.0 52.4 jit_solution(8599613899471078861)
XLA Ops:
  0.6 1.6 %cut.1 = (bf16[3,128,512]{2,1,0:T(8,128)(2,1)S(1)}, bf16[3,128,512]{2,1,0:T(8,128)(2,1)S(1)}, bf16[2,128,512]{2,1,0:T(8,128)(2,1)S(1)}, bf16[2,128,512]{2,1,0:T(8,128)(2,1)S(1)}, bf16[2,128,512]{2,1,0:T(8,128)(2,1)S(1)}) custom-call(bf16[128,2048]{1,0:T(8,128)(2,1)} %bitcast.12, bf16[128,2048]{1,0:T(8,128)(2,1)} %bitcast.13, bf16[128,2048]{1,0:T(8,128)(2,1)} %bitcast.14), custom_call_target="tpu_custom_call" | custom-call | bytes 3690000 | tf_op jit(solution)/shard_map/cut/pallas_call | solution.py:117
  2.2 3.0 %collective-permute-start.4 = (bf16[2,128,512]{2,1,0:T(8,128)(2,1)S(1)}, bf16[2,128,512]{2,1,0:T(8,128)(2,1)S(1)}, u32[]{:S(2)}, u32[]{:S(2)}) collective-permute-start(bf16[2,128,512]{2,1,0:T(8,128)(2,1)S(1)} %get-tuple-element.31), channel_id=1, source_target_pairs={{0,2},{1,3},{2,0},{3,1},{4,6},{5,7},{6,4},{7,5},{8,10},{9,11},{10,... | collective-permute-start | bytes 786440 | tf_op jit(solution)/shard_map/pairs_same/ppermute | solution.py:297
  5.2 1.7 %half.1.refs_4_ = bf16[256,512]{1,0:T(8,128)(2,1)S(1)} custom-call(f32[256,512]{1,0:T(8,128)} %bitcast.8, f32[256,512]{1,0:T(8,128)} %bitcast.9, f32[256,512]{1,0:T(8,128)} %bitcast.10, f32[256,512]{1,0:T(8,128)} %bitcast.11), custom_call_target="tpu_custom_call" | custom-call | bytes 3690000 | tf_op jit(solution)/shard_map/half/pallas_call | solution.py:70
  7.0 1.6 %collective-permute-start = (bf16[256,512]{1,0:T(8,128)(2,1)S(1)}, bf16[256,512]{1,0:T(8,128)(2,1)S(1)}, u32[]{:S(2)}, u32[]{:S(2)}) collective-permute-start(bf16[256,512]{1,0:T(8,128)(2,1)S(1)} %half.1.refs_4_), channel_id=1, source_target_pairs={{0,8},{4,12},{8,16},{12,20},{16,24},{20,28},{24,0},{28,4},{1,9},{5... | collective-permute-start | bytes 786440 | tf_op jit(solution)/shard_map/ahead1/ppermute | solution.py:256
  8.6 2.2 %collective-permute-start.1 = (bf16[256,512]{1,0:T(8,128)(2,1)S(1)}, bf16[256,512]{1,0:T(8,128)(2,1)S(1)}, u32[]{:S(2)}, u32[]{:S(2)}) collective-permute-start(bf16[256,512]{1,0:T(8,128)(2,1)S(1)} %half.1.refs_4_), channel_id=1, source_target_pairs={{0,24},{4,28},{8,0},{12,4},{16,8},{20,12},{24,16},{28,20},{1,25},{... | collective-permute-start | bytes 786440 | tf_op jit(solution)/shard_map/back1/ppermute | solution.py:256
  10.9 0.7 %collective-permute-done.4.refs_2_ = bf16[2,128,512]{2,1,0:T(8,128)(2,1)S(1)} collective-permute-done((bf16[2,128,512]{2,1,0:T(8,128)(2,1)S(1)}, bf16[2,128,512]{2,1,0:T(8,128)(2,1)S(1)}, u32[]{:S(2)}, u32[]{:S(2)}) %collective-permute-start.4) | collective-permute-done | bytes 262176 | tf_op jit(solution)/shard_map/pairs_same/ppermute | solution.py:297
  11.5 1.7 %collective-permute-start.6 = (bf16[2,128,512]{2,1,0:T(8,128)(2,1)S(1)}, bf16[2,128,512]{2,1,0:T(8,128)(2,1)S(1)}, u32[]{:S(2)}, u32[]{:S(2)}) collective-permute-start(bf16[2,128,512]{2,1,0:T(8,128)(2,1)S(1)} %get-tuple-element.35), channel_id=1, source_target_pairs={{0,2},{1,3},{2,0},{3,1},{4,6},{5,7},{6,4},{7,5},{8,10},{9,11},{10,... | collective-permute-start | bytes 786440 | tf_op jit(solution)/shard_map/queries/ppermute | solution.py:297
  13.3 1.5 %collective-permute-start.3 = (bf16[256,512]{1,0:T(8,128)(2,1)S(1)}, bf16[256,512]{1,0:T(8,128)(2,1)S(1)}, u32[]{:S(2)}, u32[]{:S(2)}) collective-permute-start(bf16[256,512]{1,0:T(8,128)(2,1)S(1)} %half.1.refs_4_), channel_id=1, source_target_pairs={{0,4},{4,0},{8,12},{12,8},{16,20},{20,16},{24,28},{28,24},{1,5},{5... | collective-permute-start | bytes 786440 | tf_op jit(solution)/shard_map/swap_own/ppermute | solution.py:260
  14.8 3.2 %collective-permute-done.refs_6_ = bf16[256,512]{1,0:T(8,128)(2,1)S(1)} collective-permute-done((bf16[256,512]{1,0:T(8,128)(2,1)S(1)}, bf16[256,512]{1,0:T(8,128)(2,1)S(1)}, u32[]{:S(2)}, u32[]{:S(2)}) %collective-permute-start) | collective-permute-done | bytes 262176 | tf_op jit(solution)/shard_map/ahead1/ppermute | solution.py:256
  18.0 4.7 %collective-permute-done.1.refs_8_ = bf16[256,512]{1,0:T(8,128)(2,1)S(1)} collective-permute-done((bf16[256,512]{1,0:T(8,128)(2,1)S(1)}, bf16[256,512]{1,0:T(8,128)(2,1)S(1)}, u32[]{:S(2)}, u32[]{:S(2)}) %collective-permute-start.1) | collective-permute-done | bytes 262176 | tf_op jit(solution)/shard_map/back1/ppermute | solution.py:256
  22.7 1.5 %collective-permute-start.8 = (bf16[256,512]{1,0:T(8,128)(2,1)S(1)}, bf16[256,512]{1,0:T(8,128)(2,1)S(1)}, u32[]{:S(2)}, u32[]{:S(2)}) collective-permute-start(bf16[256,512]{1,0:T(8,128)(2,1)S(1)} %collective-permute-done.refs_6_), channel_id=1, source_target_pairs={{0,4},{4,0},{8,12},{12,8},{16,20},{20,16},{24,28},{28,24},{1,5},{5... | collective-permute-start | bytes 786440 | tf_op jit(solution)/shard_map/swap_ahead1/ppermute | solution.py:260
  24.8 0.6 %collective-permute-start.11 = (bf16[256,512]{1,0:T(8,128)(2,1)S(1)}, bf16[256,512]{1,0:T(8,128)(2,1)S(1)}, u32[]{:S(2)}, u32[]{:S(2)}) collective-permute-start(bf16[256,512]{1,0:T(8,128)(2,1)S(1)} %collective-permute-done.1.refs_8_), channel_id=1, source_target_pairs={{0,4},{4,0},{8,12},{12,8},{16,20},{20,16},{24,28},{28,24},{1,5},{5... | collective-permute-start | bytes 786440 | tf_op jit(solution)/shard_map/swap_back1/ppermute | solution.py:260
  25.4 2.3 %attend.2.refs_0_ = bf16[2,128,512]{2,1,0:T(8,128)(2,1)S(1)} custom-call(s32[1]{0:T(128)S(6)} %copy.13.count_ref, bf16[3,128,512]{2,1,0:T(8,128)(2,1)S(1)} %get-tuple-element.30.refs_0_, bf16[3,128,512]{2,1,0:T(8,128)(2,1)S(1)} %collective-permute-done.2.refs_1_, bf16[2,128,512]{2,1,0:T(8,128)(2,1)S(1)} %collective-permute-done.4.refs_2_, ...), custom_call_target="tpu_custom_call" | custom-call | bytes 11070000 | tf_op jit(solution)/shard_map/attend/pallas_call | solution.py:168
  27.7 0.0 copy-start
  27.7 0.6 %collective-permute-start.10 = (bf16[2,128,512]{2,1,0:T(8,128)(2,1)S(1)}, bf16[2,128,512]{2,1,0:T(8,128)(2,1)S(1)}, u32[]{:S(2)}, u32[]{:S(2)}) collective-permute-start(bf16[2,128,512]{2,1,0:T(8,128)(2,1)S(1)} %attend.2.refs_0_), channel_id=1, source_target_pairs={{0,2},{1,3},{2,0},{3,1},{4,6},{5,7},{6,4},{7,5},{8,10},{9,11},{10,... | collective-permute-start | bytes 786440 | tf_op jit(solution)/shard_map/attended0_same/ppermute | solution.py:297
  28.3 0.8 %collective-permute-done.7.refs_10_ = bf16[256,512]{1,0:T(8,128)(2,1)S(1)} collective-permute-done((bf16[256,512]{1,0:T(8,128)(2,1)S(1)}, bf16[256,512]{1,0:T(8,128)(2,1)S(1)}, u32[]{:S(2)}, u32[]{:S(2)}) %collective-permute-start.7) | collective-permute-done | bytes 262176 | tf_op jit(solution)/shard_map/ahead2/ppermute | solution.py:256
  29.1 2.8 %collective-permute-done.8.refs_7_ = bf16[256,512]{1,0:T(8,128)(2,1)S(1)} collective-permute-done((bf16[256,512]{1,0:T(8,128)(2,1)S(1)}, bf16[256,512]{1,0:T(8,128)(2,1)S(1)}, u32[]{:S(2)}, u32[]{:S(2)}) %collective-permute-start.8) | collective-permute-done | bytes 262176 | tf_op jit(solution)/shard_map/swap_ahead1/ppermute | solution.py:260
  31.9 2.3 %attend.3.refs_0_ = bf16[2,128,512]{2,1,0:T(8,128)(2,1)S(1)} custom-call(s32[1]{0:T(128)S(6)} %copy.13.count_ref, bf16[3,128,512]{2,1,0:T(8,128)(2,1)S(1)} %get-tuple-element.30.refs_0_, bf16[3,128,512]{2,1,0:T(8,128)(2,1)S(1)} %collective-permute-done.2.refs_1_, bf16[2,128,512]{2,1,0:T(8,128)(2,1)S(1)} %collective-permute-done.4.refs_2_, ...), custom_call_target="tpu_custom_call" | custom-call | bytes 11070000 | tf_op jit(solution)/shard_map/attend/pallas_call | solution.py:168
  34.2 0.6 %collective-permute-start.16 = (bf16[2,128,512]{2,1,0:T(8,128)(2,1)S(1)}, bf16[2,128,512]{2,1,0:T(8,128)(2,1)S(1)}, u32[]{:S(2)}, u32[]{:S(2)}) collective-permute-start(bf16[2,128,512]{2,1,0:T(8,128)(2,1)S(1)} %attend.3.refs_0_), channel_id=1, source_target_pairs={{0,2},{1,3},{2,0},{3,1},{4,6},{5,7},{6,4},{7,5},{8,10},{9,11},{10,... | collective-permute-start | bytes 786440 | tf_op jit(solution)/shard_map/attended1_same/ppermute | solution.py:297
  34.8 1.5 %collective-permute-start.14 = (bf16[256,512]{1,0:T(8,128)(2,1)S(1)}, bf16[256,512]{1,0:T(8,128)(2,1)S(1)}, u32[]{:S(2)}, u32[]{:S(2)}) collective-permute-start(bf16[256,512]{1,0:T(8,128)(2,1)S(1)} %collective-permute-done.7.refs_10_), channel_id=1, source_target_pairs={{0,4},{4,0},{8,12},{12,8},{16,20},{20,16},{24,28},{28,24},{1,5},{5... | collective-permute-start | bytes 786440 | tf_op jit(solution)/shard_map/swap_ahead2/ppermute | solution.py:260
  36.2 1.3 %collective-permute-done.11.refs_9_ = bf16[256,512]{1,0:T(8,128)(2,1)S(1)} collective-permute-done((bf16[256,512]{1,0:T(8,128)(2,1)S(1)}, bf16[256,512]{1,0:T(8,128)(2,1)S(1)}, u32[]{:S(2)}, u32[]{:S(2)}) %collective-permute-start.11) | collective-permute-done | bytes 262176 | tf_op jit(solution)/shard_map/swap_back1/ppermute | solution.py:260
  37.5 0.5 collective-permute-start.13
  38.0 3.8 %collective-permute-done.16.refs_2_ = bf16[2,128,512]{2,1,0:T(8,128)(2,1)S(1)} collective-permute-done((bf16[2,128,512]{2,1,0:T(8,128)(2,1)S(1)}, bf16[2,128,512]{2,1,0:T(8,128)(2,1)S(1)}, u32[]{:S(2)}, u32[]{:S(2)}) %collective-permute-start.16) | collective-permute-done | bytes 262176 | tf_op jit(solution)/shard_map/attended1_same/ppermute | solution.py:297
  41.9 1.3 %project.2 = (bf16[128,512]{1,0:T(8,128)(2,1)S(1)}, bf16[128,512]{1,0:T(8,128)(2,1)S(1)}) custom-call(s32[8]{0:T(128)S(1)} %copy-done, bf16[2,128,512]{2,1,0:T(8,128)(2,1)S(1)} %attend.3.refs_0_, bf16[2,128,512]{2,1,0:T(8,128)(2,1)S(1)} %collective-permute-done.12.refs_1_, bf16[2,128,512]{2,1,0:T(8,128)(2,1)S(1)} %collective-permute-done.10.refs_2_, ...), custom_call_target="tpu_custom_call" | custom-call | bytes 7380000 | tf_op jit(solution)/shard_map/project/pallas_call | solution.py:215
  43.2 0.8 %collective-permute-start.19 = (bf16[128,512]{1,0:T(8,128)(2,1)S(1)}, bf16[128,512]{1,0:T(8,128)(2,1)S(1)}, u32[]{:S(2)}, u32[]{:S(2)}) collective-permute-start(bf16[128,512]{1,0:T(8,128)(2,1)S(1)} %get-tuple-element.39), channel_id=1, source_target_pairs={{0,2},{1,3},{2,0},{3,1},{4,6},{5,7},{6,4},{7,5},{8,10},{9,11},{10,... | collective-permute-start | bytes 393224 | tf_op jit(solution)/shard_map/out_same/ppermute | solution.py:297
  44.0 1.1 %collective-permute-start.20 = (bf16[128,512]{1,0:T(8,128)(2,1)S(1)}, bf16[128,512]{1,0:T(8,128)(2,1)S(1)}, u32[]{:S(2)}, u32[]{:S(2)}) collective-permute-start(bf16[128,512]{1,0:T(8,128)(2,1)S(1)} %get-tuple-element.45), channel_id=1, source_target_pairs={{0,3},{1,2},{2,1},{3,0},{4,7},{5,6},{6,5},{7,4},{8,11},{9,10},{10,... | collective-permute-start | bytes 393224 | tf_op jit(solution)/shard_map/out_cross/ppermute | solution.py:302
  45.2 1.3 %project.3 = (bf16[128,512]{1,0:T(8,128)(2,1)S(1)}, bf16[128,512]{1,0:T(8,128)(2,1)S(1)}) custom-call(s32[8]{0:T(128)S(1)} %copy-done, bf16[2,128,512]{2,1,0:T(8,128)(2,1)S(1)} %attend.2.refs_0_, bf16[2,128,512]{2,1,0:T(8,128)(2,1)S(1)} %collective-permute-done.15.refs_1_, bf16[2,128,512]{2,1,0:T(8,128)(2,1)S(1)} %collective-permute-done.16.refs_2_, ...), custom_call_target="tpu_custom_call" | custom-call | bytes 7380000 | tf_op jit(solution)/shard_map/project/pallas_call | solution.py:215
  46.5 0.4 collective-permute-start.18
  46.8 1.4 %multiply_subtract_fusion = (f32[1,256,512]{2,1,0:T(8,128)}, f32[1,256,512]{2,1,0:T(8,128)}, f32[1,256,512]{2,1,0:T(8,128)}) fusion(f32[1,256,512]{2,1,0:T(8,128)S(1)} %copy-done.1, f32[1,256,512]{2,1,0:T(8,128)S(1)} %copy-done.4, f32[1,256,512]{2,1,0:T(8,128)S(1)} %copy-done.2, f32[1,256,512]{2,1,0:T(8,128)S(1)} %copy-done.3), kind=kLoop, calls=%fused_computation.2 | loop fusion | flops 1966080 | bytes 3670016 | tf_op jit(solution)/shard_map/sub | solution.py:26
  48.3 1.3 %collective-permute-done.19.refs_2_ = bf16[128,512]{1,0:T(8,128)(2,1)S(1)} collective-permute-done((bf16[128,512]{1,0:T(8,128)(2,1)S(1)}, bf16[128,512]{1,0:T(8,128)(2,1)S(1)}, u32[]{:S(2)}, u32[]{:S(2)}) %collective-permute-start.19) | collective-permute-done | bytes 131104 | tf_op jit(solution)/shard_map/out_same/ppermute | solution.py:297
  49.5 2.0 %collective-permute-done.20.refs_3_ = bf16[128,512]{1,0:T(8,128)(2,1)S(1)} collective-permute-done((bf16[128,512]{1,0:T(8,128)(2,1)S(1)}, bf16[128,512]{1,0:T(8,128)(2,1)S(1)}, u32[]{:S(2)}, u32[]{:S(2)}) %collective-permute-start.20) | collective-permute-done | bytes 131104 | tf_op jit(solution)/shard_map/out_cross/ppermute | solution.py:302
  51.6 0.8 %place.1 = bf16[128,2048]{1,0:T(8,128)(2,1)} custom-call(bf16[128,512]{1,0:T(8,128)(2,1)S(1)} %get-tuple-element.43.refs_0_, bf16[128,512]{1,0:T(8,128)(2,1)S(1)} %collective-permute-done.18.refs_1_, bf16[128,512]{1,0:T(8,128)(2,1)S(1)} %collective-permute-done.19.refs_2_, bf16[128,512]{1,0:T(8,128)(2,1)S(1)} %collective-permute-done.20.refs_3_), custom_call_target="tpu_custom_call" | custom-call | bytes 3690000 | tf_op jit(solution)/shard_map/place/pallas_call | solution.py:238
  (28 shorter events, 0.1 us)
Async XLA Ops:
  2.2 9.3 %collective-permute-start.4 = (bf16[2,128,512]{2,1,0:T(8,128)(2,1)S(1)}, bf16[2,128,512]{2,1,0:T(8,128)(2,1)S(1)}, u32[]{:S(2)}, u32[]{:S(2)}) collective-permute-start(bf16[2,128,512]{2,1,0:T(8,128)(2,1)S(1)} %get-tuple-element.31), channel_id=1, source_target_pairs={{0,2},{1,3},{2,0},{3,1},{4,6},{5,7},{6,4},{7,5},{8,10},{9,11},{10,... | collective-permute-start | bytes 786440 | tf_op jit(solution)/shard_map/pairs_same/ppermute | solution.py:297
  5.2 8.0 %collective-permute-start.2 = (bf16[3,128,512]{2,1,0:T(8,128)(2,1)S(1)}, bf16[3,128,512]{2,1,0:T(8,128)(2,1)S(1)}, u32[]{:S(2)}, u32[]{:S(2)}) collective-permute-start(bf16[3,128,512]{2,1,0:T(8,128)(2,1)S(1)} %get-tuple-element.28), channel_id=1, source_target_pairs={{0,1},{1,0},{2,3},{3,2},{4,5},{5,4},{6,7},{7,6},{8,9},{9,8},{10,11... | collective-permute-start | bytes 1179656 | tf_op jit(solution)/shard_map/sibling/ppermute | solution.py:306
  7.0 11.0 %collective-permute-start = (bf16[256,512]{1,0:T(8,128)(2,1)S(1)}, bf16[256,512]{1,0:T(8,128)(2,1)S(1)}, u32[]{:S(2)}, u32[]{:S(2)}) collective-permute-start(bf16[256,512]{1,0:T(8,128)(2,1)S(1)} %half.1.refs_4_), channel_id=1, source_target_pairs={{0,8},{4,12},{8,16},{12,20},{16,24},{20,28},{24,0},{28,4},{1,9},{5... | collective-permute-start | bytes 786440 | tf_op jit(solution)/shard_map/ahead1/ppermute | solution.py:256
  8.6 14.1 %collective-permute-start.1 = (bf16[256,512]{1,0:T(8,128)(2,1)S(1)}, bf16[256,512]{1,0:T(8,128)(2,1)S(1)}, u32[]{:S(2)}, u32[]{:S(2)}) collective-permute-start(bf16[256,512]{1,0:T(8,128)(2,1)S(1)} %half.1.refs_4_), channel_id=1, source_target_pairs={{0,24},{4,28},{8,0},{12,4},{16,8},{20,12},{24,16},{28,20},{1,25},{... | collective-permute-start | bytes 786440 | tf_op jit(solution)/shard_map/back1/ppermute | solution.py:256
  11.5 12.6 %collective-permute-start.6 = (bf16[2,128,512]{2,1,0:T(8,128)(2,1)S(1)}, bf16[2,128,512]{2,1,0:T(8,128)(2,1)S(1)}, u32[]{:S(2)}, u32[]{:S(2)}) collective-permute-start(bf16[2,128,512]{2,1,0:T(8,128)(2,1)S(1)} %get-tuple-element.35), channel_id=1, source_target_pairs={{0,2},{1,3},{2,0},{3,1},{4,6},{5,7},{6,4},{7,5},{8,10},{9,11},{10,... | collective-permute-start | bytes 786440 | tf_op jit(solution)/shard_map/queries/ppermute | solution.py:297
  13.3 11.5 %collective-permute-start.3 = (bf16[256,512]{1,0:T(8,128)(2,1)S(1)}, bf16[256,512]{1,0:T(8,128)(2,1)S(1)}, u32[]{:S(2)}, u32[]{:S(2)}) collective-permute-start(bf16[256,512]{1,0:T(8,128)(2,1)S(1)} %half.1.refs_4_), channel_id=1, source_target_pairs={{0,4},{4,0},{8,12},{12,8},{16,20},{20,16},{24,28},{28,24},{1,5},{5... | collective-permute-start | bytes 786440 | tf_op jit(solution)/shard_map/swap_own/ppermute | solution.py:260
  14.8 10.7 %collective-permute-start.5 = (bf16[2,128,512]{2,1,0:T(8,128)(2,1)S(1)}, bf16[2,128,512]{2,1,0:T(8,128)(2,1)S(1)}, u32[]{:S(2)}, u32[]{:S(2)}) collective-permute-start(bf16[2,128,512]{2,1,0:T(8,128)(2,1)S(1)} %get-tuple-element.33), channel_id=1, source_target_pairs={{0,3},{1,2},{2,1},{3,0},{4,7},{5,6},{6,5},{7,4},{8,11},{9,10},{10,... | collective-permute-start | bytes 786440 | tf_op jit(solution)/shard_map/pairs_cross/ppermute | solution.py:302
  18.0 11.1 %collective-permute-start.7 = (bf16[256,512]{1,0:T(8,128)(2,1)S(1)}, bf16[256,512]{1,0:T(8,128)(2,1)S(1)}, u32[]{:S(2)}, u32[]{:S(2)}) collective-permute-start(bf16[256,512]{1,0:T(8,128)(2,1)S(1)} %collective-permute-done.refs_6_), channel_id=1, source_target_pairs={{0,8},{4,12},{8,16},{12,20},{16,24},{20,28},{24,0},{28,4},{1,9},{5... | collective-permute-start | bytes 786440 | tf_op jit(solution)/shard_map/ahead2/ppermute | solution.py:256
  22.7 9.2 %collective-permute-start.8 = (bf16[256,512]{1,0:T(8,128)(2,1)S(1)}, bf16[256,512]{1,0:T(8,128)(2,1)S(1)}, u32[]{:S(2)}, u32[]{:S(2)}) collective-permute-start(bf16[256,512]{1,0:T(8,128)(2,1)S(1)} %collective-permute-done.refs_6_), channel_id=1, source_target_pairs={{0,4},{4,0},{8,12},{12,8},{16,20},{20,16},{24,28},{28,24},{1,5},{5... | collective-permute-start | bytes 786440 | tf_op jit(solution)/shard_map/swap_ahead1/ppermute | solution.py:260
  24.2 7.8 %collective-permute-start.9 = (bf16[2,128,512]{2,1,0:T(8,128)(2,1)S(1)}, bf16[2,128,512]{2,1,0:T(8,128)(2,1)S(1)}, u32[]{:S(2)}, u32[]{:S(2)}) collective-permute-start(bf16[2,128,512]{2,1,0:T(8,128)(2,1)S(1)} %collective-permute-done.6.refs_4_), channel_id=1, source_target_pairs={{0,1},{1,0},{2,3},{3,2},{4,5},{5,4},{6,7},{7,6},{8,9},{9,8},{10,11... | collective-permute-start | bytes 786440 | tf_op jit(solution)/shard_map/queries_sibling/ppermute | solution.py:306
  24.8 12.7 %collective-permute-start.11 = (bf16[256,512]{1,0:T(8,128)(2,1)S(1)}, bf16[256,512]{1,0:T(8,128)(2,1)S(1)}, u32[]{:S(2)}, u32[]{:S(2)}) collective-permute-start(bf16[256,512]{1,0:T(8,128)(2,1)S(1)} %collective-permute-done.1.refs_8_), channel_id=1, source_target_pairs={{0,4},{4,0},{8,12},{12,8},{16,20},{20,16},{24,28},{28,24},{1,5},{5... | collective-permute-start | bytes 786440 | tf_op jit(solution)/shard_map/swap_back1/ppermute | solution.py:260
  27.7 14.2 %copy-start = (s32[8]{0:T(128)S(1)}, s32[8]{0:T(128)}, u32[]{:S(2)}) copy-start(s32[8]{0:T(128)} %bucket_ref.3) | copy-start | bytes 100
  27.7 9.8 %collective-permute-start.10 = (bf16[2,128,512]{2,1,0:T(8,128)(2,1)S(1)}, bf16[2,128,512]{2,1,0:T(8,128)(2,1)S(1)}, u32[]{:S(2)}, u32[]{:S(2)}) collective-permute-start(bf16[2,128,512]{2,1,0:T(8,128)(2,1)S(1)} %attend.2.refs_0_), channel_id=1, source_target_pairs={{0,2},{1,3},{2,0},{3,1},{4,6},{5,7},{6,4},{7,5},{8,10},{9,11},{10,... | collective-permute-start | bytes 786440 | tf_op jit(solution)/shard_map/attended0_same/ppermute | solution.py:297
  34.2 7.7 %collective-permute-start.16 = (bf16[2,128,512]{2,1,0:T(8,128)(2,1)S(1)}, bf16[2,128,512]{2,1,0:T(8,128)(2,1)S(1)}, u32[]{:S(2)}, u32[]{:S(2)}) collective-permute-start(bf16[2,128,512]{2,1,0:T(8,128)(2,1)S(1)} %attend.3.refs_0_), channel_id=1, source_target_pairs={{0,2},{1,3},{2,0},{3,1},{4,6},{5,7},{6,4},{7,5},{8,10},{9,11},{10,... | collective-permute-start | bytes 786440 | tf_op jit(solution)/shard_map/attended1_same/ppermute | solution.py:297
  34.8 7.1 %collective-permute-start.14 = (bf16[256,512]{1,0:T(8,128)(2,1)S(1)}, bf16[256,512]{1,0:T(8,128)(2,1)S(1)}, u32[]{:S(2)}, u32[]{:S(2)}) collective-permute-start(bf16[256,512]{1,0:T(8,128)(2,1)S(1)} %collective-permute-done.7.refs_10_), channel_id=1, source_target_pairs={{0,4},{4,0},{8,12},{12,8},{16,20},{20,16},{24,28},{28,24},{1,5},{5... | collective-permute-start | bytes 786440 | tf_op jit(solution)/shard_map/swap_ahead2/ppermute | solution.py:260
  37.5 4.3 %collective-permute-start.12 = (bf16[2,128,512]{2,1,0:T(8,128)(2,1)S(1)}, bf16[2,128,512]{2,1,0:T(8,128)(2,1)S(1)}, u32[]{:S(2)}, u32[]{:S(2)}) collective-permute-start(bf16[2,128,512]{2,1,0:T(8,128)(2,1)S(1)} %attend.3.refs_0_), channel_id=1, source_target_pairs={{0,1},{1,0},{2,3},{3,2},{4,5},{5,4},{6,7},{7,6},{8,9},{9,8},{10,11... | collective-permute-start | bytes 786440 | tf_op jit(solution)/shard_map/spread0_1_sibling/ppermute | solution.py:306
  37.5 4.3 %collective-permute-start.13 = (bf16[2,128,512]{2,1,0:T(8,128)(2,1)S(1)}, bf16[2,128,512]{2,1,0:T(8,128)(2,1)S(1)}, u32[]{:S(2)}, u32[]{:S(2)}) collective-permute-start(bf16[2,128,512]{2,1,0:T(8,128)(2,1)S(1)} %collective-permute-done.10.refs_2_), channel_id=1, source_target_pairs={{0,1},{1,0},{2,3},{3,2},{4,5},{5,4},{6,7},{7,6},{8,9},{9,8},{10,11... | collective-permute-start | bytes 786440 | tf_op jit(solution)/shard_map/spread1_0_sibling/ppermute | solution.py:306
  38.0 7.1 %collective-permute-start.15 = (bf16[2,128,512]{2,1,0:T(8,128)(2,1)S(1)}, bf16[2,128,512]{2,1,0:T(8,128)(2,1)S(1)}, u32[]{:S(2)}, u32[]{:S(2)}) collective-permute-start(bf16[2,128,512]{2,1,0:T(8,128)(2,1)S(1)} %attend.2.refs_0_), channel_id=1, source_target_pairs={{0,1},{1,0},{2,3},{3,2},{4,5},{5,4},{6,7},{7,6},{8,9},{9,8},{10,11... | collective-permute-start | bytes 786440 | tf_op jit(solution)/shard_map/spread0_0_sibling/ppermute | solution.py:306
  41.8 3.3 %collective-permute-start.17 = (bf16[2,128,512]{2,1,0:T(8,128)(2,1)S(1)}, bf16[2,128,512]{2,1,0:T(8,128)(2,1)S(1)}, u32[]{:S(2)}, u32[]{:S(2)}) collective-permute-start(bf16[2,128,512]{2,1,0:T(8,128)(2,1)S(1)} %collective-permute-done.16.refs_2_), channel_id=1, source_target_pairs={{0,1},{1,0},{2,3},{3,2},{4,5},{5,4},{6,7},{7,6},{8,9},{9,8},{10,11... | collective-permute-start | bytes 786440 | tf_op jit(solution)/shard_map/spread1_1_sibling/ppermute | solution.py:306
  43.2 6.4 %collective-permute-start.19 = (bf16[128,512]{1,0:T(8,128)(2,1)S(1)}, bf16[128,512]{1,0:T(8,128)(2,1)S(1)}, u32[]{:S(2)}, u32[]{:S(2)}) collective-permute-start(bf16[128,512]{1,0:T(8,128)(2,1)S(1)} %get-tuple-element.39), channel_id=1, source_target_pairs={{0,2},{1,3},{2,0},{3,1},{4,6},{5,7},{6,4},{7,5},{8,10},{9,11},{10,... | collective-permute-start | bytes 393224 | tf_op jit(solution)/shard_map/out_same/ppermute | solution.py:297
  44.0 2.8 %copy-start.1 = (f32[1,256,512]{2,1,0:T(8,128)S(1)}, f32[1,256,512]{2,1,0:T(8,128)}, u32[]{:S(2)}) copy-start(f32[1,256,512]{2,1,0:T(8,128)} %param.13) | copy-start | bytes 1572868
  44.0 2.8 %copy-start.2 = (f32[1,256,512]{2,1,0:T(8,128)S(1)}, f32[1,256,512]{2,1,0:T(8,128)}, u32[]{:S(2)}) copy-start(f32[1,256,512]{2,1,0:T(8,128)} %param.14) | copy-start | bytes 1572868
  44.0 2.8 %copy-start.3 = (f32[1,256,512]{2,1,0:T(8,128)S(1)}, f32[1,256,512]{2,1,0:T(8,128)}, u32[]{:S(2)}) copy-start(f32[1,256,512]{2,1,0:T(8,128)} %param.15) | copy-start | bytes 1572868
  44.0 2.8 %copy-start.4 = (f32[1,256,512]{2,1,0:T(8,128)S(1)}, f32[1,256,512]{2,1,0:T(8,128)}, u32[]{:S(2)}) copy-start(f32[1,256,512]{2,1,0:T(8,128)} %param.16) | copy-start | bytes 1572868
  44.0 7.5 %collective-permute-start.20 = (bf16[128,512]{1,0:T(8,128)(2,1)S(1)}, bf16[128,512]{1,0:T(8,128)(2,1)S(1)}, u32[]{:S(2)}, u32[]{:S(2)}) collective-permute-start(bf16[128,512]{1,0:T(8,128)(2,1)S(1)} %get-tuple-element.45), channel_id=1, source_target_pairs={{0,3},{1,2},{2,1},{3,0},{4,7},{5,6},{6,5},{7,4},{8,11},{9,10},{10,... | collective-permute-start | bytes 393224 | tf_op jit(solution)/shard_map/out_cross/ppermute | solution.py:302
  46.5 5.1 %collective-permute-start.18 = (bf16[128,512]{1,0:T(8,128)(2,1)S(1)}, bf16[128,512]{1,0:T(8,128)(2,1)S(1)}, u32[]{:S(2)}, u32[]{:S(2)}) collective-permute-start(bf16[128,512]{1,0:T(8,128)(2,1)S(1)} %get-tuple-element.44), channel_id=1, source_target_pairs={{0,1},{1,0},{2,3},{3,2},{4,5},{5,4},{6,7},{7,6},{8,9},{9,8},{10,11... | collective-permute-start | bytes 393224 | tf_op jit(solution)/shard_map/out_sibling/ppermute | solution.py:306

commit v4 on v3

--- a/solution.py
+++ b/solution.py
@@ -33,6 +33,20 @@
 HALF_STEPS = 2
 PROJECT_US = 2
 
+FIRST = {
+    "half": ["cut"],
+    "queries1_same": ["pairs1_same"],
+    "queries1_cross": ["pairs1_same", "sibling", "pairs1_cross"],
+    "attend0": ["swap_own"],
+    "attend1": ["attend0", "ahead3"],
+    "attended1_to1": ["swap_ahead1"],
+    "sibling0_for1": ["attended0_to1"],
+    "sibling1_for1": ["swap_ahead3"],
+    "sibling0_for0": ["attended0_to1"],
+    "project0": ["project1"],
+    "states": ["attended0_to1"],
+}
+
 SMALL = pltpu.CompilerParams(vmem_limit_bytes=16 * 1024 * 1024)
 IN_VMEM = pl.BlockSpec(memory_space=pltpu.VMEM)
 IN_SMEM = pl.BlockSpec(memory_space=pltpu.SMEM)
@@ -52,8 +66,22 @@
     return jnp.where(moved >= size, moved - size, moved)
 
 
-def after(value, *others):
-    return lax.optimization_barrier((value,) + others)[0]
+class Seen:
+    def __init__(self):
+        self.values = {}
+
+    def add(self, name, value):
+        self.values[name] = value
+        return value
+
+    def after(self, name, value):
+        others = [self.values[n] for n in FIRST.get(name, ()) if n in self.values]
+        return lax.optimization_barrier((value, *others))[0] if others else value
+
+    def permute(self, name, array, axis, perm):
+        array = self.after(name, array)
+        with jax.named_scope(name):
+            return self.add(name, lax.ppermute(array, axis, perm))
 
 
 def half_kernel(master_ref, first_ref, second_ref, gradient_ref, half_ref):
@@ -84,7 +112,7 @@
 
 def cut_kernel(query, key, value, *refs):
     blocks, sems = refs[:-1], refs[-1]
-    chips = (len(blocks) - 2) // 3 + 1
+    chips = (len(blocks) - 2) // 4 + 1
     wide = blocks[0].shape[-1]
     chip, core = chip_and_core()
     copies = []
@@ -97,13 +125,13 @@
     for step in range(1, chips):
         for crossed in range(2):
             for i, array in enumerate((key, value)):
-                copy(array, step, crossed, blocks[3 * step - 1 + crossed].at[i])
+                copy(array, step, crossed, blocks[4 * step - 2 + crossed].at[i])
     for crossed in (1, 0):
         for i, array in enumerate((query, key, value)):
             copy(array, 0, crossed, blocks[crossed].at[i])
     for step in range(1, chips):
         for crossed in range(2):
-            copy(query, step, crossed, blocks[3 * step + 1].at[crossed])
+            copy(query, step, crossed, blocks[4 * step + crossed].at[0])
     for one in copies:
         one.start()
     for one in copies:
@@ -113,7 +141,7 @@
 def cut(*arrays):
     groups = lax.axis_size("seq")
     rows, width = arrays[0].shape
-    counts = [3, 3] + [2] * (3 * (groups // 2 - 1))
+    counts = [3, 3] + [2, 2, 1, 1] * (groups // 2 - 1)
     return pl.pallas_call(
         cut_kernel,
         out_shape=[
@@ -164,7 +192,7 @@
 def attend(counts, pairs, queries=()):
     _, rows, wide = pairs[0].shape
     n_pairs = len(pairs)
-    picks = ((n_pairs, 0), (n_pairs + 1, 1)) if queries else ((0, 0), (1, 0))
+    picks = ((n_pairs, 0), (n_pairs + 1, 0)) if queries else ((0, 0), (1, 0))
     return pl.pallas_call(
         functools.partial(attend_kernel, n_pairs, picks),
         out_shape=jax.ShapeDtypeStruct((2, rows, wide), jnp.bfloat16),
@@ -246,35 +274,27 @@
     )(*blocks)
 
 
-def gather_weights(shard, first):
+def gather_weights(seen, shard):
     owners = lax.axis_size("dp")
     ring = owners // 2
 
     def moved(block, step, name):
         perm = [(o, (o // 2 + step) % ring * 2 + o % 2) for o in range(owners)]
-        with jax.named_scope(name):
-            return lax.ppermute(block, "dp", perm)
-
-    def swapped(block, name):
-        with jax.named_scope(name):
-            return lax.ppermute(block, "dp", [(o, o ^ 1) for o in range(owners)])
-
-    steps, held, names = [0], [shard], ["swap_own"]
-    ahead, back = shard, shard
+        return seen.permute(name, block, "dp", perm)
+
+    held = [(0, shard, "swap_own")]
+    ahead = back = shard
     for step in range(1, ring // 2 + 1):
         ahead = moved(ahead, 1, f"ahead{step}")
-        held.append(ahead)
-        names.append(f"swap_ahead{step}")
-        steps.append((-step) % ring)
+        held.append((-step % ring, ahead, f"swap_ahead{step}"))
         if step <= (ring - 1) // 2:
             back = moved(back, -1, f"back{step}")
-            held.append(back)
-            names.append(f"swap_back{step}")
-            steps.append(step)
-    blocks = [shard, swapped(after(shard, first), names[0])]
-    for block, name in zip(held[1:], names[1:]):
-        blocks += [block, swapped(block, name)]
-    return steps, blocks, held[1:]
+            held.append((step, back, f"swap_back{step}"))
+    blocks = []
+    for _, block, name in held:
+        swapped = seen.permute(name, block, "dp", [(o, o ^ 1) for o in range(owners)])
+        blocks += [block, swapped]
+    return [step for step, _, _ in held], blocks
 
 
 def body(
@@ -290,68 +310,66 @@
 ):
     groups = lax.axis_size("seq")
     chips = groups // 2
-
-    def to_same(array, step, name):
+    seen = Seen()
+
+    def to_same(name, array, step):
         perm = [(s, (s // 2 + step) % chips * 2 + s % 2) for s in range(groups)]
-        with jax.named_scope(name):
-            return lax.ppermute(array, "seq", perm)
-
-    def to_cross(array, step, name):
+        return seen.permute(name, array, "seq", perm)
+
+    def to_cross(name, array, step):
         perm = [(s, (s // 2 + step) % chips * 2 + 1 - s % 2) for s in range(groups)]
-        with jax.named_scope(name):
-            return lax.ppermute(array, "seq", perm)
-
-    def to_sibling(array, name):
-        with jax.named_scope(name):
-            return lax.ppermute(array, "seq", [(s, s ^ 1) for s in range(groups)])
-
-    master, first = master_weight[0], first_moment[0]
-    second, grad = second_moment[0], gradient[0]
+        return seen.permute(name, array, "seq", perm)
+
+    def to_sibling(name, array):
+        return seen.permute(name, array, "seq", [(s, s ^ 1) for s in range(groups)])
 
     own, other, *rest = cut(queries[0], hit_keys[0], hit_values[0])
-    rounded = half(master, first, second, grad)
-    sibling = to_sibling(other, "sibling")
-    steps, weights, ring = gather_weights(rounded, sibling)
-    pairs, asked = [own, sibling], [()]
+    seen.add("cut", own)
+    master = seen.after("half", master_weight[0])
+    rounded = seen.add("half", half(master, first_moment[0], second_moment[0], gradient[0]))
+    pairs = [own, to_sibling("sibling", other)]
     for step in range(1, chips):
-        same, cross, queries_for = rest[3 * step - 3 : 3 * step]
+        same, cross = rest[4 * step - 4 : 4 * step - 4 + 2]
         pairs += [
-            to_same(same, step, "pairs_same"),
-            to_cross(after(cross, sibling), step, "pairs_cross"),
+            to_same(f"pairs{step}_same", same, step),
+            to_cross(f"pairs{step}_cross", cross, step),
         ]
-        here = to_same(after(queries_for, pairs[-2], rounded), step, "queries")
-        asked.append((here, to_sibling(here, "queries_sibling")))
-
-    attended = [attend(hit_counts, [after(own, ring[0], ring[1], weights[1])] + pairs[1:])]
-    for here, beside in asked[1:]:
-        attended.append(attend(hit_counts, pairs, (after(here, attended[-1], ring[2], weights[3]), beside)))
-    pass
+    steps, weights = gather_weights(seen, rounded)
+    asked = [()]
+    for step in range(1, chips):
+        for_same, for_cross = rest[4 * step - 2 : 4 * step]
+        asked.append(
+            (
+                to_same(f"queries{step}_same", for_same, step),
+                to_cross(f"queries{step}_cross", for_cross, step),
+            )
+        )
+    own = seen.after("attend0", own)
+    attended = [seen.add("attend0", attend(hit_counts, [own] + pairs[1:]))]
+    for e, (here, far) in enumerate(asked[1:], 1):
+        here = seen.after(f"attend{e}", here)
+        attended.append(seen.add(f"attend{e}", attend(hit_counts, pairs, (here, far))))
     spread = [attended] + [
-        [to_same(a, step, f"attended{e}_same") for e, a in enumerate(attended)]
+        [to_same(f"attended{e}_to{step}", a, step) for e, a in enumerate(attended)]
         for step in range(1, chips)
     ]
-    beside = [
-        [to_sibling(after(a, spread[1][0], weights[5]), f"spread{d}_{e}_sibling") for e, a in enumerate(row)]
-        for d, row in enumerate(spread)
-    ]
-
     columns = [None] * groups
     for e in list(range(1, chips)) + [0]:
         att = []
         for d in range(chips):
-            att += [spread[d][(e - d) % chips], beside[d][(e - d) % chips]]
+            a = spread[d][(e - d) % chips]
+            att += [a, to_sibling(f"sibling{d}_for{e}", a)]
+        att[0] = seen.after(f"project{e}", att[0])
+        out, other = project(owner_bucket, att, steps, weights)
+        seen.add(f"project{e}", out)
         if e == 0:
-            att[0] = after(att[0], out)
-        out, other = project(owner_bucket, att, steps, weights)
-        if e == 0:
-            columns[0], columns[1] = out, to_sibling(other, "out_sibling")
+            columns[0], columns[1] = out, to_sibling("out_sibling", other)
         else:
-            columns[2 * e] = to_same(out, chips - e, "out_same")
-            columns[2 * e + 1] = to_cross(other, chips - e, "out_cross")
+            columns[2 * e] = to_same(f"out{e}_same", out, chips - e)
+            columns[2 * e + 1] = to_cross(f"out{e}_cross", other, chips - e)
     projected = place(columns)[None]
-    new_master, new_first, new_second = adam_update(*lax.optimization_barrier(
-        (master_weight, first_moment, second_moment, gradient, columns[0]))[:4])
-    return (projected, new_master, new_first, new_second)
+    states = adam_update(seen.after("states", master_weight), first_moment, second_moment, gradient)
+    return (projected, *states)
 
 
 def solution(mesh):

time: 52.6 us -> 49 us (0.932)
  waiting for transfers between devices: 20.6 us -> 11.7 us
  starting transfers between devices: 17.7 us -> 22.5 us
    ppermute x21, waiting for transfers between devices: 20.6 us -> 11.7 us  [permute(): return self.add(name, lax.ppermute(array, axis, perm))]
    ppermute x21, starting transfers between devices: 17.7 us -> 22.5 us  [permute(): return self.add(name, lax.ppermute(array, axis, perm))]
  transfers between devices with their start and end apart: 21 -> 21, of which waited for: 9 -> 8; matrix products, arithmetic and copies ran while one was open for 3% -> 3% of each run, Pallas kernels for 17% -> 18%
where the time goes in v4:
time: 49 us; the launch traced here: 48.3 us
  starting transfers between devices  22.5 us (46%)
  waiting for transfers between devices  11.7 us (24%)
  Pallas kernels  11.2 us (23%)
  other arithmetic  1.43 us (3%)
  between operations  1.39 us (3%)
    ppermute x21, starting transfers between devices, permute(): return self.add(name, lax.ppermute(array, axis, perm))  22.5 us
    ppermute x21, waiting for transfers between devices, permute(): return self.add(name, lax.ppermute(array, axis, perm))  11.7 us
    pallas_call x2, Pallas kernels, attend(): pl.pallas_call(functools.partial(attend_kernel, n_pairs, picks), out_shap...  4.51 us
    pallas_call x2, Pallas kernels, project(): pl.pallas_call(functools.partial(project_kernel, len(att), steps), out_sh...  2.59 us
    pallas_call x1, Pallas kernels, half(): pl.pallas_call(half_kernel, grid=(HALF_STEPS,), out_shape=jax.ShapeDtypeS...  1.73 us
    pallas_call x1, Pallas kernels, cut(): pl.pallas_call(cut_kernel, out_shape=[jax.ShapeDtypeStruct((n, rows, widt...  1.57 us
    sub x1, other arithmetic, adam_update(): master_weight - learn_rate * (first_hat / (jnp.sqrt(second_hat) + epsilon...  1.43 us
  transfers between devices with their start and end apart: 21, of which 8 were waited for; matrix products, arithmetic and copies ran while one was open for 3% of the time, Pallas kernels for 18%

profile of v4, /device:TPU:0, one launch (start us, length us, event | category | flops | bytes accessed | tf_op | source)
XLA Modules:
  0.0 48.3 jit_solution(12466999546212462493)
XLA Ops:
  0.6 1.6 %cut.1 = (bf16[3,128,512]{2,1,0:T(8,128)(2,1)S(1)}, bf16[3,128,512]{2,1,0:T(8,128)(2,1)S(1)}, bf16[2,128,512]{2,1,0:T(8,128)(2,1)S(1)}, bf16[2,128,512]{2,1,0:T(...) custom-call(bf16[128,2048]{1,0:T(8,128)(2,1)} %bitcast.12, ...), custom_call_target="tpu_custom_call" | custom-call | bytes 3690000 | tf_op jit(solution)/shard_map/cut/pallas_call | solution.py:145
  2.2 0.5 %collective-permute-start.1 = (bf16[3,128,512]{2,1,0:T(8,128)(2,1)S(1)}, bf16[3,128,512]{2,1,0:T(8,128)(2,1)S(1)}, u32[]{:S(2)}, u32[]{:S(2)}) collective-permute-start(bf16[3,128,512]{2,1,0:T(8,128)(2,1)S(1)} %get-tuple-element.27), channel_id=1, source_target_pairs={{0,1},{1,0},{2,3},{3,2},{4,5},{5,4},{6,7},{7,6},{8,9},{9,8},{10,11... | collective-permute-start | bytes 1179656 | tf_op jit(solution)/shard_map/sibling/ppermute | solution.py:84
  2.7 2.6 %collective-permute-start.2 = (bf16[2,128,512]{2,1,0:T(8,128)(2,1)S(1)}, bf16[2,128,512]{2,1,0:T(8,128)(2,1)S(1)}, u32[]{:S(2)}, u32[]{:S(2)}) collective-permute-start(bf16[2,128,512]{2,1,0:T(8,128)(2,1)S(1)} %get-tuple-element.28), channel_id=1, source_target_pairs={{0,2},{1,3},{2,0},{3,1},{4,6},{5,7},{6,4},{7,5},{8,10},{9,11},{10,... | collective-permute-start | bytes 786440 | tf_op jit(solution)/shard_map/pairs1_same/ppermute | solution.py:84
  5.3 1.7 %half.1.refs_4_ = bf16[256,512]{1,0:T(8,128)(2,1)S(1)} custom-call(f32[256,512]{1,0:T(8,128)} %bitcast.8, f32[256,512]{1,0:T(8,128)} %bitcast.9, f32[256,512]{1,0:T(8,128)} %bitcast.10, f32[256,512]{1,0:T(8,128)} %bitcast.11), custom_call_target="tpu_custom_call" | custom-call | bytes 3690000 | tf_op jit(solution)/shard_map/half/pallas_call | solution.py:98
  7.1 1.6 %collective-permute-start.9 = (bf16[256,512]{1,0:T(8,128)(2,1)S(1)}, bf16[256,512]{1,0:T(8,128)(2,1)S(1)}, u32[]{:S(2)}, u32[]{:S(2)}) collective-permute-start(bf16[256,512]{1,0:T(8,128)(2,1)S(1)} %half.1.refs_4_), channel_id=1, source_target_pairs={{0,8},{4,12},{8,16},{12,20},{16,24},{20,28},{24,0},{28,4},{1,9},{5... | collective-permute-start | bytes 786440 | tf_op jit(solution)/shard_map/ahead1/ppermute | solution.py:84
  8.7 1.5 %collective-permute-start = (bf16[256,512]{1,0:T(8,128)(2,1)S(1)}, bf16[256,512]{1,0:T(8,128)(2,1)S(1)}, u32[]{:S(2)}, u32[]{:S(2)}) collective-permute-start(bf16[256,512]{1,0:T(8,128)(2,1)S(1)} %half.1.refs_4_), channel_id=1, source_target_pairs={{0,4},{4,0},{8,12},{12,8},{16,20},{20,16},{24,28},{28,24},{1,5},{5... | collective-permute-start | bytes 786440 | tf_op jit(solution)/shard_map/swap_own/ppermute | solution.py:84
  10.2 2.3 %collective-permute-done.2.refs_2_ = bf16[2,128,512]{2,1,0:T(8,128)(2,1)S(1)} collective-permute-done((bf16[2,128,512]{2,1,0:T(8,128)(2,1)S(1)}, bf16[2,128,512]{2,1,0:T(8,128)(2,1)S(1)}, u32[]{:S(2)}, u32[]{:S(2)}) %collective-permute-start.2) | collective-permute-done | bytes 262176 | tf_op jit(solution)/shard_map/pairs1_same/ppermute | solution.py:84
  12.5 4.0 %collective-permute-start.11 = (bf16[256,512]{1,0:T(8,128)(2,1)S(1)}, bf16[256,512]{1,0:T(8,128)(2,1)S(1)}, u32[]{:S(2)}, u32[]{:S(2)}) collective-permute-start(bf16[256,512]{1,0:T(8,128)(2,1)S(1)} %half.1.refs_4_), channel_id=1, source_target_pairs={{0,24},{4,28},{8,0},{12,4},{16,8},{20,12},{24,16},{28,20},{1,25},{... | collective-permute-start | bytes 786440 | tf_op jit(solution)/shard_map/back1/ppermute | solution.py:84
  16.5 1.4 %collective-permute-done.9.refs_6_ = bf16[256,512]{1,0:T(8,128)(2,1)S(1)} collective-permute-done((bf16[256,512]{1,0:T(8,128)(2,1)S(1)}, bf16[256,512]{1,0:T(8,128)(2,1)S(1)}, u32[]{:S(2)}, u32[]{:S(2)}) %collective-permute-start.9) | collective-permute-done | bytes 262176 | tf_op jit(solution)/shard_map/ahead1/ppermute | solution.py:84
  17.9 1.5 %collective-permute-start.10 = (bf16[256,512]{1,0:T(8,128)(2,1)S(1)}, bf16[256,512]{1,0:T(8,128)(2,1)S(1)}, u32[]{:S(2)}, u32[]{:S(2)}) collective-permute-start(bf16[256,512]{1,0:T(8,128)(2,1)S(1)} %collective-permute-done.9.refs_6_), channel_id=1, source_target_pairs={{0,4},{4,0},{8,12},{12,8},{16,20},{20,16},{24,28},{28,24},{1,5},{5... | collective-permute-start | bytes 786440 | tf_op jit(solution)/shard_map/swap_ahead1/ppermute | solution.py:84
  19.4 0.1 collective-permute-start.4
  20.2 1.6 %collective-permute-start.13 = (bf16[256,512]{1,0:T(8,128)(2,1)S(1)}, bf16[256,512]{1,0:T(8,128)(2,1)S(1)}, u32[]{:S(2)}, u32[]{:S(2)}) collective-permute-start(bf16[256,512]{1,0:T(8,128)(2,1)S(1)} %collective-permute-done.9.refs_6_), channel_id=1, source_target_pairs={{0,8},{4,12},{8,16},{12,20},{16,24},{20,28},{24,0},{28,4},{1,9},{5... | collective-permute-start | bytes 786440 | tf_op jit(solution)/shard_map/ahead2/ppermute | solution.py:84
  21.8 2.3 %attend.2.refs_0_ = bf16[2,128,512]{2,1,0:T(8,128)(2,1)S(1)} custom-call(s32[1]{0:T(128)S(6)} %copy.13.count_ref, bf16[3,128,512]{2,1,0:T(8,128)(2,1)S(1)} %get-tuple-element.26.refs_0_, bf16[3,128,512]{2,1,0:T(8,128)(2,1)S(1)} %collective-permute-done.1.refs_1_, bf16[2,128,512]{2,1,0:T(8,128)(2,1)S(1)} %collective-permute-done.2.refs_2_, ...), custom_call_target="tpu_custom_call" | custom-call | bytes 11070000 | tf_op jit(solution)/shard_map/attend/pallas_call | solution.py:196
  24.1 1.6 %collective-permute-start.6 = (bf16[2,128,512]{2,1,0:T(8,128)(2,1)S(1)}, bf16[2,128,512]{2,1,0:T(8,128)(2,1)S(1)}, u32[]{:S(2)}, u32[]{:S(2)}) collective-permute-start(bf16[2,128,512]{2,1,0:T(8,128)(2,1)S(1)} %attend.2.refs_0_), channel_id=1, source_target_pairs={{0,2},{1,3},{2,0},{3,1},{4,6},{5,7},{6,4},{7,5},{8,10},{9,11},{10,... | collective-permute-start | bytes 786440 | tf_op jit(solution)/shard_map/attended0_to1/ppermute | solution.py:84
  25.7 1.5 %collective-permute-start.12 = (bf16[256,512]{1,0:T(8,128)(2,1)S(1)}, bf16[256,512]{1,0:T(8,128)(2,1)S(1)}, u32[]{:S(2)}, u32[]{:S(2)}) collective-permute-start(bf16[256,512]{1,0:T(8,128)(2,1)S(1)} %collective-permute-done.11.refs_8_), channel_id=1, source_target_pairs={{0,4},{4,0},{8,12},{12,8},{16,20},{20,16},{24,28},{28,24},{1,5},{5... | collective-permute-start | bytes 786440 | tf_op jit(solution)/shard_map/swap_back1/ppermute | solution.py:84
  27.2 2.3 %attend.3.refs_0_ = bf16[2,128,512]{2,1,0:T(8,128)(2,1)S(1)} custom-call(s32[1]{0:T(128)S(6)} %copy.13.count_ref, bf16[3,128,512]{2,1,0:T(8,128)(2,1)S(1)} %get-tuple-element.26.refs_0_, bf16[3,128,512]{2,1,0:T(8,128)(2,1)S(1)} %collective-permute-done.1.refs_1_, bf16[2,128,512]{2,1,0:T(8,128)(2,1)S(1)} %collective-permute-done.2.refs_2_, ...), custom_call_target="tpu_custom_call" | custom-call | bytes 11070000 | tf_op jit(solution)/shard_map/attend/pallas_call | solution.py:196
  29.5 0.6 %collective-permute-start.16 = (bf16[2,128,512]{2,1,0:T(8,128)(2,1)S(1)}, bf16[2,128,512]{2,1,0:T(8,128)(2,1)S(1)}, u32[]{:S(2)}, u32[]{:S(2)}) collective-permute-start(bf16[2,128,512]{2,1,0:T(8,128)(2,1)S(1)} %attend.3.refs_0_), channel_id=1, source_target_pairs={{0,2},{1,3},{2,0},{3,1},{4,6},{5,7},{6,4},{7,5},{8,10},{9,11},{10,... | collective-permute-start | bytes 786440 | tf_op jit(solution)/shard_map/attended1_to1/ppermute | solution.py:84
  30.1 0.1 collective-permute-done.13.refs_10_
  30.2 2.5 %collective-permute-start.14 = (bf16[256,512]{1,0:T(8,128)(2,1)S(1)}, bf16[256,512]{1,0:T(8,128)(2,1)S(1)}, u32[]{:S(2)}, u32[]{:S(2)}) collective-permute-start(bf16[256,512]{1,0:T(8,128)(2,1)S(1)} %collective-permute-done.13.refs_10_), channel_id=1, source_target_pairs={{0,4},{4,0},{8,12},{12,8},{16,20},{20,16},{24,28},{28,24},{1,5},{5... | collective-permute-start | bytes 786440 | tf_op jit(solution)/shard_map/swap_ahead2/ppermute | solution.py:84
  32.7 0.6 %collective-permute-done.6.refs_2_ = bf16[2,128,512]{2,1,0:T(8,128)(2,1)S(1)} collective-permute-done((bf16[2,128,512]{2,1,0:T(8,128)(2,1)S(1)}, bf16[2,128,512]{2,1,0:T(8,128)(2,1)S(1)}, u32[]{:S(2)}, u32[]{:S(2)}) %collective-permute-start.6) | collective-permute-done | bytes 262176 | tf_op jit(solution)/shard_map/attended0_to1/ppermute | solution.py:84
  33.3 0.5 %collective-permute-start.8 = (bf16[2,128,512]{2,1,0:T(8,128)(2,1)S(1)}, bf16[2,128,512]{2,1,0:T(8,128)(2,1)S(1)}, u32[]{:S(2)}, u32[]{:S(2)}) collective-permute-start(bf16[2,128,512]{2,1,0:T(8,128)(2,1)S(1)} %collective-permute-done.6.refs_2_), channel_id=1, source_target_pairs={{0,1},{1,0},{2,3},{3,2},{4,5},{5,4},{6,7},{7,6},{8,9},{9,8},{10,11... | collective-permute-start | bytes 786440 | tf_op jit(solution)/shard_map/sibling1_for1/ppermute | solution.py:84
  33.8 4.6 %collective-permute-done.16.refs_2_ = bf16[2,128,512]{2,1,0:T(8,128)(2,1)S(1)} collective-permute-done((bf16[2,128,512]{2,1,0:T(8,128)(2,1)S(1)}, bf16[2,128,512]{2,1,0:T(8,128)(2,1)S(1)}, u32[]{:S(2)}, u32[]{:S(2)}) %collective-permute-start.16) | collective-permute-done | bytes 262176 | tf_op jit(solution)/shard_map/attended1_to1/ppermute | solution.py:84
  38.5 0.8 %collective-permute-done.14.refs_11_ = bf16[256,512]{1,0:T(8,128)(2,1)S(1)} collective-permute-done((bf16[256,512]{1,0:T(8,128)(2,1)S(1)}, bf16[256,512]{1,0:T(8,128)(2,1)S(1)}, u32[]{:S(2)}, u32[]{:S(2)}) %collective-permute-start.14) | collective-permute-done | bytes 262176 | tf_op jit(solution)/shard_map/swap_ahead2/ppermute | solution.py:84
  39.3 1.3 %project.2 = (bf16[128,512]{1,0:T(8,128)(2,1)S(1)}, bf16[128,512]{1,0:T(8,128)(2,1)S(1)}) custom-call(s32[8]{0:T(128)S(1)} %copy-done, bf16[2,128,512]{2,1,0:T(8,128)(2,1)S(1)} %attend.3.refs_0_, bf16[2,128,512]{2,1,0:T(8,128)(2,1)S(1)} %collective-permute-done.7.refs_1_, bf16[2,128,512]{2,1,0:T(8,128)(2,1)S(1)} %collective-permute-done.6.refs_2_, ...), custom_call_target="tpu_custom_call" | custom-call | bytes 7380000 | tf_op jit(solution)/shard_map/project/pallas_call | solution.py:243
  40.6 1.0 %collective-permute-start.19 = (bf16[128,512]{1,0:T(8,128)(2,1)S(1)}, bf16[128,512]{1,0:T(8,128)(2,1)S(1)}, u32[]{:S(2)}, u32[]{:S(2)}) collective-permute-start(bf16[128,512]{1,0:T(8,128)(2,1)S(1)} %get-tuple-element.36), channel_id=1, source_target_pairs={{0,2},{1,3},{2,0},{3,1},{4,6},{5,7},{6,4},{7,5},{8,10},{9,11},{10,... | collective-permute-start | bytes 393224 | tf_op jit(solution)/shard_map/out1_same/ppermute | solution.py:84
  41.6 0.2 collective-permute-start.20
  41.8 1.3 %project.3 = (bf16[128,512]{1,0:T(8,128)(2,1)S(1)}, bf16[128,512]{1,0:T(8,128)(2,1)S(1)}) custom-call(s32[8]{0:T(128)S(1)} %copy-done, bf16[2,128,512]{2,1,0:T(8,128)(2,1)S(1)} %attend.2.refs_0_, bf16[2,128,512]{2,1,0:T(8,128)(2,1)S(1)} %collective-permute-done.15.refs_1_, bf16[2,128,512]{2,1,0:T(8,128)(2,1)S(1)} %collective-permute-done.16.refs_2_, ...), custom_call_target="tpu_custom_call" | custom-call | bytes 7380000 | tf_op jit(solution)/shard_map/project/pallas_call | solution.py:243
  43.1 1.1 %collective-permute-start.18 = (bf16[128,512]{1,0:T(8,128)(2,1)S(1)}, bf16[128,512]{1,0:T(8,128)(2,1)S(1)}, u32[]{:S(2)}, u32[]{:S(2)}) collective-permute-start(bf16[128,512]{1,0:T(8,128)(2,1)S(1)} %get-tuple-element.41), channel_id=1, source_target_pairs={{0,1},{1,0},{2,3},{3,2},{4,5},{5,4},{6,7},{7,6},{8,9},{9,8},{10,11... | collective-permute-start | bytes 393224 | tf_op jit(solution)/shard_map/out_sibling/ppermute | solution.py:84
  44.2 1.4 %multiply_subtract_fusion = (f32[1,256,512]{2,1,0:T(8,128)}, f32[1,256,512]{2,1,0:T(8,128)}, f32[1,256,512]{2,1,0:T(8,128)}) fusion(f32[1,256,512]{2,1,0:T(8,128)S(1)} %copy-done.1, f32[1,256,512]{2,1,0:T(8,128)S(1)} %copy-done.4, f32[1,256,512]{2,1,0:T(8,128)S(1)} %copy-done.2, f32[1,256,512]{2,1,0:T(8,128)S(1)} %copy-done.3), kind=kLoop, calls=%fused_computation.2 | loop fusion | flops 1966080 | bytes 3670016 | tf_op jit(solution)/shard_map/sub | solution.py:26
  45.7 1.2 %collective-permute-done.19.refs_2_ = bf16[128,512]{1,0:T(8,128)(2,1)S(1)} collective-permute-done((bf16[128,512]{1,0:T(8,128)(2,1)S(1)}, bf16[128,512]{1,0:T(8,128)(2,1)S(1)}, u32[]{:S(2)}, u32[]{:S(2)}) %collective-permute-start.19) | collective-permute-done | bytes 131104 | tf_op jit(solution)/shard_map/out1_same/ppermute | solution.py:84
  46.9 0.6 %collective-permute-done.20.refs_3_ = bf16[128,512]{1,0:T(8,128)(2,1)S(1)} collective-permute-done((bf16[128,512]{1,0:T(8,128)(2,1)S(1)}, bf16[128,512]{1,0:T(8,128)(2,1)S(1)}, u32[]{:S(2)}, u32[]{:S(2)}) %collective-permute-start.20) | collective-permute-done | bytes 131104 | tf_op jit(solution)/shard_map/out1_cross/ppermute | solution.py:84
  47.5 0.8 %place.1 = bf16[128,2048]{1,0:T(8,128)(2,1)} custom-call(bf16[128,512]{1,0:T(8,128)(2,1)S(1)} %get-tuple-element.40.refs_0_, bf16[128,512]{1,0:T(8,128)(2,1)S(1)} %collective-permute-done.18.refs_1_, bf16[128,512]{1,0:T(8,128)(2,1)S(1)} %collective-permute-done.19.refs_2_, bf16[128,512]{1,0:T(8,128)(2,1)S(1)} %collective-permute-done.20.refs_3_), custom_call_target="tpu_custom_call" | custom-call | bytes 3690000 | tf_op jit(solution)/shard_map/place/pallas_call | solution.py:266
  (28 shorter events, 0.1 us)
Async XLA Ops:
  2.2 17.3 %collective-permute-start.1 = (bf16[3,128,512]{2,1,0:T(8,128)(2,1)S(1)}, bf16[3,128,512]{2,1,0:T(8,128)(2,1)S(1)}, u32[]{:S(2)}, u32[]{:S(2)}) collective-permute-start(bf16[3,128,512]{2,1,0:T(8,128)(2,1)S(1)} %get-tuple-element.27), channel_id=1, source_target_pairs={{0,1},{1,0},{2,3},{3,2},{4,5},{5,4},{6,7},{7,6},{8,9},{9,8},{10,11... | collective-permute-start | bytes 1179656 | tf_op jit(solution)/shard_map/sibling/ppermute | solution.py:84
  2.7 9.8 %collective-permute-start.2 = (bf16[2,128,512]{2,1,0:T(8,128)(2,1)S(1)}, bf16[2,128,512]{2,1,0:T(8,128)(2,1)S(1)}, u32[]{:S(2)}, u32[]{:S(2)}) collective-permute-start(bf16[2,128,512]{2,1,0:T(8,128)(2,1)S(1)} %get-tuple-element.28), channel_id=1, source_target_pairs={{0,2},{1,3},{2,0},{3,1},{4,6},{5,7},{6,4},{7,5},{8,10},{9,11},{10,... | collective-permute-start | bytes 786440 | tf_op jit(solution)/shard_map/pairs1_same/ppermute | solution.py:84
  7.1 10.8 %collective-permute-start.9 = (bf16[256,512]{1,0:T(8,128)(2,1)S(1)}, bf16[256,512]{1,0:T(8,128)(2,1)S(1)}, u32[]{:S(2)}, u32[]{:S(2)}) collective-permute-start(bf16[256,512]{1,0:T(8,128)(2,1)S(1)} %half.1.refs_4_), channel_id=1, source_target_pairs={{0,8},{4,12},{8,16},{12,20},{16,24},{20,28},{24,0},{28,4},{1,9},{5... | collective-permute-start | bytes 786440 | tf_op jit(solution)/shard_map/ahead1/ppermute | solution.py:84
  8.7 10.7 %collective-permute-start.3 = (bf16[2,128,512]{2,1,0:T(8,128)(2,1)S(1)}, bf16[2,128,512]{2,1,0:T(8,128)(2,1)S(1)}, u32[]{:S(2)}, u32[]{:S(2)}) collective-permute-start(bf16[2,128,512]{2,1,0:T(8,128)(2,1)S(1)} %get-tuple-element.29), channel_id=1, source_target_pairs={{0,3},{1,2},{2,1},{3,0},{4,7},{5,6},{6,5},{7,4},{8,11},{9,10},{10,... | collective-permute-start | bytes 786440 | tf_op jit(solution)/shard_map/pairs1_cross/ppermute | solution.py:84
  8.7 11.5 %collective-permute-start = (bf16[256,512]{1,0:T(8,128)(2,1)S(1)}, bf16[256,512]{1,0:T(8,128)(2,1)S(1)}, u32[]{:S(2)}, u32[]{:S(2)}) collective-permute-start(bf16[256,512]{1,0:T(8,128)(2,1)S(1)} %half.1.refs_4_), channel_id=1, source_target_pairs={{0,4},{4,0},{8,12},{12,8},{16,20},{20,16},{24,28},{28,24},{1,5},{5... | collective-permute-start | bytes 786440 | tf_op jit(solution)/shard_map/swap_own/ppermute | solution.py:84
  12.5 11.6 %collective-permute-start.11 = (bf16[256,512]{1,0:T(8,128)(2,1)S(1)}, bf16[256,512]{1,0:T(8,128)(2,1)S(1)}, u32[]{:S(2)}, u32[]{:S(2)}) collective-permute-start(bf16[256,512]{1,0:T(8,128)(2,1)S(1)} %half.1.refs_4_), channel_id=1, source_target_pairs={{0,24},{4,28},{8,0},{12,4},{16,8},{20,12},{24,16},{28,20},{1,25},{... | collective-permute-start | bytes 786440 | tf_op jit(solution)/shard_map/back1/ppermute | solution.py:84
  17.9 11.6 %collective-permute-start.10 = (bf16[256,512]{1,0:T(8,128)(2,1)S(1)}, bf16[256,512]{1,0:T(8,128)(2,1)S(1)}, u32[]{:S(2)}, u32[]{:S(2)}) collective-permute-start(bf16[256,512]{1,0:T(8,128)(2,1)S(1)} %collective-permute-done.9.refs_6_), channel_id=1, source_target_pairs={{0,4},{4,0},{8,12},{12,8},{16,20},{20,16},{24,28},{28,24},{1,5},{5... | collective-permute-start | bytes 786440 | tf_op jit(solution)/shard_map/swap_ahead1/ppermute | solution.py:84
  19.4 6.3 %collective-permute-start.4 = (bf16[1,128,512]{2,1,0:T(8,128)(2,1)S(1)}, bf16[1,128,512]{2,1,0:T(8,128)(2,1)S(1)}, u32[]{:S(2)}, u32[]{:S(2)}) collective-permute-start(bf16[1,128,512]{2,1,0:T(8,128)(2,1)S(1)} %get-tuple-element.31), channel_id=1, source_target_pairs={{0,2},{1,3},{2,0},{3,1},{4,6},{5,7},{6,4},{7,5},{8,10},{9,11},{10,... | collective-permute-start | bytes 393224 | tf_op jit(solution)/shard_map/queries1_same/ppermute | solution.py:84
  19.5 7.7 %collective-permute-start.5 = (bf16[1,128,512]{2,1,0:T(8,128)(2,1)S(1)}, bf16[1,128,512]{2,1,0:T(8,128)(2,1)S(1)}, u32[]{:S(2)}, u32[]{:S(2)}) collective-permute-start(bf16[1,128,512]{2,1,0:T(8,128)(2,1)S(1)} %get-tuple-element.34), channel_id=1, source_target_pairs={{0,3},{1,2},{2,1},{3,0},{4,7},{5,6},{6,5},{7,4},{8,11},{9,10},{10,... | collective-permute-start | bytes 393224 | tf_op jit(solution)/shard_map/queries1_cross/ppermute | solution.py:84
  20.2 10.0 %collective-permute-start.13 = (bf16[256,512]{1,0:T(8,128)(2,1)S(1)}, bf16[256,512]{1,0:T(8,128)(2,1)S(1)}, u32[]{:S(2)}, u32[]{:S(2)}) collective-permute-start(bf16[256,512]{1,0:T(8,128)(2,1)S(1)} %collective-permute-done.9.refs_6_), channel_id=1, source_target_pairs={{0,8},{4,12},{8,16},{12,20},{16,24},{20,28},{24,0},{28,4},{1,9},{5... | collective-permute-start | bytes 786440 | tf_op jit(solution)/shard_map/ahead2/ppermute | solution.py:84
  24.1 15.2 %copy-start = (s32[8]{0:T(128)S(1)}, s32[8]{0:T(128)}, u32[]{:S(2)}) copy-start(s32[8]{0:T(128)} %bucket_ref.3) | copy-start | bytes 100
  24.1 9.2 %collective-permute-start.6 = (bf16[2,128,512]{2,1,0:T(8,128)(2,1)S(1)}, bf16[2,128,512]{2,1,0:T(8,128)(2,1)S(1)}, u32[]{:S(2)}, u32[]{:S(2)}) collective-permute-start(bf16[2,128,512]{2,1,0:T(8,128)(2,1)S(1)} %attend.2.refs_0_), channel_id=1, source_target_pairs={{0,2},{1,3},{2,0},{3,1},{4,6},{5,7},{6,4},{7,5},{8,10},{9,11},{10,... | collective-permute-start | bytes 786440 | tf_op jit(solution)/shard_map/attended0_to1/ppermute | solution.py:84
  25.7 8.1 %collective-permute-start.12 = (bf16[256,512]{1,0:T(8,128)(2,1)S(1)}, bf16[256,512]{1,0:T(8,128)(2,1)S(1)}, u32[]{:S(2)}, u32[]{:S(2)}) collective-permute-start(bf16[256,512]{1,0:T(8,128)(2,1)S(1)} %collective-permute-done.11.refs_8_), channel_id=1, source_target_pairs={{0,4},{4,0},{8,12},{12,8},{16,20},{20,16},{24,28},{28,24},{1,5},{5... | collective-permute-start | bytes 786440 | tf_op jit(solution)/shard_map/swap_back1/ppermute | solution.py:84
  29.5 9.0 %collective-permute-start.16 = (bf16[2,128,512]{2,1,0:T(8,128)(2,1)S(1)}, bf16[2,128,512]{2,1,0:T(8,128)(2,1)S(1)}, u32[]{:S(2)}, u32[]{:S(2)}) collective-permute-start(bf16[2,128,512]{2,1,0:T(8,128)(2,1)S(1)} %attend.3.refs_0_), channel_id=1, source_target_pairs={{0,2},{1,3},{2,0},{3,1},{4,6},{5,7},{6,4},{7,5},{8,10},{9,11},{10,... | collective-permute-start | bytes 786440 | tf_op jit(solution)/shard_map/attended1_to1/ppermute | solution.py:84
  30.2 9.1 %collective-permute-start.14 = (bf16[256,512]{1,0:T(8,128)(2,1)S(1)}, bf16[256,512]{1,0:T(8,128)(2,1)S(1)}, u32[]{:S(2)}, u32[]{:S(2)}) collective-permute-start(bf16[256,512]{1,0:T(8,128)(2,1)S(1)} %collective-permute-done.13.refs_10_), channel_id=1, source_target_pairs={{0,4},{4,0},{8,12},{12,8},{16,20},{20,16},{24,28},{28,24},{1,5},{5... | collective-permute-start | bytes 786440 | tf_op jit(solution)/shard_map/swap_ahead2/ppermute | solution.py:84
  33.3 6.0 %collective-permute-start.7 = (bf16[2,128,512]{2,1,0:T(8,128)(2,1)S(1)}, bf16[2,128,512]{2,1,0:T(8,128)(2,1)S(1)}, u32[]{:S(2)}, u32[]{:S(2)}) collective-permute-start(bf16[2,128,512]{2,1,0:T(8,128)(2,1)S(1)} %attend.3.refs_0_), channel_id=1, source_target_pairs={{0,1},{1,0},{2,3},{3,2},{4,5},{5,4},{6,7},{7,6},{8,9},{9,8},{10,11... | collective-permute-start | bytes 786440 | tf_op jit(solution)/shard_map/sibling0_for1/ppermute | solution.py:84
  33.3 6.0 %collective-permute-start.8 = (bf16[2,128,512]{2,1,0:T(8,128)(2,1)S(1)}, bf16[2,128,512]{2,1,0:T(8,128)(2,1)S(1)}, u32[]{:S(2)}, u32[]{:S(2)}) collective-permute-start(bf16[2,128,512]{2,1,0:T(8,128)(2,1)S(1)} %collective-permute-done.6.refs_2_), channel_id=1, source_target_pairs={{0,1},{1,0},{2,3},{3,2},{4,5},{5,4},{6,7},{7,6},{8,9},{9,8},{10,11... | collective-permute-start | bytes 786440 | tf_op jit(solution)/shard_map/sibling1_for1/ppermute | solution.py:84
  33.8 8.0 %collective-permute-start.15 = (bf16[2,128,512]{2,1,0:T(8,128)(2,1)S(1)}, bf16[2,128,512]{2,1,0:T(8,128)(2,1)S(1)}, u32[]{:S(2)}, u32[]{:S(2)}) collective-permute-start(bf16[2,128,512]{2,1,0:T(8,128)(2,1)S(1)} %attend.2.refs_0_), channel_id=1, source_target_pairs={{0,1},{1,0},{2,3},{3,2},{4,5},{5,4},{6,7},{7,6},{8,9},{9,8},{10,11... | collective-permute-start | bytes 786440 | tf_op jit(solution)/shard_map/sibling0_for0/ppermute | solution.py:84
  38.5 3.3 %collective-permute-start.17 = (bf16[2,128,512]{2,1,0:T(8,128)(2,1)S(1)}, bf16[2,128,512]{2,1,0:T(8,128)(2,1)S(1)}, u32[]{:S(2)}, u32[]{:S(2)}) collective-permute-start(bf16[2,128,512]{2,1,0:T(8,128)(2,1)S(1)} %collective-permute-done.16.refs_2_), channel_id=1, source_target_pairs={{0,1},{1,0},{2,3},{3,2},{4,5},{5,4},{6,7},{7,6},{8,9},{9,8},{10,11... | collective-permute-start | bytes 786440 | tf_op jit(solution)/shard_map/sibling1_for0/ppermute | solution.py:84
  40.6 6.3 %collective-permute-start.19 = (bf16[128,512]{1,0:T(8,128)(2,1)S(1)}, bf16[128,512]{1,0:T(8,128)(2,1)S(1)}, u32[]{:S(2)}, u32[]{:S(2)}) collective-permute-start(bf16[128,512]{1,0:T(8,128)(2,1)S(1)} %get-tuple-element.36), channel_id=1, source_target_pairs={{0,2},{1,3},{2,0},{3,1},{4,6},{5,7},{6,4},{7,5},{8,10},{9,11},{10,... | collective-permute-start | bytes 393224 | tf_op jit(solution)/shard_map/out1_same/ppermute | solution.py:84
  41.6 2.6 %copy-start.1 = (f32[1,256,512]{2,1,0:T(8,128)S(1)}, f32[1,256,512]{2,1,0:T(8,128)}, u32[]{:S(2)}) copy-start(f32[1,256,512]{2,1,0:T(8,128)} %param.13) | copy-start | bytes 1572868
  41.6 2.6 %copy-start.2 = (f32[1,256,512]{2,1,0:T(8,128)S(1)}, f32[1,256,512]{2,1,0:T(8,128)}, u32[]{:S(2)}) copy-start(f32[1,256,512]{2,1,0:T(8,128)} %param.14) | copy-start | bytes 1572868
  41.6 2.6 %copy-start.3 = (f32[1,256,512]{2,1,0:T(8,128)S(1)}, f32[1,256,512]{2,1,0:T(8,128)}, u32[]{:S(2)}) copy-start(f32[1,256,512]{2,1,0:T(8,128)} %param.15) | copy-start | bytes 1572868
  41.6 2.6 %copy-start.4 = (f32[1,256,512]{2,1,0:T(8,128)S(1)}, f32[1,256,512]{2,1,0:T(8,128)}, u32[]{:S(2)}) copy-start(f32[1,256,512]{2,1,0:T(8,128)} %param.16) | copy-start | bytes 1572868
  41.6 5.9 %collective-permute-start.20 = (bf16[128,512]{1,0:T(8,128)(2,1)S(1)}, bf16[128,512]{1,0:T(8,128)(2,1)S(1)}, u32[]{:S(2)}, u32[]{:S(2)}) collective-permute-start(bf16[128,512]{1,0:T(8,128)(2,1)S(1)} %get-tuple-element.42), channel_id=1, source_target_pairs={{0,3},{1,2},{2,1},{3,0},{4,7},{5,6},{6,5},{7,4},{8,11},{9,10},{10,... | collective-permute-start | bytes 393224 | tf_op jit(solution)/shard_map/out1_cross/ppermute | solution.py:84
  43.1 4.4 %collective-permute-start.18 = (bf16[128,512]{1,0:T(8,128)(2,1)S(1)}, bf16[128,512]{1,0:T(8,128)(2,1)S(1)}, u32[]{:S(2)}, u32[]{:S(2)}) collective-permute-start(bf16[128,512]{1,0:T(8,128)(2,1)S(1)} %get-tuple-element.41), channel_id=1, source_target_pairs={{0,1},{1,0},{2,3},{3,2},{4,5},{5,4},{6,7},{7,6},{8,9},{9,8},{10,11... | collective-permute-start | bytes 393224 | tf_op jit(solution)/shard_map/out_sibling/ppermute | solution.py:84

commit v5 on v4

--- a/solution.py
+++ b/solution.py
@@ -36,15 +36,16 @@
 FIRST = {
     "half": ["cut"],
     "queries1_same": ["pairs1_same"],
-    "queries1_cross": ["pairs1_same", "sibling", "pairs1_cross"],
-    "attend0": ["swap_own"],
-    "attend1": ["attend0", "ahead3"],
+    "queries1_cross": ["pairs1_same", "pairs1_cross"],
+    "attend0": ["swap_own", "back1"],
+    "attend1": ["attend0", "back1", "swap_ahead1"],
     "attended1_to1": ["swap_ahead1"],
     "sibling0_for1": ["attended0_to1"],
-    "sibling1_for1": ["swap_ahead3"],
+    "sibling1_for1": ["swap_back1"],
     "sibling0_for0": ["attended0_to1"],
     "project0": ["project1"],
     "states": ["attended0_to1"],
+    "sibling": ["half"],
 }
 
 SMALL = pltpu.CompilerParams(vmem_limit_bytes=16 * 1024 * 1024)
@@ -92,26 +93,19 @@
 
 
 def half(master_weight, first_moment, second_moment, gradient):
-    depth, columns = master_weight.shape
-    rows = depth // HALF_STEPS
-    spec = pl.BlockSpec((rows, columns), lambda i: (i, 0))
     return pl.pallas_call(
         half_kernel,
-        grid=(HALF_STEPS,),
-        out_shape=jax.ShapeDtypeStruct((depth, columns), jnp.bfloat16),
-        in_specs=[spec] * 4,
-        out_specs=spec,
+        out_shape=jax.ShapeDtypeStruct(master_weight.shape, jnp.bfloat16),
+        in_specs=[IN_VMEM] * 4,
+        out_specs=IN_VMEM,
         compiler_params=SMALL,
         cost_estimate=estimate(1),
         name="half",
-    )(*[
-        pltpu.with_memory_space_constraint(array, pltpu.HBM)
-        for array in (master_weight, first_moment, second_moment, gradient)
-    ])
-
-
-def cut_kernel(query, key, value, *refs):
-    blocks, sems = refs[:-1], refs[-1]
+    )(master_weight, first_moment, second_moment, gradient)
+
+
+def cut_kernel(query, key, value, extra, *refs):
+    blocks, brought, sems = refs[:-2], refs[-2], refs[-1]
     chips = (len(blocks) - 2) // 4 + 1
     wide = blocks[0].shape[-1]
     chip, core = chip_and_core()
@@ -132,6 +126,7 @@
     for step in range(1, chips):
         for crossed in range(2):
             copy(query, step, crossed, blocks[4 * step + crossed].at[0])
+    copies.append(pltpu.make_async_copy(extra, brought, sems.at[len(copies)]))
     for one in copies:
         one.start()
     for one in copies:
@@ -146,10 +141,11 @@
         cut_kernel,
         out_shape=[
             jax.ShapeDtypeStruct((n, rows, width // groups), jnp.bfloat16) for n in counts
-        ],
-        in_specs=[pl.BlockSpec(memory_space=pl.ANY)] * 3,
-        out_specs=[IN_VMEM] * len(counts),
-        scratch_shapes=[pltpu.SemaphoreType.DMA((3 * groups,))],
+        ]
+        + [jax.ShapeDtypeStruct(arrays[3].shape, arrays[3].dtype)],
+        in_specs=[pl.BlockSpec(memory_space=pl.ANY)] * 4,
+        out_specs=[IN_VMEM] * (len(counts) + 1),
+        scratch_shapes=[pltpu.SemaphoreType.DMA((3 * groups + 1,))],
         compiler_params=SMALL,
         cost_estimate=estimate(1),
         name="cut",
@@ -323,11 +319,11 @@
     def to_sibling(name, array):
         return seen.permute(name, array, "seq", [(s, s ^ 1) for s in range(groups)])
 
-    own, other, *rest = cut(queries[0], hit_keys[0], hit_values[0])
+    own, other, *rest, grad = cut(queries[0], hit_keys[0], hit_values[0], gradient[0])
     seen.add("cut", own)
     master = seen.after("half", master_weight[0])
-    rounded = seen.add("half", half(master, first_moment[0], second_moment[0], gradient[0]))
-    pairs = [own, to_sibling("sibling", other)]
+    rounded = seen.add("half", half(master, first_moment[0], second_moment[0], grad))
+    pairs = []
     for step in range(1, chips):
         same, cross = rest[4 * step - 4 : 4 * step - 4 + 2]
         pairs += [
@@ -335,6 +331,7 @@
             to_cross(f"pairs{step}_cross", cross, step),
         ]
     steps, weights = gather_weights(seen, rounded)
+    pairs = [own, to_sibling("sibling", other)] + pairs
     asked = [()]
     for step in range(1, chips):
         for_same, for_cross = rest[4 * step - 2 : 4 * step]

time: 49 us -> 48.3 us (0.986); the launches traced: 48.3 us -> 48.1 us
  waiting for transfers between devices: 11.7 us -> 13.6 us
  starting transfers between devices: 22.5 us -> 21.4 us
  Pallas kernels: 11.2 us -> 10.2 us
    ppermute x21, waiting for transfers between devices: 11.7 us -> 13.6 us  [permute(): return self.add(name, lax.ppermute(array, axis, perm))]
    pallas_call x1, Pallas kernels: 1.73 us -> 0.42 us  [half(): pl.pallas_call(half_kernel, out_shape=jax.ShapeDtypeStruct(master_weight....]
    ppermute x21, starting transfers between devices: 22.5 us -> 21.4 us  [permute(): return self.add(name, lax.ppermute(array, axis, perm))]
  transfers between devices with their start and end apart: 21 -> 21, of which waited for: 8 -> 9; matrix products, arithmetic and copies ran while one was open for 3% -> 3% of each run, Pallas kernels for 18% -> 16%
where the time goes in v5:
time: 48.3 us; the launch traced here: 48.1 us
  starting transfers between devices  21.4 us (44%)
  waiting for transfers between devices  13.6 us (28%)
  Pallas kernels  10.2 us (21%)
  other arithmetic  1.43 us (3%)
  between operations  1.39 us (3%)
    ppermute x21, starting transfers between devices, permute(): return self.add(name, lax.ppermute(array, axis, perm))  21.4 us
    ppermute x21, waiting for transfers between devices, permute(): return self.add(name, lax.ppermute(array, axis, perm))  13.6 us
    pallas_call x2, Pallas kernels, attend(): pl.pallas_call(functools.partial(attend_kernel, n_pairs, picks), out_shap...  4.52 us
    pallas_call x2, Pallas kernels, project(): pl.pallas_call(functools.partial(project_kernel, len(att), steps), out_sh...  2.59 us
    pallas_call x1, Pallas kernels, cut(): pl.pallas_call(cut_kernel, out_shape=[jax.ShapeDtypeStruct((n, rows, widt...  1.86 us
    sub x1, other arithmetic, adam_update(): master_weight - learn_rate * (first_hat / (jnp.sqrt(second_hat) + epsilon...  1.43 us
  transfers between devices with their start and end apart: 21, of which 9 were waited for; matrix products, arithmetic and copies ran while one was open for 3% of the time, Pallas kernels for 16%

profile of v5, /device:TPU:0, one launch (start us, length us, event | category | flops | bytes accessed | tf_op | source)
XLA Modules:
  0.0 48.1 jit_solution(12680836337709755033)
XLA Ops:
  0.7 1.9 %cut.1 = (bf16[3,128,512]{2,1,0:T(8,128)(2,1)S(1)}, bf16[3,128,512]{2,1,0:T(8,128)(2,1)S(1)}, bf16[2,128,512]{2,1,0:T(8,128)(2,1)S(1)}, bf16[2,128,512]{2,1,0:T(...) custom-call(bf16[128,2048]{1,0:T(8,128)(2,1)} %bitcast.13, ...), custom_call_target="tpu_custom_call" | custom-call | bytes 3690000 | tf_op jit(solution)/shard_map/cut/pallas_call | solution.py:140
  2.5 3.0 %collective-permute-start.3 = (bf16[2,128,512]{2,1,0:T(8,128)(2,1)S(1)}, bf16[2,128,512]{2,1,0:T(8,128)(2,1)S(1)}, u32[]{:S(2)}, u32[]{:S(2)}) collective-permute-start(bf16[2,128,512]{2,1,0:T(8,128)(2,1)S(1)} %get-tuple-element.33), channel_id=1, source_target_pairs={{0,2},{1,3},{2,0},{3,1},{4,6},{5,7},{6,4},{7,5},{8,10},{9,11},{10,... | collective-permute-start | bytes 786440 | tf_op jit(solution)/shard_map/pairs1_same/ppermute | solution.py:85
  5.6 0.4 half.1.refs_4_
  6.0 1.6 %collective-permute-start.6 = (bf16[256,512]{1,0:T(8,128)(2,1)S(1)}, bf16[256,512]{1,0:T(8,128)(2,1)S(1)}, u32[]{:S(2)}, u32[]{:S(2)}) collective-permute-start(bf16[256,512]{1,0:T(8,128)(2,1)S(1)} %half.1.refs_4_), channel_id=1, source_target_pairs={{0,8},{4,12},{8,16},{12,20},{16,24},{20,28},{24,0},{28,4},{1,9},{5... | collective-permute-start | bytes 786440 | tf_op jit(solution)/shard_map/ahead1/ppermute | solution.py:85
  7.6 0.6 %collective-permute-start.4 = (bf16[2,128,512]{2,1,0:T(8,128)(2,1)S(1)}, bf16[2,128,512]{2,1,0:T(8,128)(2,1)S(1)}, u32[]{:S(2)}, u32[]{:S(2)}) collective-permute-start(bf16[2,128,512]{2,1,0:T(8,128)(2,1)S(1)} %get-tuple-element.34), channel_id=1, source_target_pairs={{0,3},{1,2},{2,1},{3,0},{4,7},{5,6},{6,5},{7,4},{8,11},{9,10},{10,... | collective-permute-start | bytes 786440 | tf_op jit(solution)/shard_map/pairs1_cross/ppermute | solution.py:85
  8.2 1.5 %collective-permute-start = (bf16[256,512]{1,0:T(8,128)(2,1)S(1)}, bf16[256,512]{1,0:T(8,128)(2,1)S(1)}, u32[]{:S(2)}, u32[]{:S(2)}) collective-permute-start(bf16[256,512]{1,0:T(8,128)(2,1)S(1)} %half.1.refs_4_), channel_id=1, source_target_pairs={{0,4},{4,0},{8,12},{12,8},{16,20},{20,16},{24,28},{28,24},{1,5},{5... | collective-permute-start | bytes 786440 | tf_op jit(solution)/shard_map/swap_own/ppermute | solution.py:85
  9.7 3.0 %collective-permute-done.3.refs_2_ = bf16[2,128,512]{2,1,0:T(8,128)(2,1)S(1)} collective-permute-done((bf16[2,128,512]{2,1,0:T(8,128)(2,1)S(1)}, bf16[2,128,512]{2,1,0:T(8,128)(2,1)S(1)}, u32[]{:S(2)}, u32[]{:S(2)}) %collective-permute-start.3) | collective-permute-done | bytes 262176 | tf_op jit(solution)/shard_map/pairs1_same/ppermute | solution.py:85
  12.7 4.1 %collective-permute-start.1 = (bf16[256,512]{1,0:T(8,128)(2,1)S(1)}, bf16[256,512]{1,0:T(8,128)(2,1)S(1)}, u32[]{:S(2)}, u32[]{:S(2)}) collective-permute-start(bf16[256,512]{1,0:T(8,128)(2,1)S(1)} %half.1.refs_4_), channel_id=1, source_target_pairs={{0,24},{4,28},{8,0},{12,4},{16,8},{20,12},{24,16},{28,20},{1,25},{... | collective-permute-start | bytes 786440 | tf_op jit(solution)/shard_map/back1/ppermute | solution.py:85
  16.8 1.5 %collective-permute-start.7 = (bf16[256,512]{1,0:T(8,128)(2,1)S(1)}, bf16[256,512]{1,0:T(8,128)(2,1)S(1)}, u32[]{:S(2)}, u32[]{:S(2)}) collective-permute-start(bf16[256,512]{1,0:T(8,128)(2,1)S(1)} %collective-permute-done.6.refs_6_), channel_id=1, source_target_pairs={{0,4},{4,0},{8,12},{12,8},{16,20},{20,16},{24,28},{28,24},{1,5},{5... | collective-permute-start | bytes 786440 | tf_op jit(solution)/shard_map/swap_ahead1/ppermute | solution.py:85
  18.3 1.5 %collective-permute-start.5 = (bf16[1,128,512]{2,1,0:T(8,128)(2,1)S(1)}, bf16[1,128,512]{2,1,0:T(8,128)(2,1)S(1)}, u32[]{:S(2)}, u32[]{:S(2)}) collective-permute-start(bf16[1,128,512]{2,1,0:T(8,128)(2,1)S(1)} %get-tuple-element.36), channel_id=1, source_target_pairs={{0,2},{1,3},{2,0},{3,1},{4,6},{5,7},{6,4},{7,5},{8,10},{9,11},{10,... | collective-permute-start | bytes 393224 | tf_op jit(solution)/shard_map/queries1_same/ppermute | solution.py:85
  20.5 0.8 %collective-permute-done.1.refs_8_ = bf16[256,512]{1,0:T(8,128)(2,1)S(1)} collective-permute-done((bf16[256,512]{1,0:T(8,128)(2,1)S(1)}, bf16[256,512]{1,0:T(8,128)(2,1)S(1)}, u32[]{:S(2)}, u32[]{:S(2)}) %collective-permute-start.1) | collective-permute-done | bytes 262176 | tf_op jit(solution)/shard_map/back1/ppermute | solution.py:85
  21.3 0.6 %collective-permute-start.13 = (bf16[256,512]{1,0:T(8,128)(2,1)S(1)}, bf16[256,512]{1,0:T(8,128)(2,1)S(1)}, u32[]{:S(2)}, u32[]{:S(2)}) collective-permute-start(bf16[256,512]{1,0:T(8,128)(2,1)S(1)} %collective-permute-done.6.refs_6_), channel_id=1, source_target_pairs={{0,8},{4,12},{8,16},{12,20},{16,24},{20,28},{24,0},{28,4},{1,9},{5... | collective-permute-start | bytes 786440 | tf_op jit(solution)/shard_map/ahead2/ppermute | solution.py:85
  21.9 2.3 %attend.2.refs_0_ = bf16[2,128,512]{2,1,0:T(8,128)(2,1)S(1)} custom-call(s32[1]{0:T(128)S(6)} %copy.13.count_ref, bf16[3,128,512]{2,1,0:T(8,128)(2,1)S(1)} %get-tuple-element.30.refs_0_, bf16[3,128,512]{2,1,0:T(8,128)(2,1)S(1)} %collective-permute-done.2.refs_1_, bf16[2,128,512]{2,1,0:T(8,128)(2,1)S(1)} %collective-permute-done.3.refs_2_, ...), custom_call_target="tpu_custom_call" | custom-call | bytes 11070000 | tf_op jit(solution)/shard_map/attend/pallas_call | solution.py:192
  24.1 1.2 %collective-permute-start.9 = (bf16[2,128,512]{2,1,0:T(8,128)(2,1)S(1)}, bf16[2,128,512]{2,1,0:T(8,128)(2,1)S(1)}, u32[]{:S(2)}, u32[]{:S(2)}) collective-permute-start(bf16[2,128,512]{2,1,0:T(8,128)(2,1)S(1)} %attend.2.refs_0_), channel_id=1, source_target_pairs={{0,2},{1,3},{2,0},{3,1},{4,6},{5,7},{6,4},{7,5},{8,10},{9,11},{10,... | collective-permute-start | bytes 786440 | tf_op jit(solution)/shard_map/attended0_to1/ppermute | solution.py:85
  25.4 1.5 %collective-permute-start.11 = (bf16[256,512]{1,0:T(8,128)(2,1)S(1)}, bf16[256,512]{1,0:T(8,128)(2,1)S(1)}, u32[]{:S(2)}, u32[]{:S(2)}) collective-permute-start(bf16[256,512]{1,0:T(8,128)(2,1)S(1)} %collective-permute-done.1.refs_8_), channel_id=1, source_target_pairs={{0,4},{4,0},{8,12},{12,8},{16,20},{20,16},{24,28},{28,24},{1,5},{5... | collective-permute-start | bytes 786440 | tf_op jit(solution)/shard_map/swap_back1/ppermute | solution.py:85
  26.9 2.3 %attend.3.refs_0_ = bf16[2,128,512]{2,1,0:T(8,128)(2,1)S(1)} custom-call(s32[1]{0:T(128)S(6)} %copy.13.count_ref, bf16[3,128,512]{2,1,0:T(8,128)(2,1)S(1)} %get-tuple-element.30.refs_0_, bf16[3,128,512]{2,1,0:T(8,128)(2,1)S(1)} %collective-permute-done.2.refs_1_, bf16[2,128,512]{2,1,0:T(8,128)(2,1)S(1)} %collective-permute-done.3.refs_2_, ...), custom_call_target="tpu_custom_call" | custom-call | bytes 11070000 | tf_op jit(solution)/shard_map/attend/pallas_call | solution.py:192
  29.1 0.9 %collective-permute-start.16 = (bf16[2,128,512]{2,1,0:T(8,128)(2,1)S(1)}, bf16[2,128,512]{2,1,0:T(8,128)(2,1)S(1)}, u32[]{:S(2)}, u32[]{:S(2)}) collective-permute-start(bf16[2,128,512]{2,1,0:T(8,128)(2,1)S(1)} %attend.3.refs_0_), channel_id=1, source_target_pairs={{0,2},{1,3},{2,0},{3,1},{4,6},{5,7},{6,4},{7,5},{8,10},{9,11},{10,... | collective-permute-start | bytes 786440 | tf_op jit(solution)/shard_map/attended1_to1/ppermute | solution.py:85
  30.1 1.1 %collective-permute-done.13.refs_10_ = bf16[256,512]{1,0:T(8,128)(2,1)S(1)} collective-permute-done((bf16[256,512]{1,0:T(8,128)(2,1)S(1)}, bf16[256,512]{1,0:T(8,128)(2,1)S(1)}, u32[]{:S(2)}, u32[]{:S(2)}) %collective-permute-start.13) | collective-permute-done | bytes 262176 | tf_op jit(solution)/shard_map/ahead2/ppermute | solution.py:85
  31.2 0.5 %collective-permute-start.14 = (bf16[256,512]{1,0:T(8,128)(2,1)S(1)}, bf16[256,512]{1,0:T(8,128)(2,1)S(1)}, u32[]{:S(2)}, u32[]{:S(2)}) collective-permute-start(bf16[256,512]{1,0:T(8,128)(2,1)S(1)} %collective-permute-done.13.refs_10_), channel_id=1, source_target_pairs={{0,4},{4,0},{8,12},{12,8},{16,20},{20,16},{24,28},{28,24},{1,5},{5... | collective-permute-start | bytes 786440 | tf_op jit(solution)/shard_map/swap_ahead2/ppermute | solution.py:85
  31.7 0.9 %collective-permute-done.9.refs_2_ = bf16[2,128,512]{2,1,0:T(8,128)(2,1)S(1)} collective-permute-done((bf16[2,128,512]{2,1,0:T(8,128)(2,1)S(1)}, bf16[2,128,512]{2,1,0:T(8,128)(2,1)S(1)}, u32[]{:S(2)}, u32[]{:S(2)}) %collective-permute-start.9) | collective-permute-done | bytes 262176 | tf_op jit(solution)/shard_map/attended0_to1/ppermute | solution.py:85
  32.6 0.5 %collective-permute-done.11.refs_9_ = bf16[256,512]{1,0:T(8,128)(2,1)S(1)} collective-permute-done((bf16[256,512]{1,0:T(8,128)(2,1)S(1)}, bf16[256,512]{1,0:T(8,128)(2,1)S(1)}, u32[]{:S(2)}, u32[]{:S(2)}) %collective-permute-start.11) | collective-permute-done | bytes 262176 | tf_op jit(solution)/shard_map/swap_back1/ppermute | solution.py:85
  33.1 0.5 %collective-permute-start.15 = (bf16[2,128,512]{2,1,0:T(8,128)(2,1)S(1)}, bf16[2,128,512]{2,1,0:T(8,128)(2,1)S(1)}, u32[]{:S(2)}, u32[]{:S(2)}) collective-permute-start(bf16[2,128,512]{2,1,0:T(8,128)(2,1)S(1)} %attend.2.refs_0_), channel_id=1, source_target_pairs={{0,1},{1,0},{2,3},{3,2},{4,5},{5,4},{6,7},{7,6},{8,9},{9,8},{10,11... | collective-permute-start | bytes 786440 | tf_op jit(solution)/shard_map/sibling0_for0/ppermute | solution.py:85
  33.6 3.8 %collective-permute-done.16.refs_2_ = bf16[2,128,512]{2,1,0:T(8,128)(2,1)S(1)} collective-permute-done((bf16[2,128,512]{2,1,0:T(8,128)(2,1)S(1)}, bf16[2,128,512]{2,1,0:T(8,128)(2,1)S(1)}, u32[]{:S(2)}, u32[]{:S(2)}) %collective-permute-start.16) | collective-permute-done | bytes 262176 | tf_op jit(solution)/shard_map/attended1_to1/ppermute | solution.py:85
  37.4 1.2 %collective-permute-done.14.refs_11_ = bf16[256,512]{1,0:T(8,128)(2,1)S(1)} collective-permute-done((bf16[256,512]{1,0:T(8,128)(2,1)S(1)}, bf16[256,512]{1,0:T(8,128)(2,1)S(1)}, u32[]{:S(2)}, u32[]{:S(2)}) %collective-permute-start.14) | collective-permute-done | bytes 262176 | tf_op jit(solution)/shard_map/swap_ahead2/ppermute | solution.py:85
  38.6 1.3 %project.2 = (bf16[128,512]{1,0:T(8,128)(2,1)S(1)}, bf16[128,512]{1,0:T(8,128)(2,1)S(1)}) custom-call(s32[8]{0:T(128)S(1)} %copy-done.3, bf16[2,128,512]{2,1,0:T(8,128)(2,1)S(1)} %attend.3.refs_0_, bf16[2,128,512]{2,1,0:T(8,128)(2,1)S(1)} %collective-permute-done.10.refs_1_, bf16[2,128,512]{2,1,0:T(8,128)(2,1)S(1)} %collective-permute-done.9.refs_2_, ...), custom_call_target="tpu_custom_call" | custom-call | bytes 7380000 | tf_op jit(solution)/shard_map/project/pallas_call | solution.py:239
  40.0 1.5 %collective-permute-start.19 = (bf16[128,512]{1,0:T(8,128)(2,1)S(1)}, bf16[128,512]{1,0:T(8,128)(2,1)S(1)}, u32[]{:S(2)}, u32[]{:S(2)}) collective-permute-start(bf16[128,512]{1,0:T(8,128)(2,1)S(1)} %get-tuple-element.42), channel_id=1, source_target_pairs={{0,2},{1,3},{2,0},{3,1},{4,6},{5,7},{6,4},{7,5},{8,10},{9,11},{10,... | collective-permute-start | bytes 393224 | tf_op jit(solution)/shard_map/out1_same/ppermute | solution.py:85
  41.5 1.3 %project.3 = (bf16[128,512]{1,0:T(8,128)(2,1)S(1)}, bf16[128,512]{1,0:T(8,128)(2,1)S(1)}) custom-call(s32[8]{0:T(128)S(1)} %copy-done.3, bf16[2,128,512]{2,1,0:T(8,128)(2,1)S(1)} %attend.2.refs_0_, bf16[2,128,512]{2,1,0:T(8,128)(2,1)S(1)} %collective-permute-done.15.refs_1_, bf16[2,128,512]{2,1,0:T(8,128)(2,1)S(1)} %collective-permute-done.16.refs_2_, ...), custom_call_target="tpu_custom_call" | custom-call | bytes 7380000 | tf_op jit(solution)/shard_map/project/pallas_call | solution.py:239
  42.8 0.7 %collective-permute-start.18 = (bf16[128,512]{1,0:T(8,128)(2,1)S(1)}, bf16[128,512]{1,0:T(8,128)(2,1)S(1)}, u32[]{:S(2)}, u32[]{:S(2)}) collective-permute-start(bf16[128,512]{1,0:T(8,128)(2,1)S(1)} %get-tuple-element.47), channel_id=1, source_target_pairs={{0,1},{1,0},{2,3},{3,2},{4,5},{5,4},{6,7},{7,6},{8,9},{9,8},{10,11... | collective-permute-start | bytes 393224 | tf_op jit(solution)/shard_map/out_sibling/ppermute | solution.py:85
  43.5 1.4 %multiply_subtract_fusion = (f32[1,256,512]{2,1,0:T(8,128)}, f32[1,256,512]{2,1,0:T(8,128)}, f32[1,256,512]{2,1,0:T(8,128)}) fusion(f32[1,256,512]{2,1,0:T(8,128)S(1)} %copy-done, f32[1,256,512]{2,1,0:T(8,128)S(1)} %copy-done.4, f32[1,256,512]{2,1,0:T(8,128)S(1)} %copy-done.1, f32[1,256,512]{2,1,0:T(8,128)S(1)} %copy-done.2), kind=kLoop, calls=%fused_computation.2 | loop fusion | flops 1966080 | bytes 3670016 | tf_op jit(solution)/shard_map/sub | solution.py:26
  45.0 0.5 %collective-permute-done.19.refs_2_ = bf16[128,512]{1,0:T(8,128)(2,1)S(1)} collective-permute-done((bf16[128,512]{1,0:T(8,128)(2,1)S(1)}, bf16[128,512]{1,0:T(8,128)(2,1)S(1)}, u32[]{:S(2)}, u32[]{:S(2)}) %collective-permute-start.19) | collective-permute-done | bytes 131104 | tf_op jit(solution)/shard_map/out1_same/ppermute | solution.py:85
  45.5 1.7 %collective-permute-done.20.refs_3_ = bf16[128,512]{1,0:T(8,128)(2,1)S(1)} collective-permute-done((bf16[128,512]{1,0:T(8,128)(2,1)S(1)}, bf16[128,512]{1,0:T(8,128)(2,1)S(1)}, u32[]{:S(2)}, u32[]{:S(2)}) %collective-permute-start.20) | collective-permute-done | bytes 131104 | tf_op jit(solution)/shard_map/out1_cross/ppermute | solution.py:85
  47.3 0.8 %place.1 = bf16[128,2048]{1,0:T(8,128)(2,1)} custom-call(bf16[128,512]{1,0:T(8,128)(2,1)S(1)} %get-tuple-element.46.refs_0_, bf16[128,512]{1,0:T(8,128)(2,1)S(1)} %collective-permute-done.18.refs_1_, bf16[128,512]{1,0:T(8,128)(2,1)S(1)} %collective-permute-done.19.refs_2_, bf16[128,512]{1,0:T(8,128)(2,1)S(1)} %collective-permute-done.20.refs_3_), custom_call_target="tpu_custom_call" | custom-call | bytes 3690000 | tf_op jit(solution)/shard_map/place/pallas_call | solution.py:262
  (28 shorter events, 0.1 us)
Async XLA Ops:
  0.6 4.9 %copy-start = (f32[1,256,512]{2,1,0:T(8,128)S(1)}, f32[1,256,512]{2,1,0:T(8,128)}, u32[]{:S(2)}) copy-start(f32[1,256,512]{2,1,0:T(8,128)} %param.13) | copy-start | bytes 1572868
  0.6 4.9 %copy-start.1 = (f32[1,256,512]{2,1,0:T(8,128)S(1)}, f32[1,256,512]{2,1,0:T(8,128)}, u32[]{:S(2)}) copy-start(f32[1,256,512]{2,1,0:T(8,128)} %param.14) | copy-start | bytes 1572868
  0.7 4.9 %copy-start.2 = (f32[1,256,512]{2,1,0:T(8,128)S(1)}, f32[1,256,512]{2,1,0:T(8,128)}, u32[]{:S(2)}) copy-start(f32[1,256,512]{2,1,0:T(8,128)} %param.15) | copy-start | bytes 1572868
  2.5 10.2 %collective-permute-start.3 = (bf16[2,128,512]{2,1,0:T(8,128)(2,1)S(1)}, bf16[2,128,512]{2,1,0:T(8,128)(2,1)S(1)}, u32[]{:S(2)}, u32[]{:S(2)}) collective-permute-start(bf16[2,128,512]{2,1,0:T(8,128)(2,1)S(1)} %get-tuple-element.33), channel_id=1, source_target_pairs={{0,2},{1,3},{2,0},{3,1},{4,6},{5,7},{6,4},{7,5},{8,10},{9,11},{10,... | collective-permute-start | bytes 786440 | tf_op jit(solution)/shard_map/pairs1_same/ppermute | solution.py:85
  6.0 10.8 %collective-permute-start.6 = (bf16[256,512]{1,0:T(8,128)(2,1)S(1)}, bf16[256,512]{1,0:T(8,128)(2,1)S(1)}, u32[]{:S(2)}, u32[]{:S(2)}) collective-permute-start(bf16[256,512]{1,0:T(8,128)(2,1)S(1)} %half.1.refs_4_), channel_id=1, source_target_pairs={{0,8},{4,12},{8,16},{12,20},{16,24},{20,28},{24,0},{28,4},{1,9},{5... | collective-permute-start | bytes 786440 | tf_op jit(solution)/shard_map/ahead1/ppermute | solution.py:85
  7.6 14.2 %collective-permute-start.2 = (bf16[3,128,512]{2,1,0:T(8,128)(2,1)S(1)}, bf16[3,128,512]{2,1,0:T(8,128)(2,1)S(1)}, u32[]{:S(2)}, u32[]{:S(2)}) collective-permute-start(bf16[3,128,512]{2,1,0:T(8,128)(2,1)S(1)} %get-tuple-element.32), channel_id=1, source_target_pairs={{0,1},{1,0},{2,3},{3,2},{4,5},{5,4},{6,7},{7,6},{8,9},{9,8},{10,11... | collective-permute-start | bytes 1179656 | tf_op jit(solution)/shard_map/sibling/ppermute | solution.py:85
  7.6 10.7 %collective-permute-start.4 = (bf16[2,128,512]{2,1,0:T(8,128)(2,1)S(1)}, bf16[2,128,512]{2,1,0:T(8,128)(2,1)S(1)}, u32[]{:S(2)}, u32[]{:S(2)}) collective-permute-start(bf16[2,128,512]{2,1,0:T(8,128)(2,1)S(1)} %get-tuple-element.34), channel_id=1, source_target_pairs={{0,3},{1,2},{2,1},{3,0},{4,7},{5,6},{6,5},{7,4},{8,11},{9,10},{10,... | collective-permute-start | bytes 786440 | tf_op jit(solution)/shard_map/pairs1_cross/ppermute | solution.py:85
  8.2 11.6 %collective-permute-start = (bf16[256,512]{1,0:T(8,128)(2,1)S(1)}, bf16[256,512]{1,0:T(8,128)(2,1)S(1)}, u32[]{:S(2)}, u32[]{:S(2)}) collective-permute-start(bf16[256,512]{1,0:T(8,128)(2,1)S(1)} %half.1.refs_4_), channel_id=1, source_target_pairs={{0,4},{4,0},{8,12},{12,8},{16,20},{20,16},{24,28},{28,24},{1,5},{5... | collective-permute-start | bytes 786440 | tf_op jit(solution)/shard_map/swap_own/ppermute | solution.py:85
  12.7 8.6 %collective-permute-start.1 = (bf16[256,512]{1,0:T(8,128)(2,1)S(1)}, bf16[256,512]{1,0:T(8,128)(2,1)S(1)}, u32[]{:S(2)}, u32[]{:S(2)}) collective-permute-start(bf16[256,512]{1,0:T(8,128)(2,1)S(1)} %half.1.refs_4_), channel_id=1, source_target_pairs={{0,24},{4,28},{8,0},{12,4},{16,8},{20,12},{24,16},{28,20},{1,25},{... | collective-permute-start | bytes 786440 | tf_op jit(solution)/shard_map/back1/ppermute | solution.py:85
  16.8 10.0 %collective-permute-start.7 = (bf16[256,512]{1,0:T(8,128)(2,1)S(1)}, bf16[256,512]{1,0:T(8,128)(2,1)S(1)}, u32[]{:S(2)}, u32[]{:S(2)}) collective-permute-start(bf16[256,512]{1,0:T(8,128)(2,1)S(1)} %collective-permute-done.6.refs_6_), channel_id=1, source_target_pairs={{0,4},{4,0},{8,12},{12,8},{16,20},{20,16},{24,28},{28,24},{1,5},{5... | collective-permute-start | bytes 786440 | tf_op jit(solution)/shard_map/swap_ahead1/ppermute | solution.py:85
  18.3 7.0 %collective-permute-start.5 = (bf16[1,128,512]{2,1,0:T(8,128)(2,1)S(1)}, bf16[1,128,512]{2,1,0:T(8,128)(2,1)S(1)}, u32[]{:S(2)}, u32[]{:S(2)}) collective-permute-start(bf16[1,128,512]{2,1,0:T(8,128)(2,1)S(1)} %get-tuple-element.36), channel_id=1, source_target_pairs={{0,2},{1,3},{2,0},{3,1},{4,6},{5,7},{6,4},{7,5},{8,10},{9,11},{10,... | collective-permute-start | bytes 393224 | tf_op jit(solution)/shard_map/queries1_same/ppermute | solution.py:85
  19.9 7.0 %collective-permute-start.8 = (bf16[1,128,512]{2,1,0:T(8,128)(2,1)S(1)}, bf16[1,128,512]{2,1,0:T(8,128)(2,1)S(1)}, u32[]{:S(2)}, u32[]{:S(2)}) collective-permute-start(bf16[1,128,512]{2,1,0:T(8,128)(2,1)S(1)} %get-tuple-element.39), channel_id=1, source_target_pairs={{0,3},{1,2},{2,1},{3,0},{4,7},{5,6},{6,5},{7,4},{8,11},{9,10},{10,... | collective-permute-start | bytes 393224 | tf_op jit(solution)/shard_map/queries1_cross/ppermute | solution.py:85
  21.3 9.9 %collective-permute-start.13 = (bf16[256,512]{1,0:T(8,128)(2,1)S(1)}, bf16[256,512]{1,0:T(8,128)(2,1)S(1)}, u32[]{:S(2)}, u32[]{:S(2)}) collective-permute-start(bf16[256,512]{1,0:T(8,128)(2,1)S(1)} %collective-permute-done.6.refs_6_), channel_id=1, source_target_pairs={{0,8},{4,12},{8,16},{12,20},{16,24},{20,28},{24,0},{28,4},{1,9},{5... | collective-permute-start | bytes 786440 | tf_op jit(solution)/shard_map/ahead2/ppermute | solution.py:85
  24.1 14.5 %copy-start.3 = (s32[8]{0:T(128)S(1)}, s32[8]{0:T(128)}, u32[]{:S(2)}) copy-start(s32[8]{0:T(128)} %bucket_ref.3) | copy-start | bytes 100
  24.1 8.5 %collective-permute-start.9 = (bf16[2,128,512]{2,1,0:T(8,128)(2,1)S(1)}, bf16[2,128,512]{2,1,0:T(8,128)(2,1)S(1)}, u32[]{:S(2)}, u32[]{:S(2)}) collective-permute-start(bf16[2,128,512]{2,1,0:T(8,128)(2,1)S(1)} %attend.2.refs_0_), channel_id=1, source_target_pairs={{0,2},{1,3},{2,0},{3,1},{4,6},{5,7},{6,4},{7,5},{8,10},{9,11},{10,... | collective-permute-start | bytes 786440 | tf_op jit(solution)/shard_map/attended0_to1/ppermute | solution.py:85
  25.4 7.8 %collective-permute-start.11 = (bf16[256,512]{1,0:T(8,128)(2,1)S(1)}, bf16[256,512]{1,0:T(8,128)(2,1)S(1)}, u32[]{:S(2)}, u32[]{:S(2)}) collective-permute-start(bf16[256,512]{1,0:T(8,128)(2,1)S(1)} %collective-permute-done.1.refs_8_), channel_id=1, source_target_pairs={{0,4},{4,0},{8,12},{12,8},{16,20},{20,16},{24,28},{28,24},{1,5},{5... | collective-permute-start | bytes 786440 | tf_op jit(solution)/shard_map/swap_back1/ppermute | solution.py:85
  29.1 8.3 %collective-permute-start.16 = (bf16[2,128,512]{2,1,0:T(8,128)(2,1)S(1)}, bf16[2,128,512]{2,1,0:T(8,128)(2,1)S(1)}, u32[]{:S(2)}, u32[]{:S(2)}) collective-permute-start(bf16[2,128,512]{2,1,0:T(8,128)(2,1)S(1)} %attend.3.refs_0_), channel_id=1, source_target_pairs={{0,2},{1,3},{2,0},{3,1},{4,6},{5,7},{6,4},{7,5},{8,10},{9,11},{10,... | collective-permute-start | bytes 786440 | tf_op jit(solution)/shard_map/attended1_to1/ppermute | solution.py:85
  31.2 7.4 %collective-permute-start.14 = (bf16[256,512]{1,0:T(8,128)(2,1)S(1)}, bf16[256,512]{1,0:T(8,128)(2,1)S(1)}, u32[]{:S(2)}, u32[]{:S(2)}) collective-permute-start(bf16[256,512]{1,0:T(8,128)(2,1)S(1)} %collective-permute-done.13.refs_10_), channel_id=1, source_target_pairs={{0,4},{4,0},{8,12},{12,8},{16,20},{20,16},{24,28},{28,24},{1,5},{5... | collective-permute-start | bytes 786440 | tf_op jit(solution)/shard_map/swap_ahead2/ppermute | solution.py:85
  32.6 6.0 %collective-permute-start.10 = (bf16[2,128,512]{2,1,0:T(8,128)(2,1)S(1)}, bf16[2,128,512]{2,1,0:T(8,128)(2,1)S(1)}, u32[]{:S(2)}, u32[]{:S(2)}) collective-permute-start(bf16[2,128,512]{2,1,0:T(8,128)(2,1)S(1)} %attend.3.refs_0_), channel_id=1, source_target_pairs={{0,1},{1,0},{2,3},{3,2},{4,5},{5,4},{6,7},{7,6},{8,9},{9,8},{10,11... | collective-permute-start | bytes 786440 | tf_op jit(solution)/shard_map/sibling0_for1/ppermute | solution.py:85
  33.1 5.5 %collective-permute-start.12 = (bf16[2,128,512]{2,1,0:T(8,128)(2,1)S(1)}, bf16[2,128,512]{2,1,0:T(8,128)(2,1)S(1)}, u32[]{:S(2)}, u32[]{:S(2)}) collective-permute-start(bf16[2,128,512]{2,1,0:T(8,128)(2,1)S(1)} %collective-permute-done.9.refs_2_), channel_id=1, source_target_pairs={{0,1},{1,0},{2,3},{3,2},{4,5},{5,4},{6,7},{7,6},{8,9},{9,8},{10,11... | collective-permute-start | bytes 786440 | tf_op jit(solution)/shard_map/sibling1_for1/ppermute | solution.py:85
  33.1 8.3 %collective-permute-start.15 = (bf16[2,128,512]{2,1,0:T(8,128)(2,1)S(1)}, bf16[2,128,512]{2,1,0:T(8,128)(2,1)S(1)}, u32[]{:S(2)}, u32[]{:S(2)}) collective-permute-start(bf16[2,128,512]{2,1,0:T(8,128)(2,1)S(1)} %attend.2.refs_0_), channel_id=1, source_target_pairs={{0,1},{1,0},{2,3},{3,2},{4,5},{5,4},{6,7},{7,6},{8,9},{9,8},{10,11... | collective-permute-start | bytes 786440 | tf_op jit(solution)/shard_map/sibling0_for0/ppermute | solution.py:85
  37.4 4.1 %collective-permute-start.17 = (bf16[2,128,512]{2,1,0:T(8,128)(2,1)S(1)}, bf16[2,128,512]{2,1,0:T(8,128)(2,1)S(1)}, u32[]{:S(2)}, u32[]{:S(2)}) collective-permute-start(bf16[2,128,512]{2,1,0:T(8,128)(2,1)S(1)} %collective-permute-done.16.refs_2_), channel_id=1, source_target_pairs={{0,1},{1,0},{2,3},{3,2},{4,5},{5,4},{6,7},{7,6},{8,9},{9,8},{10,11... | collective-permute-start | bytes 786440 | tf_op jit(solution)/shard_map/sibling1_for0/ppermute | solution.py:85
  40.0 5.6 %collective-permute-start.19 = (bf16[128,512]{1,0:T(8,128)(2,1)S(1)}, bf16[128,512]{1,0:T(8,128)(2,1)S(1)}, u32[]{:S(2)}, u32[]{:S(2)}) collective-permute-start(bf16[128,512]{1,0:T(8,128)(2,1)S(1)} %get-tuple-element.42), channel_id=1, source_target_pairs={{0,2},{1,3},{2,0},{3,1},{4,6},{5,7},{6,4},{7,5},{8,10},{9,11},{10,... | collective-permute-start | bytes 393224 | tf_op jit(solution)/shard_map/out1_same/ppermute | solution.py:85
  41.5 2.1 %copy-start.4 = (f32[1,256,512]{2,1,0:T(8,128)S(1)}, f32[1,256,512]{2,1,0:T(8,128)}, u32[]{:S(2)}) copy-start(f32[1,256,512]{2,1,0:T(8,128)} %param.16) | copy-start | bytes 1572868
  41.5 5.8 %collective-permute-start.20 = (bf16[128,512]{1,0:T(8,128)(2,1)S(1)}, bf16[128,512]{1,0:T(8,128)(2,1)S(1)}, u32[]{:S(2)}, u32[]{:S(2)}) collective-permute-start(bf16[128,512]{1,0:T(8,128)(2,1)S(1)} %get-tuple-element.48), channel_id=1, source_target_pairs={{0,3},{1,2},{2,1},{3,0},{4,7},{5,6},{6,5},{7,4},{8,11},{9,10},{10,... | collective-permute-start | bytes 393224 | tf_op jit(solution)/shard_map/out1_cross/ppermute | solution.py:85
  42.8 4.5 %collective-permute-start.18 = (bf16[128,512]{1,0:T(8,128)(2,1)S(1)}, bf16[128,512]{1,0:T(8,128)(2,1)S(1)}, u32[]{:S(2)}, u32[]{:S(2)}) collective-permute-start(bf16[128,512]{1,0:T(8,128)(2,1)S(1)} %get-tuple-element.47), channel_id=1, source_target_pairs={{0,1},{1,0},{2,3},{3,2},{4,5},{5,4},{6,7},{7,6},{8,9},{9,8},{10,11... | collective-permute-start | bytes 393224 | tf_op jit(solution)/shard_map/out_sibling/ppermute | solution.py:85

commit v6 on v5

--- a/solution.py
+++ b/solution.py
@@ -249,12 +249,17 @@
 
 
 def place_kernel(n, *refs):
-    out_ref = refs[n]
+    out_ref, sems = refs[n:]
     columns = refs[0].shape[1]
     chip, core = chip_and_core()
+    copies = []
     for i in range(n):
         group = 2 * turned(chip, i // 2, n // 2) + (core if i % 2 == 0 else 1 - core)
-        out_ref[:, pl.ds(pl.multiple_of(group * columns, columns), columns)] = refs[i][...]
+        lanes = pl.ds(pl.multiple_of(group * columns, columns), columns)
+        copies.append(pltpu.make_async_copy(refs[i], out_ref.at[:, lanes], sems.at[i]))
+        copies[-1].start()
+    for copy in copies:
+        copy.wait()
 
 
 def place(blocks):
@@ -263,7 +268,8 @@
         functools.partial(place_kernel, len(blocks)),
         out_shape=jax.ShapeDtypeStruct((rows, columns * len(blocks)), jnp.bfloat16),
         in_specs=[IN_VMEM] * len(blocks),
-        out_specs=IN_VMEM,
+        out_specs=pl.BlockSpec(memory_space=pltpu.HBM),
+        scratch_shapes=[pltpu.SemaphoreType.DMA((len(blocks),))],
         compiler_params=SMALL,
         cost_estimate=estimate(1),
         name="place",

time: 48.3 us -> 48.2 us (level)
  no operation moved by 1% of the time
where the time goes in v6:
time: 48.2 us; the launch traced here: 48.1 us
  starting transfers between devices  21.4 us (44%)
  waiting for transfers between devices  13.6 us (28%)
  Pallas kernels  10.2 us (21%)
  other arithmetic  1.43 us (3%)
  between operations  1.39 us (3%)
    ppermute x21, starting transfers between devices, permute(): return self.add(name, lax.ppermute(array, axis, perm))  21.4 us
    ppermute x21, waiting for transfers between devices, permute(): return self.add(name, lax.ppermute(array, axis, perm))  13.6 us
    pallas_call x2, Pallas kernels, attend(): pl.pallas_call(functools.partial(attend_kernel, n_pairs, picks), out_shap...  4.52 us
    pallas_call x2, Pallas kernels, project(): pl.pallas_call(functools.partial(project_kernel, len(att), steps), out_sh...  2.59 us
    pallas_call x1, Pallas kernels, cut(): pl.pallas_call(cut_kernel, out_shape=[jax.ShapeDtypeStruct((n, rows, widt...  1.86 us
    sub x1, other arithmetic, adam_update(): master_weight - learn_rate * (first_hat / (jnp.sqrt(second_hat) + epsilon...  1.43 us
  transfers between devices with their start and end apart: 21, of which 9 were waited for; matrix products, arithmetic and copies ran while one was open for 3% of the time, Pallas kernels for 16%

profile of v6, /device:TPU:0, one launch (start us, length us, event | category | flops | bytes accessed | tf_op | source)
XLA Modules:
  0.0 48.1 jit_solution(3207796117505939327)
XLA Ops:
  0.7 1.9 %cut.1 = (bf16[3,128,512]{2,1,0:T(8,128)(2,1)S(1)}, bf16[3,128,512]{2,1,0:T(8,128)(2,1)S(1)}, bf16[2,128,512]{2,1,0:T(8,128)(2,1)S(1)}, bf16[2,128,512]{2,1,0:T(...) custom-call(bf16[128,2048]{1,0:T(8,128)(2,1)} %bitcast.13, ...), custom_call_target="tpu_custom_call" | custom-call | bytes 3690000 | tf_op jit(solution)/shard_map/cut/pallas_call | solution.py:140
  2.5 3.0 %collective-permute-start.3 = (bf16[2,128,512]{2,1,0:T(8,128)(2,1)S(1)}, bf16[2,128,512]{2,1,0:T(8,128)(2,1)S(1)}, u32[]{:S(2)}, u32[]{:S(2)}) collective-permute-start(bf16[2,128,512]{2,1,0:T(8,128)(2,1)S(1)} %get-tuple-element.33), channel_id=1, source_target_pairs={{0,2},{1,3},{2,0},{3,1},{4,6},{5,7},{6,4},{7,5},{8,10},{9,11},{10,... | collective-permute-start | bytes 786440 | tf_op jit(solution)/shard_map/pairs1_same/ppermute | solution.py:85
  5.6 0.4 half.1.refs_4_
  6.0 1.6 %collective-permute-start.6 = (bf16[256,512]{1,0:T(8,128)(2,1)S(1)}, bf16[256,512]{1,0:T(8,128)(2,1)S(1)}, u32[]{:S(2)}, u32[]{:S(2)}) collective-permute-start(bf16[256,512]{1,0:T(8,128)(2,1)S(1)} %half.1.refs_4_), channel_id=1, source_target_pairs={{0,8},{4,12},{8,16},{12,20},{16,24},{20,28},{24,0},{28,4},{1,9},{5... | collective-permute-start | bytes 786440 | tf_op jit(solution)/shard_map/ahead1/ppermute | solution.py:85
  7.6 0.6 %collective-permute-start.4 = (bf16[2,128,512]{2,1,0:T(8,128)(2,1)S(1)}, bf16[2,128,512]{2,1,0:T(8,128)(2,1)S(1)}, u32[]{:S(2)}, u32[]{:S(2)}) collective-permute-start(bf16[2,128,512]{2,1,0:T(8,128)(2,1)S(1)} %get-tuple-element.34), channel_id=1, source_target_pairs={{0,3},{1,2},{2,1},{3,0},{4,7},{5,6},{6,5},{7,4},{8,11},{9,10},{10,... | collective-permute-start | bytes 786440 | tf_op jit(solution)/shard_map/pairs1_cross/ppermute | solution.py:85
  8.2 1.5 %collective-permute-start = (bf16[256,512]{1,0:T(8,128)(2,1)S(1)}, bf16[256,512]{1,0:T(8,128)(2,1)S(1)}, u32[]{:S(2)}, u32[]{:S(2)}) collective-permute-start(bf16[256,512]{1,0:T(8,128)(2,1)S(1)} %half.1.refs_4_), channel_id=1, source_target_pairs={{0,4},{4,0},{8,12},{12,8},{16,20},{20,16},{24,28},{28,24},{1,5},{5... | collective-permute-start | bytes 786440 | tf_op jit(solution)/shard_map/swap_own/ppermute | solution.py:85
  9.7 3.0 %collective-permute-done.3.refs_2_ = bf16[2,128,512]{2,1,0:T(8,128)(2,1)S(1)} collective-permute-done((bf16[2,128,512]{2,1,0:T(8,128)(2,1)S(1)}, bf16[2,128,512]{2,1,0:T(8,128)(2,1)S(1)}, u32[]{:S(2)}, u32[]{:S(2)}) %collective-permute-start.3) | collective-permute-done | bytes 262176 | tf_op jit(solution)/shard_map/pairs1_same/ppermute | solution.py:85
  12.7 4.1 %collective-permute-start.1 = (bf16[256,512]{1,0:T(8,128)(2,1)S(1)}, bf16[256,512]{1,0:T(8,128)(2,1)S(1)}, u32[]{:S(2)}, u32[]{:S(2)}) collective-permute-start(bf16[256,512]{1,0:T(8,128)(2,1)S(1)} %half.1.refs_4_), channel_id=1, source_target_pairs={{0,24},{4,28},{8,0},{12,4},{16,8},{20,12},{24,16},{28,20},{1,25},{... | collective-permute-start | bytes 786440 | tf_op jit(solution)/shard_map/back1/ppermute | solution.py:85
  16.8 1.5 %collective-permute-start.7 = (bf16[256,512]{1,0:T(8,128)(2,1)S(1)}, bf16[256,512]{1,0:T(8,128)(2,1)S(1)}, u32[]{:S(2)}, u32[]{:S(2)}) collective-permute-start(bf16[256,512]{1,0:T(8,128)(2,1)S(1)} %collective-permute-done.6.refs_6_), channel_id=1, source_target_pairs={{0,4},{4,0},{8,12},{12,8},{16,20},{20,16},{24,28},{28,24},{1,5},{5... | collective-permute-start | bytes 786440 | tf_op jit(solution)/shard_map/swap_ahead1/ppermute | solution.py:85
  18.3 1.5 %collective-permute-start.5 = (bf16[1,128,512]{2,1,0:T(8,128)(2,1)S(1)}, bf16[1,128,512]{2,1,0:T(8,128)(2,1)S(1)}, u32[]{:S(2)}, u32[]{:S(2)}) collective-permute-start(bf16[1,128,512]{2,1,0:T(8,128)(2,1)S(1)} %get-tuple-element.36), channel_id=1, source_target_pairs={{0,2},{1,3},{2,0},{3,1},{4,6},{5,7},{6,4},{7,5},{8,10},{9,11},{10,... | collective-permute-start | bytes 393224 | tf_op jit(solution)/shard_map/queries1_same/ppermute | solution.py:85
  20.5 0.8 %collective-permute-done.1.refs_8_ = bf16[256,512]{1,0:T(8,128)(2,1)S(1)} collective-permute-done((bf16[256,512]{1,0:T(8,128)(2,1)S(1)}, bf16[256,512]{1,0:T(8,128)(2,1)S(1)}, u32[]{:S(2)}, u32[]{:S(2)}) %collective-permute-start.1) | collective-permute-done | bytes 262176 | tf_op jit(solution)/shard_map/back1/ppermute | solution.py:85
  21.3 0.6 %collective-permute-start.13 = (bf16[256,512]{1,0:T(8,128)(2,1)S(1)}, bf16[256,512]{1,0:T(8,128)(2,1)S(1)}, u32[]{:S(2)}, u32[]{:S(2)}) collective-permute-start(bf16[256,512]{1,0:T(8,128)(2,1)S(1)} %collective-permute-done.6.refs_6_), channel_id=1, source_target_pairs={{0,8},{4,12},{8,16},{12,20},{16,24},{20,28},{24,0},{28,4},{1,9},{5... | collective-permute-start | bytes 786440 | tf_op jit(solution)/shard_map/ahead2/ppermute | solution.py:85
  21.9 2.3 %attend.2.refs_0_ = bf16[2,128,512]{2,1,0:T(8,128)(2,1)S(1)} custom-call(s32[1]{0:T(128)S(6)} %copy.13.count_ref, bf16[3,128,512]{2,1,0:T(8,128)(2,1)S(1)} %get-tuple-element.30.refs_0_, bf16[3,128,512]{2,1,0:T(8,128)(2,1)S(1)} %collective-permute-done.2.refs_1_, bf16[2,128,512]{2,1,0:T(8,128)(2,1)S(1)} %collective-permute-done.3.refs_2_, ...), custom_call_target="tpu_custom_call" | custom-call | bytes 11070000 | tf_op jit(solution)/shard_map/attend/pallas_call | solution.py:192
  24.1 1.2 %collective-permute-start.9 = (bf16[2,128,512]{2,1,0:T(8,128)(2,1)S(1)}, bf16[2,128,512]{2,1,0:T(8,128)(2,1)S(1)}, u32[]{:S(2)}, u32[]{:S(2)}) collective-permute-start(bf16[2,128,512]{2,1,0:T(8,128)(2,1)S(1)} %attend.2.refs_0_), channel_id=1, source_target_pairs={{0,2},{1,3},{2,0},{3,1},{4,6},{5,7},{6,4},{7,5},{8,10},{9,11},{10,... | collective-permute-start | bytes 786440 | tf_op jit(solution)/shard_map/attended0_to1/ppermute | solution.py:85
  25.4 1.5 %collective-permute-start.11 = (bf16[256,512]{1,0:T(8,128)(2,1)S(1)}, bf16[256,512]{1,0:T(8,128)(2,1)S(1)}, u32[]{:S(2)}, u32[]{:S(2)}) collective-permute-start(bf16[256,512]{1,0:T(8,128)(2,1)S(1)} %collective-permute-done.1.refs_8_), channel_id=1, source_target_pairs={{0,4},{4,0},{8,12},{12,8},{16,20},{20,16},{24,28},{28,24},{1,5},{5... | collective-permute-start | bytes 786440 | tf_op jit(solution)/shard_map/swap_back1/ppermute | solution.py:85
  26.9 2.3 %attend.3.refs_0_ = bf16[2,128,512]{2,1,0:T(8,128)(2,1)S(1)} custom-call(s32[1]{0:T(128)S(6)} %copy.13.count_ref, bf16[3,128,512]{2,1,0:T(8,128)(2,1)S(1)} %get-tuple-element.30.refs_0_, bf16[3,128,512]{2,1,0:T(8,128)(2,1)S(1)} %collective-permute-done.2.refs_1_, bf16[2,128,512]{2,1,0:T(8,128)(2,1)S(1)} %collective-permute-done.3.refs_2_, ...), custom_call_target="tpu_custom_call" | custom-call | bytes 11070000 | tf_op jit(solution)/shard_map/attend/pallas_call | solution.py:192
  29.1 0.9 %collective-permute-start.16 = (bf16[2,128,512]{2,1,0:T(8,128)(2,1)S(1)}, bf16[2,128,512]{2,1,0:T(8,128)(2,1)S(1)}, u32[]{:S(2)}, u32[]{:S(2)}) collective-permute-start(bf16[2,128,512]{2,1,0:T(8,128)(2,1)S(1)} %attend.3.refs_0_), channel_id=1, source_target_pairs={{0,2},{1,3},{2,0},{3,1},{4,6},{5,7},{6,4},{7,5},{8,10},{9,11},{10,... | collective-permute-start | bytes 786440 | tf_op jit(solution)/shard_map/attended1_to1/ppermute | solution.py:85
  30.1 1.1 %collective-permute-done.13.refs_10_ = bf16[256,512]{1,0:T(8,128)(2,1)S(1)} collective-permute-done((bf16[256,512]{1,0:T(8,128)(2,1)S(1)}, bf16[256,512]{1,0:T(8,128)(2,1)S(1)}, u32[]{:S(2)}, u32[]{:S(2)}) %collective-permute-start.13) | collective-permute-done | bytes 262176 | tf_op jit(solution)/shard_map/ahead2/ppermute | solution.py:85
  31.2 0.5 %collective-permute-start.14 = (bf16[256,512]{1,0:T(8,128)(2,1)S(1)}, bf16[256,512]{1,0:T(8,128)(2,1)S(1)}, u32[]{:S(2)}, u32[]{:S(2)}) collective-permute-start(bf16[256,512]{1,0:T(8,128)(2,1)S(1)} %collective-permute-done.13.refs_10_), channel_id=1, source_target_pairs={{0,4},{4,0},{8,12},{12,8},{16,20},{20,16},{24,28},{28,24},{1,5},{5... | collective-permute-start | bytes 786440 | tf_op jit(solution)/shard_map/swap_ahead2/ppermute | solution.py:85
  31.7 0.9 %collective-permute-done.9.refs_2_ = bf16[2,128,512]{2,1,0:T(8,128)(2,1)S(1)} collective-permute-done((bf16[2,128,512]{2,1,0:T(8,128)(2,1)S(1)}, bf16[2,128,512]{2,1,0:T(8,128)(2,1)S(1)}, u32[]{:S(2)}, u32[]{:S(2)}) %collective-permute-start.9) | collective-permute-done | bytes 262176 | tf_op jit(solution)/shard_map/attended0_to1/ppermute | solution.py:85
  32.6 0.5 %collective-permute-done.11.refs_9_ = bf16[256,512]{1,0:T(8,128)(2,1)S(1)} collective-permute-done((bf16[256,512]{1,0:T(8,128)(2,1)S(1)}, bf16[256,512]{1,0:T(8,128)(2,1)S(1)}, u32[]{:S(2)}, u32[]{:S(2)}) %collective-permute-start.11) | collective-permute-done | bytes 262176 | tf_op jit(solution)/shard_map/swap_back1/ppermute | solution.py:85
  33.1 0.5 %collective-permute-start.15 = (bf16[2,128,512]{2,1,0:T(8,128)(2,1)S(1)}, bf16[2,128,512]{2,1,0:T(8,128)(2,1)S(1)}, u32[]{:S(2)}, u32[]{:S(2)}) collective-permute-start(bf16[2,128,512]{2,1,0:T(8,128)(2,1)S(1)} %attend.2.refs_0_), channel_id=1, source_target_pairs={{0,1},{1,0},{2,3},{3,2},{4,5},{5,4},{6,7},{7,6},{8,9},{9,8},{10,11... | collective-permute-start | bytes 786440 | tf_op jit(solution)/shard_map/sibling0_for0/ppermute | solution.py:85
  33.6 3.8 %collective-permute-done.16.refs_2_ = bf16[2,128,512]{2,1,0:T(8,128)(2,1)S(1)} collective-permute-done((bf16[2,128,512]{2,1,0:T(8,128)(2,1)S(1)}, bf16[2,128,512]{2,1,0:T(8,128)(2,1)S(1)}, u32[]{:S(2)}, u32[]{:S(2)}) %collective-permute-start.16) | collective-permute-done | bytes 262176 | tf_op jit(solution)/shard_map/attended1_to1/ppermute | solution.py:85
  37.4 1.2 %collective-permute-done.14.refs_11_ = bf16[256,512]{1,0:T(8,128)(2,1)S(1)} collective-permute-done((bf16[256,512]{1,0:T(8,128)(2,1)S(1)}, bf16[256,512]{1,0:T(8,128)(2,1)S(1)}, u32[]{:S(2)}, u32[]{:S(2)}) %collective-permute-start.14) | collective-permute-done | bytes 262176 | tf_op jit(solution)/shard_map/swap_ahead2/ppermute | solution.py:85
  38.6 1.3 %project.2 = (bf16[128,512]{1,0:T(8,128)(2,1)S(1)}, bf16[128,512]{1,0:T(8,128)(2,1)S(1)}) custom-call(s32[8]{0:T(128)S(1)} %copy-done.3, bf16[2,128,512]{2,1,0:T(8,128)(2,1)S(1)} %attend.3.refs_0_, bf16[2,128,512]{2,1,0:T(8,128)(2,1)S(1)} %collective-permute-done.10.refs_1_, bf16[2,128,512]{2,1,0:T(8,128)(2,1)S(1)} %collective-permute-done.9.refs_2_, ...), custom_call_target="tpu_custom_call" | custom-call | bytes 7380000 | tf_op jit(solution)/shard_map/project/pallas_call | solution.py:239
  40.0 1.5 %collective-permute-start.19 = (bf16[128,512]{1,0:T(8,128)(2,1)S(1)}, bf16[128,512]{1,0:T(8,128)(2,1)S(1)}, u32[]{:S(2)}, u32[]{:S(2)}) collective-permute-start(bf16[128,512]{1,0:T(8,128)(2,1)S(1)} %get-tuple-element.42), channel_id=1, source_target_pairs={{0,2},{1,3},{2,0},{3,1},{4,6},{5,7},{6,4},{7,5},{8,10},{9,11},{10,... | collective-permute-start | bytes 393224 | tf_op jit(solution)/shard_map/out1_same/ppermute | solution.py:85
  41.5 1.3 %project.3 = (bf16[128,512]{1,0:T(8,128)(2,1)S(1)}, bf16[128,512]{1,0:T(8,128)(2,1)S(1)}) custom-call(s32[8]{0:T(128)S(1)} %copy-done.3, bf16[2,128,512]{2,1,0:T(8,128)(2,1)S(1)} %attend.2.refs_0_, bf16[2,128,512]{2,1,0:T(8,128)(2,1)S(1)} %collective-permute-done.15.refs_1_, bf16[2,128,512]{2,1,0:T(8,128)(2,1)S(1)} %collective-permute-done.16.refs_2_, ...), custom_call_target="tpu_custom_call" | custom-call | bytes 7380000 | tf_op jit(solution)/shard_map/project/pallas_call | solution.py:239
  42.8 0.7 %collective-permute-start.18 = (bf16[128,512]{1,0:T(8,128)(2,1)S(1)}, bf16[128,512]{1,0:T(8,128)(2,1)S(1)}, u32[]{:S(2)}, u32[]{:S(2)}) collective-permute-start(bf16[128,512]{1,0:T(8,128)(2,1)S(1)} %get-tuple-element.47), channel_id=1, source_target_pairs={{0,1},{1,0},{2,3},{3,2},{4,5},{5,4},{6,7},{7,6},{8,9},{9,8},{10,11... | collective-permute-start | bytes 393224 | tf_op jit(solution)/shard_map/out_sibling/ppermute | solution.py:85
  43.5 1.4 %multiply_subtract_fusion = (f32[1,256,512]{2,1,0:T(8,128)}, f32[1,256,512]{2,1,0:T(8,128)}, f32[1,256,512]{2,1,0:T(8,128)}) fusion(f32[1,256,512]{2,1,0:T(8,128)S(1)} %copy-done, f32[1,256,512]{2,1,0:T(8,128)S(1)} %copy-done.4, f32[1,256,512]{2,1,0:T(8,128)S(1)} %copy-done.1, f32[1,256,512]{2,1,0:T(8,128)S(1)} %copy-done.2), kind=kLoop, calls=%fused_computation.2 | loop fusion | flops 1966080 | bytes 3670016 | tf_op jit(solution)/shard_map/sub | solution.py:26
  45.0 0.5 %collective-permute-done.19.refs_2_ = bf16[128,512]{1,0:T(8,128)(2,1)S(1)} collective-permute-done((bf16[128,512]{1,0:T(8,128)(2,1)S(1)}, bf16[128,512]{1,0:T(8,128)(2,1)S(1)}, u32[]{:S(2)}, u32[]{:S(2)}) %collective-permute-start.19) | collective-permute-done | bytes 131104 | tf_op jit(solution)/shard_map/out1_same/ppermute | solution.py:85
  45.5 1.7 %collective-permute-done.20.refs_3_ = bf16[128,512]{1,0:T(8,128)(2,1)S(1)} collective-permute-done((bf16[128,512]{1,0:T(8,128)(2,1)S(1)}, bf16[128,512]{1,0:T(8,128)(2,1)S(1)}, u32[]{:S(2)}, u32[]{:S(2)}) %collective-permute-start.20) | collective-permute-done | bytes 131104 | tf_op jit(solution)/shard_map/out1_cross/ppermute | solution.py:85
  47.3 0.8 %place.1 = bf16[128,2048]{1,0:T(8,128)(2,1)} custom-call(bf16[128,512]{1,0:T(8,128)(2,1)S(1)} %get-tuple-element.46.refs_0_, bf16[128,512]{1,0:T(8,128)(2,1)S(1)} %collective-permute-done.18.refs_1_, bf16[128,512]{1,0:T(8,128)(2,1)S(1)} %collective-permute-done.19.refs_2_, bf16[128,512]{1,0:T(8,128)(2,1)S(1)} %collective-permute-done.20.refs_3_), custom_call_target="tpu_custom_call" | custom-call | bytes 3690000 | tf_op jit(solution)/shard_map/place/pallas_call | solution.py:267
  (28 shorter events, 0.1 us)
Async XLA Ops:
  0.6 4.9 %copy-start = (f32[1,256,512]{2,1,0:T(8,128)S(1)}, f32[1,256,512]{2,1,0:T(8,128)}, u32[]{:S(2)}) copy-start(f32[1,256,512]{2,1,0:T(8,128)} %param.13) | copy-start | bytes 1572868
  0.6 4.9 %copy-start.1 = (f32[1,256,512]{2,1,0:T(8,128)S(1)}, f32[1,256,512]{2,1,0:T(8,128)}, u32[]{:S(2)}) copy-start(f32[1,256,512]{2,1,0:T(8,128)} %param.14) | copy-start | bytes 1572868
  0.7 4.9 %copy-start.2 = (f32[1,256,512]{2,1,0:T(8,128)S(1)}, f32[1,256,512]{2,1,0:T(8,128)}, u32[]{:S(2)}) copy-start(f32[1,256,512]{2,1,0:T(8,128)} %param.15) | copy-start | bytes 1572868
  2.5 10.2 %collective-permute-start.3 = (bf16[2,128,512]{2,1,0:T(8,128)(2,1)S(1)}, bf16[2,128,512]{2,1,0:T(8,128)(2,1)S(1)}, u32[]{:S(2)}, u32[]{:S(2)}) collective-permute-start(bf16[2,128,512]{2,1,0:T(8,128)(2,1)S(1)} %get-tuple-element.33), channel_id=1, source_target_pairs={{0,2},{1,3},{2,0},{3,1},{4,6},{5,7},{6,4},{7,5},{8,10},{9,11},{10,... | collective-permute-start | bytes 786440 | tf_op jit(solution)/shard_map/pairs1_same/ppermute | solution.py:85
  6.0 10.8 %collective-permute-start.6 = (bf16[256,512]{1,0:T(8,128)(2,1)S(1)}, bf16[256,512]{1,0:T(8,128)(2,1)S(1)}, u32[]{:S(2)}, u32[]{:S(2)}) collective-permute-start(bf16[256,512]{1,0:T(8,128)(2,1)S(1)} %half.1.refs_4_), channel_id=1, source_target_pairs={{0,8},{4,12},{8,16},{12,20},{16,24},{20,28},{24,0},{28,4},{1,9},{5... | collective-permute-start | bytes 786440 | tf_op jit(solution)/shard_map/ahead1/ppermute | solution.py:85
  7.6 14.2 %collective-permute-start.2 = (bf16[3,128,512]{2,1,0:T(8,128)(2,1)S(1)}, bf16[3,128,512]{2,1,0:T(8,128)(2,1)S(1)}, u32[]{:S(2)}, u32[]{:S(2)}) collective-permute-start(bf16[3,128,512]{2,1,0:T(8,128)(2,1)S(1)} %get-tuple-element.32), channel_id=1, source_target_pairs={{0,1},{1,0},{2,3},{3,2},{4,5},{5,4},{6,7},{7,6},{8,9},{9,8},{10,11... | collective-permute-start | bytes 1179656 | tf_op jit(solution)/shard_map/sibling/ppermute | solution.py:85
  7.6 10.7 %collective-permute-start.4 = (bf16[2,128,512]{2,1,0:T(8,128)(2,1)S(1)}, bf16[2,128,512]{2,1,0:T(8,128)(2,1)S(1)}, u32[]{:S(2)}, u32[]{:S(2)}) collective-permute-start(bf16[2,128,512]{2,1,0:T(8,128)(2,1)S(1)} %get-tuple-element.34), channel_id=1, source_target_pairs={{0,3},{1,2},{2,1},{3,0},{4,7},{5,6},{6,5},{7,4},{8,11},{9,10},{10,... | collective-permute-start | bytes 786440 | tf_op jit(solution)/shard_map/pairs1_cross/ppermute | solution.py:85
  8.2 11.6 %collective-permute-start = (bf16[256,512]{1,0:T(8,128)(2,1)S(1)}, bf16[256,512]{1,0:T(8,128)(2,1)S(1)}, u32[]{:S(2)}, u32[]{:S(2)}) collective-permute-start(bf16[256,512]{1,0:T(8,128)(2,1)S(1)} %half.1.refs_4_), channel_id=1, source_target_pairs={{0,4},{4,0},{8,12},{12,8},{16,20},{20,16},{24,28},{28,24},{1,5},{5... | collective-permute-start | bytes 786440 | tf_op jit(solution)/shard_map/swap_own/ppermute | solution.py:85
  12.7 8.6 %collective-permute-start.1 = (bf16[256,512]{1,0:T(8,128)(2,1)S(1)}, bf16[256,512]{1,0:T(8,128)(2,1)S(1)}, u32[]{:S(2)}, u32[]{:S(2)}) collective-permute-start(bf16[256,512]{1,0:T(8,128)(2,1)S(1)} %half.1.refs_4_), channel_id=1, source_target_pairs={{0,24},{4,28},{8,0},{12,4},{16,8},{20,12},{24,16},{28,20},{1,25},{... | collective-permute-start | bytes 786440 | tf_op jit(solution)/shard_map/back1/ppermute | solution.py:85
  16.8 10.0 %collective-permute-start.7 = (bf16[256,512]{1,0:T(8,128)(2,1)S(1)}, bf16[256,512]{1,0:T(8,128)(2,1)S(1)}, u32[]{:S(2)}, u32[]{:S(2)}) collective-permute-start(bf16[256,512]{1,0:T(8,128)(2,1)S(1)} %collective-permute-done.6.refs_6_), channel_id=1, source_target_pairs={{0,4},{4,0},{8,12},{12,8},{16,20},{20,16},{24,28},{28,24},{1,5},{5... | collective-permute-start | bytes 786440 | tf_op jit(solution)/shard_map/swap_ahead1/ppermute | solution.py:85
  18.3 7.0 %collective-permute-start.5 = (bf16[1,128,512]{2,1,0:T(8,128)(2,1)S(1)}, bf16[1,128,512]{2,1,0:T(8,128)(2,1)S(1)}, u32[]{:S(2)}, u32[]{:S(2)}) collective-permute-start(bf16[1,128,512]{2,1,0:T(8,128)(2,1)S(1)} %get-tuple-element.36), channel_id=1, source_target_pairs={{0,2},{1,3},{2,0},{3,1},{4,6},{5,7},{6,4},{7,5},{8,10},{9,11},{10,... | collective-permute-start | bytes 393224 | tf_op jit(solution)/shard_map/queries1_same/ppermute | solution.py:85
  19.9 7.0 %collective-permute-start.8 = (bf16[1,128,512]{2,1,0:T(8,128)(2,1)S(1)}, bf16[1,128,512]{2,1,0:T(8,128)(2,1)S(1)}, u32[]{:S(2)}, u32[]{:S(2)}) collective-permute-start(bf16[1,128,512]{2,1,0:T(8,128)(2,1)S(1)} %get-tuple-element.39), channel_id=1, source_target_pairs={{0,3},{1,2},{2,1},{3,0},{4,7},{5,6},{6,5},{7,4},{8,11},{9,10},{10,... | collective-permute-start | bytes 393224 | tf_op jit(solution)/shard_map/queries1_cross/ppermute | solution.py:85
  21.3 9.9 %collective-permute-start.13 = (bf16[256,512]{1,0:T(8,128)(2,1)S(1)}, bf16[256,512]{1,0:T(8,128)(2,1)S(1)}, u32[]{:S(2)}, u32[]{:S(2)}) collective-permute-start(bf16[256,512]{1,0:T(8,128)(2,1)S(1)} %collective-permute-done.6.refs_6_), channel_id=1, source_target_pairs={{0,8},{4,12},{8,16},{12,20},{16,24},{20,28},{24,0},{28,4},{1,9},{5... | collective-permute-start | bytes 786440 | tf_op jit(solution)/shard_map/ahead2/ppermute | solution.py:85
  24.1 14.5 %copy-start.3 = (s32[8]{0:T(128)S(1)}, s32[8]{0:T(128)}, u32[]{:S(2)}) copy-start(s32[8]{0:T(128)} %bucket_ref.3) | copy-start | bytes 100
  24.1 8.5 %collective-permute-start.9 = (bf16[2,128,512]{2,1,0:T(8,128)(2,1)S(1)}, bf16[2,128,512]{2,1,0:T(8,128)(2,1)S(1)}, u32[]{:S(2)}, u32[]{:S(2)}) collective-permute-start(bf16[2,128,512]{2,1,0:T(8,128)(2,1)S(1)} %attend.2.refs_0_), channel_id=1, source_target_pairs={{0,2},{1,3},{2,0},{3,1},{4,6},{5,7},{6,4},{7,5},{8,10},{9,11},{10,... | collective-permute-start | bytes 786440 | tf_op jit(solution)/shard_map/attended0_to1/ppermute | solution.py:85
  25.4 7.8 %collective-permute-start.11 = (bf16[256,512]{1,0:T(8,128)(2,1)S(1)}, bf16[256,512]{1,0:T(8,128)(2,1)S(1)}, u32[]{:S(2)}, u32[]{:S(2)}) collective-permute-start(bf16[256,512]{1,0:T(8,128)(2,1)S(1)} %collective-permute-done.1.refs_8_), channel_id=1, source_target_pairs={{0,4},{4,0},{8,12},{12,8},{16,20},{20,16},{24,28},{28,24},{1,5},{5... | collective-permute-start | bytes 786440 | tf_op jit(solution)/shard_map/swap_back1/ppermute | solution.py:85
  29.1 8.3 %collective-permute-start.16 = (bf16[2,128,512]{2,1,0:T(8,128)(2,1)S(1)}, bf16[2,128,512]{2,1,0:T(8,128)(2,1)S(1)}, u32[]{:S(2)}, u32[]{:S(2)}) collective-permute-start(bf16[2,128,512]{2,1,0:T(8,128)(2,1)S(1)} %attend.3.refs_0_), channel_id=1, source_target_pairs={{0,2},{1,3},{2,0},{3,1},{4,6},{5,7},{6,4},{7,5},{8,10},{9,11},{10,... | collective-permute-start | bytes 786440 | tf_op jit(solution)/shard_map/attended1_to1/ppermute | solution.py:85
  31.2 7.4 %collective-permute-start.14 = (bf16[256,512]{1,0:T(8,128)(2,1)S(1)}, bf16[256,512]{1,0:T(8,128)(2,1)S(1)}, u32[]{:S(2)}, u32[]{:S(2)}) collective-permute-start(bf16[256,512]{1,0:T(8,128)(2,1)S(1)} %collective-permute-done.13.refs_10_), channel_id=1, source_target_pairs={{0,4},{4,0},{8,12},{12,8},{16,20},{20,16},{24,28},{28,24},{1,5},{5... | collective-permute-start | bytes 786440 | tf_op jit(solution)/shard_map/swap_ahead2/ppermute | solution.py:85
  32.6 6.0 %collective-permute-start.10 = (bf16[2,128,512]{2,1,0:T(8,128)(2,1)S(1)}, bf16[2,128,512]{2,1,0:T(8,128)(2,1)S(1)}, u32[]{:S(2)}, u32[]{:S(2)}) collective-permute-start(bf16[2,128,512]{2,1,0:T(8,128)(2,1)S(1)} %attend.3.refs_0_), channel_id=1, source_target_pairs={{0,1},{1,0},{2,3},{3,2},{4,5},{5,4},{6,7},{7,6},{8,9},{9,8},{10,11... | collective-permute-start | bytes 786440 | tf_op jit(solution)/shard_map/sibling0_for1/ppermute | solution.py:85
  33.1 5.5 %collective-permute-start.12 = (bf16[2,128,512]{2,1,0:T(8,128)(2,1)S(1)}, bf16[2,128,512]{2,1,0:T(8,128)(2,1)S(1)}, u32[]{:S(2)}, u32[]{:S(2)}) collective-permute-start(bf16[2,128,512]{2,1,0:T(8,128)(2,1)S(1)} %collective-permute-done.9.refs_2_), channel_id=1, source_target_pairs={{0,1},{1,0},{2,3},{3,2},{4,5},{5,4},{6,7},{7,6},{8,9},{9,8},{10,11... | collective-permute-start | bytes 786440 | tf_op jit(solution)/shard_map/sibling1_for1/ppermute | solution.py:85
  33.1 8.3 %collective-permute-start.15 = (bf16[2,128,512]{2,1,0:T(8,128)(2,1)S(1)}, bf16[2,128,512]{2,1,0:T(8,128)(2,1)S(1)}, u32[]{:S(2)}, u32[]{:S(2)}) collective-permute-start(bf16[2,128,512]{2,1,0:T(8,128)(2,1)S(1)} %attend.2.refs_0_), channel_id=1, source_target_pairs={{0,1},{1,0},{2,3},{3,2},{4,5},{5,4},{6,7},{7,6},{8,9},{9,8},{10,11... | collective-permute-start | bytes 786440 | tf_op jit(solution)/shard_map/sibling0_for0/ppermute | solution.py:85
  37.4 4.1 %collective-permute-start.17 = (bf16[2,128,512]{2,1,0:T(8,128)(2,1)S(1)}, bf16[2,128,512]{2,1,0:T(8,128)(2,1)S(1)}, u32[]{:S(2)}, u32[]{:S(2)}) collective-permute-start(bf16[2,128,512]{2,1,0:T(8,128)(2,1)S(1)} %collective-permute-done.16.refs_2_), channel_id=1, source_target_pairs={{0,1},{1,0},{2,3},{3,2},{4,5},{5,4},{6,7},{7,6},{8,9},{9,8},{10,11... | collective-permute-start | bytes 786440 | tf_op jit(solution)/shard_map/sibling1_for0/ppermute | solution.py:85
  40.0 5.6 %collective-permute-start.19 = (bf16[128,512]{1,0:T(8,128)(2,1)S(1)}, bf16[128,512]{1,0:T(8,128)(2,1)S(1)}, u32[]{:S(2)}, u32[]{:S(2)}) collective-permute-start(bf16[128,512]{1,0:T(8,128)(2,1)S(1)} %get-tuple-element.42), channel_id=1, source_target_pairs={{0,2},{1,3},{2,0},{3,1},{4,6},{5,7},{6,4},{7,5},{8,10},{9,11},{10,... | collective-permute-start | bytes 393224 | tf_op jit(solution)/shard_map/out1_same/ppermute | solution.py:85
  41.5 2.1 %copy-start.4 = (f32[1,256,512]{2,1,0:T(8,128)S(1)}, f32[1,256,512]{2,1,0:T(8,128)}, u32[]{:S(2)}) copy-start(f32[1,256,512]{2,1,0:T(8,128)} %param.16) | copy-start | bytes 1572868
  41.5 5.8 %collective-permute-start.20 = (bf16[128,512]{1,0:T(8,128)(2,1)S(1)}, bf16[128,512]{1,0:T(8,128)(2,1)S(1)}, u32[]{:S(2)}, u32[]{:S(2)}) collective-permute-start(bf16[128,512]{1,0:T(8,128)(2,1)S(1)} %get-tuple-element.48), channel_id=1, source_target_pairs={{0,3},{1,2},{2,1},{3,0},{4,7},{5,6},{6,5},{7,4},{8,11},{9,10},{10,... | collective-permute-start | bytes 393224 | tf_op jit(solution)/shard_map/out1_cross/ppermute | solution.py:85
  42.8 4.5 %collective-permute-start.18 = (bf16[128,512]{1,0:T(8,128)(2,1)S(1)}, bf16[128,512]{1,0:T(8,128)(2,1)S(1)}, u32[]{:S(2)}, u32[]{:S(2)}) collective-permute-start(bf16[128,512]{1,0:T(8,128)(2,1)S(1)} %get-tuple-element.47), channel_id=1, source_target_pairs={{0,1},{1,0},{2,3},{3,2},{4,5},{5,4},{6,7},{7,6},{8,9},{9,8},{10,11... | collective-permute-start | bytes 393224 | tf_op jit(solution)/shard_map/out_sibling/ppermute | solution.py:85

commit v7 on v5

--- a/solution.py
+++ b/solution.py
@@ -38,14 +38,13 @@
     "queries1_same": ["pairs1_same"],
     "queries1_cross": ["pairs1_same", "pairs1_cross"],
     "attend0": ["swap_own", "back1"],
-    "attend1": ["attend0", "back1", "swap_ahead1"],
+    "attend1": ["attend0"],
     "attended1_to1": ["swap_ahead1"],
     "sibling0_for1": ["attended0_to1"],
     "sibling1_for1": ["swap_back1"],
     "sibling0_for0": ["attended0_to1"],
     "project0": ["project1"],
     "states": ["attended0_to1"],
-    "sibling": ["half"],
 }
 
 SMALL = pltpu.CompilerParams(vmem_limit_bytes=16 * 1024 * 1024)

time: 48.3 us -> 48.3 us (level)
  no operation moved by 1% of the time
where the time goes in v7:
time: 48.3 us; the launch traced here: 48.1 us
  starting transfers between devices  21.4 us (44%)
  waiting for transfers between devices  13.6 us (28%)
  Pallas kernels  10.2 us (21%)
  other arithmetic  1.43 us (3%)
  between operations  1.4 us (3%)
    ppermute x21, starting transfers between devices, permute(): return self.add(name, lax.ppermute(array, axis, perm))  21.4 us
    ppermute x21, waiting for transfers between devices, permute(): return self.add(name, lax.ppermute(array, axis, perm))  13.6 us
    pallas_call x2, Pallas kernels, attend(): pl.pallas_call(functools.partial(attend_kernel, n_pairs, picks), out_shap...  4.53 us
    pallas_call x2, Pallas kernels, project(): pl.pallas_call(functools.partial(project_kernel, len(att), steps), out_sh...  2.59 us
    pallas_call x1, Pallas kernels, cut(): pl.pallas_call(cut_kernel, out_shape=[jax.ShapeDtypeStruct((n, rows, widt...  1.86 us
    sub x1, other arithmetic, adam_update(): master_weight - learn_rate * (first_hat / (jnp.sqrt(second_hat) + epsilon...  1.43 us
  transfers between devices with their start and end apart: 21, of which 9 were waited for; matrix products, arithmetic and copies ran while one was open for 3% of the time, Pallas kernels for 16%

profile of v7, /device:TPU:0, one launch (start us, length us, event | category | flops | bytes accessed | tf_op | source)
XLA Modules:
  0.0 48.1 jit_solution(15404197902114648410)
XLA Ops:
  0.7 1.9 %cut.1 = (bf16[3,128,512]{2,1,0:T(8,128)(2,1)S(1)}, bf16[3,128,512]{2,1,0:T(8,128)(2,1)S(1)}, bf16[2,128,512]{2,1,0:T(8,128)(2,1)S(1)}, bf16[2,128,512]{2,1,0:T(...) custom-call(bf16[128,2048]{1,0:T(8,128)(2,1)} %bitcast.13, ...), custom_call_target="tpu_custom_call" | custom-call | bytes 3690000 | tf_op jit(solution)/shard_map/cut/pallas_call | solution.py:139
  2.5 3.0 %collective-permute-start.3 = (bf16[2,128,512]{2,1,0:T(8,128)(2,1)S(1)}, bf16[2,128,512]{2,1,0:T(8,128)(2,1)S(1)}, u32[]{:S(2)}, u32[]{:S(2)}) collective-permute-start(bf16[2,128,512]{2,1,0:T(8,128)(2,1)S(1)} %get-tuple-element.31), channel_id=1, source_target_pairs={{0,2},{1,3},{2,0},{3,1},{4,6},{5,7},{6,4},{7,5},{8,10},{9,11},{10,... | collective-permute-start | bytes 786440 | tf_op jit(solution)/shard_map/pairs1_same/ppermute | solution.py:84
  5.6 0.4 half.1.refs_4_
  6.0 1.6 %collective-permute-start.11 = (bf16[256,512]{1,0:T(8,128)(2,1)S(1)}, bf16[256,512]{1,0:T(8,128)(2,1)S(1)}, u32[]{:S(2)}, u32[]{:S(2)}) collective-permute-start(bf16[256,512]{1,0:T(8,128)(2,1)S(1)} %half.1.refs_4_), channel_id=1, source_target_pairs={{0,8},{4,12},{8,16},{12,20},{16,24},{20,28},{24,0},{28,4},{1,9},{5... | collective-permute-start | bytes 786440 | tf_op jit(solution)/shard_map/ahead1/ppermute | solution.py:84
  7.6 0.6 %collective-permute-start.4 = (bf16[2,128,512]{2,1,0:T(8,128)(2,1)S(1)}, bf16[2,128,512]{2,1,0:T(8,128)(2,1)S(1)}, u32[]{:S(2)}, u32[]{:S(2)}) collective-permute-start(bf16[2,128,512]{2,1,0:T(8,128)(2,1)S(1)} %get-tuple-element.32), channel_id=1, source_target_pairs={{0,3},{1,2},{2,1},{3,0},{4,7},{5,6},{6,5},{7,4},{8,11},{9,10},{10,... | collective-permute-start | bytes 786440 | tf_op jit(solution)/shard_map/pairs1_cross/ppermute | solution.py:84
  8.2 1.5 %collective-permute-start = (bf16[256,512]{1,0:T(8,128)(2,1)S(1)}, bf16[256,512]{1,0:T(8,128)(2,1)S(1)}, u32[]{:S(2)}, u32[]{:S(2)}) collective-permute-start(bf16[256,512]{1,0:T(8,128)(2,1)S(1)} %half.1.refs_4_), channel_id=1, source_target_pairs={{0,4},{4,0},{8,12},{12,8},{16,20},{20,16},{24,28},{28,24},{1,5},{5... | collective-permute-start | bytes 786440 | tf_op jit(solution)/shard_map/swap_own/ppermute | solution.py:84
  9.7 3.0 %collective-permute-done.3.refs_2_ = bf16[2,128,512]{2,1,0:T(8,128)(2,1)S(1)} collective-permute-done((bf16[2,128,512]{2,1,0:T(8,128)(2,1)S(1)}, bf16[2,128,512]{2,1,0:T(8,128)(2,1)S(1)}, u32[]{:S(2)}, u32[]{:S(2)}) %collective-permute-start.3) | collective-permute-done | bytes 262176 | tf_op jit(solution)/shard_map/pairs1_same/ppermute | solution.py:84
  12.7 4.1 %collective-permute-start.1 = (bf16[256,512]{1,0:T(8,128)(2,1)S(1)}, bf16[256,512]{1,0:T(8,128)(2,1)S(1)}, u32[]{:S(2)}, u32[]{:S(2)}) collective-permute-start(bf16[256,512]{1,0:T(8,128)(2,1)S(1)} %half.1.refs_4_), channel_id=1, source_target_pairs={{0,24},{4,28},{8,0},{12,4},{16,8},{20,12},{24,16},{28,20},{1,25},{... | collective-permute-start | bytes 786440 | tf_op jit(solution)/shard_map/back1/ppermute | solution.py:84
  16.8 1.5 %collective-permute-start.12 = (bf16[256,512]{1,0:T(8,128)(2,1)S(1)}, bf16[256,512]{1,0:T(8,128)(2,1)S(1)}, u32[]{:S(2)}, u32[]{:S(2)}) collective-permute-start(bf16[256,512]{1,0:T(8,128)(2,1)S(1)} %collective-permute-done.11.refs_6_), channel_id=1, source_target_pairs={{0,4},{4,0},{8,12},{12,8},{16,20},{20,16},{24,28},{28,24},{1,5},{5... | collective-permute-start | bytes 786440 | tf_op jit(solution)/shard_map/swap_ahead1/ppermute | solution.py:84
  18.3 1.5 %collective-permute-start.5 = (bf16[1,128,512]{2,1,0:T(8,128)(2,1)S(1)}, bf16[1,128,512]{2,1,0:T(8,128)(2,1)S(1)}, u32[]{:S(2)}, u32[]{:S(2)}) collective-permute-start(bf16[1,128,512]{2,1,0:T(8,128)(2,1)S(1)} %get-tuple-element.34), channel_id=1, source_target_pairs={{0,2},{1,3},{2,0},{3,1},{4,6},{5,7},{6,4},{7,5},{8,10},{9,11},{10,... | collective-permute-start | bytes 393224 | tf_op jit(solution)/shard_map/queries1_same/ppermute | solution.py:84
  20.5 0.8 %collective-permute-done.1.refs_8_ = bf16[256,512]{1,0:T(8,128)(2,1)S(1)} collective-permute-done((bf16[256,512]{1,0:T(8,128)(2,1)S(1)}, bf16[256,512]{1,0:T(8,128)(2,1)S(1)}, u32[]{:S(2)}, u32[]{:S(2)}) %collective-permute-start.1) | collective-permute-done | bytes 262176 | tf_op jit(solution)/shard_map/back1/ppermute | solution.py:84
  21.3 0.6 %collective-permute-start.13 = (bf16[256,512]{1,0:T(8,128)(2,1)S(1)}, bf16[256,512]{1,0:T(8,128)(2,1)S(1)}, u32[]{:S(2)}, u32[]{:S(2)}) collective-permute-start(bf16[256,512]{1,0:T(8,128)(2,1)S(1)} %collective-permute-done.11.refs_6_), channel_id=1, source_target_pairs={{0,8},{4,12},{8,16},{12,20},{16,24},{20,28},{24,0},{28,4},{1,9},{5... | collective-permute-start | bytes 786440 | tf_op jit(solution)/shard_map/ahead2/ppermute | solution.py:84
  21.9 2.3 %attend.2.refs_0_ = bf16[2,128,512]{2,1,0:T(8,128)(2,1)S(1)} custom-call(s32[1]{0:T(128)S(6)} %copy.13.count_ref, bf16[3,128,512]{2,1,0:T(8,128)(2,1)S(1)} %get-tuple-element.29.refs_0_, bf16[3,128,512]{2,1,0:T(8,128)(2,1)S(1)} %collective-permute-done.2.refs_1_, bf16[2,128,512]{2,1,0:T(8,128)(2,1)S(1)} %collective-permute-done.3.refs_2_, ...), custom_call_target="tpu_custom_call" | custom-call | bytes 11070000 | tf_op jit(solution)/shard_map/attend/pallas_call | solution.py:191
  24.1 1.2 %collective-permute-start.7 = (bf16[2,128,512]{2,1,0:T(8,128)(2,1)S(1)}, bf16[2,128,512]{2,1,0:T(8,128)(2,1)S(1)}, u32[]{:S(2)}, u32[]{:S(2)}) collective-permute-start(bf16[2,128,512]{2,1,0:T(8,128)(2,1)S(1)} %attend.2.refs_0_), channel_id=1, source_target_pairs={{0,2},{1,3},{2,0},{3,1},{4,6},{5,7},{6,4},{7,5},{8,10},{9,11},{10,... | collective-permute-start | bytes 786440 | tf_op jit(solution)/shard_map/attended0_to1/ppermute | solution.py:84
  25.4 1.5 %collective-permute-start.9 = (bf16[256,512]{1,0:T(8,128)(2,1)S(1)}, bf16[256,512]{1,0:T(8,128)(2,1)S(1)}, u32[]{:S(2)}, u32[]{:S(2)}) collective-permute-start(bf16[256,512]{1,0:T(8,128)(2,1)S(1)} %collective-permute-done.1.refs_8_), channel_id=1, source_target_pairs={{0,4},{4,0},{8,12},{12,8},{16,20},{20,16},{24,28},{28,24},{1,5},{5... | collective-permute-start | bytes 786440 | tf_op jit(solution)/shard_map/swap_back1/ppermute | solution.py:84
  26.9 2.3 %attend.3.refs_0_ = bf16[2,128,512]{2,1,0:T(8,128)(2,1)S(1)} custom-call(s32[1]{0:T(128)S(6)} %copy.13.count_ref, bf16[3,128,512]{2,1,0:T(8,128)(2,1)S(1)} %get-tuple-element.29.refs_0_, bf16[3,128,512]{2,1,0:T(8,128)(2,1)S(1)} %collective-permute-done.2.refs_1_, bf16[2,128,512]{2,1,0:T(8,128)(2,1)S(1)} %collective-permute-done.3.refs_2_, ...), custom_call_target="tpu_custom_call" | custom-call | bytes 11070000 | tf_op jit(solution)/shard_map/attend/pallas_call | solution.py:191
  29.1 0.9 %collective-permute-start.16 = (bf16[2,128,512]{2,1,0:T(8,128)(2,1)S(1)}, bf16[2,128,512]{2,1,0:T(8,128)(2,1)S(1)}, u32[]{:S(2)}, u32[]{:S(2)}) collective-permute-start(bf16[2,128,512]{2,1,0:T(8,128)(2,1)S(1)} %attend.3.refs_0_), channel_id=1, source_target_pairs={{0,2},{1,3},{2,0},{3,1},{4,6},{5,7},{6,4},{7,5},{8,10},{9,11},{10,... | collective-permute-start | bytes 786440 | tf_op jit(solution)/shard_map/attended1_to1/ppermute | solution.py:84
  30.1 1.1 %collective-permute-done.13.refs_10_ = bf16[256,512]{1,0:T(8,128)(2,1)S(1)} collective-permute-done((bf16[256,512]{1,0:T(8,128)(2,1)S(1)}, bf16[256,512]{1,0:T(8,128)(2,1)S(1)}, u32[]{:S(2)}, u32[]{:S(2)}) %collective-permute-start.13) | collective-permute-done | bytes 262176 | tf_op jit(solution)/shard_map/ahead2/ppermute | solution.py:84
  31.2 0.5 %collective-permute-start.14 = (bf16[256,512]{1,0:T(8,128)(2,1)S(1)}, bf16[256,512]{1,0:T(8,128)(2,1)S(1)}, u32[]{:S(2)}, u32[]{:S(2)}) collective-permute-start(bf16[256,512]{1,0:T(8,128)(2,1)S(1)} %collective-permute-done.13.refs_10_), channel_id=1, source_target_pairs={{0,4},{4,0},{8,12},{12,8},{16,20},{20,16},{24,28},{28,24},{1,5},{5... | collective-permute-start | bytes 786440 | tf_op jit(solution)/shard_map/swap_ahead2/ppermute | solution.py:84
  31.7 0.9 %collective-permute-done.7.refs_2_ = bf16[2,128,512]{2,1,0:T(8,128)(2,1)S(1)} collective-permute-done((bf16[2,128,512]{2,1,0:T(8,128)(2,1)S(1)}, bf16[2,128,512]{2,1,0:T(8,128)(2,1)S(1)}, u32[]{:S(2)}, u32[]{:S(2)}) %collective-permute-start.7) | collective-permute-done | bytes 262176 | tf_op jit(solution)/shard_map/attended0_to1/ppermute | solution.py:84
  32.6 0.5 %collective-permute-done.9.refs_9_ = bf16[256,512]{1,0:T(8,128)(2,1)S(1)} collective-permute-done((bf16[256,512]{1,0:T(8,128)(2,1)S(1)}, bf16[256,512]{1,0:T(8,128)(2,1)S(1)}, u32[]{:S(2)}, u32[]{:S(2)}) %collective-permute-start.9) | collective-permute-done | bytes 262176 | tf_op jit(solution)/shard_map/swap_back1/ppermute | solution.py:84
  33.1 0.5 %collective-permute-start.15 = (bf16[2,128,512]{2,1,0:T(8,128)(2,1)S(1)}, bf16[2,128,512]{2,1,0:T(8,128)(2,1)S(1)}, u32[]{:S(2)}, u32[]{:S(2)}) collective-permute-start(bf16[2,128,512]{2,1,0:T(8,128)(2,1)S(1)} %attend.2.refs_0_), channel_id=1, source_target_pairs={{0,1},{1,0},{2,3},{3,2},{4,5},{5,4},{6,7},{7,6},{8,9},{9,8},{10,11... | collective-permute-start | bytes 786440 | tf_op jit(solution)/shard_map/sibling0_for0/ppermute | solution.py:84
  33.6 3.8 %collective-permute-done.16.refs_2_ = bf16[2,128,512]{2,1,0:T(8,128)(2,1)S(1)} collective-permute-done((bf16[2,128,512]{2,1,0:T(8,128)(2,1)S(1)}, bf16[2,128,512]{2,1,0:T(8,128)(2,1)S(1)}, u32[]{:S(2)}, u32[]{:S(2)}) %collective-permute-start.16) | collective-permute-done | bytes 262176 | tf_op jit(solution)/shard_map/attended1_to1/ppermute | solution.py:84
  37.4 1.2 %collective-permute-done.14.refs_11_ = bf16[256,512]{1,0:T(8,128)(2,1)S(1)} collective-permute-done((bf16[256,512]{1,0:T(8,128)(2,1)S(1)}, bf16[256,512]{1,0:T(8,128)(2,1)S(1)}, u32[]{:S(2)}, u32[]{:S(2)}) %collective-permute-start.14) | collective-permute-done | bytes 262176 | tf_op jit(solution)/shard_map/swap_ahead2/ppermute | solution.py:84
  38.6 1.3 %project.2 = (bf16[128,512]{1,0:T(8,128)(2,1)S(1)}, bf16[128,512]{1,0:T(8,128)(2,1)S(1)}) custom-call(s32[8]{0:T(128)S(1)} %copy-done.3, bf16[2,128,512]{2,1,0:T(8,128)(2,1)S(1)} %attend.3.refs_0_, bf16[2,128,512]{2,1,0:T(8,128)(2,1)S(1)} %collective-permute-done.8.refs_1_, bf16[2,128,512]{2,1,0:T(8,128)(2,1)S(1)} %collective-permute-done.7.refs_2_, ...), custom_call_target="tpu_custom_call" | custom-call | bytes 7380000 | tf_op jit(solution)/shard_map/project/pallas_call | solution.py:238
  40.0 1.5 %collective-permute-start.19 = (bf16[128,512]{1,0:T(8,128)(2,1)S(1)}, bf16[128,512]{1,0:T(8,128)(2,1)S(1)}, u32[]{:S(2)}, u32[]{:S(2)}) collective-permute-start(bf16[128,512]{1,0:T(8,128)(2,1)S(1)} %get-tuple-element.40), channel_id=1, source_target_pairs={{0,2},{1,3},{2,0},{3,1},{4,6},{5,7},{6,4},{7,5},{8,10},{9,11},{10,... | collective-permute-start | bytes 393224 | tf_op jit(solution)/shard_map/out1_same/ppermute | solution.py:84
  41.5 1.3 %project.3 = (bf16[128,512]{1,0:T(8,128)(2,1)S(1)}, bf16[128,512]{1,0:T(8,128)(2,1)S(1)}) custom-call(s32[8]{0:T(128)S(1)} %copy-done.3, bf16[2,128,512]{2,1,0:T(8,128)(2,1)S(1)} %attend.2.refs_0_, bf16[2,128,512]{2,1,0:T(8,128)(2,1)S(1)} %collective-permute-done.15.refs_1_, bf16[2,128,512]{2,1,0:T(8,128)(2,1)S(1)} %collective-permute-done.16.refs_2_, ...), custom_call_target="tpu_custom_call" | custom-call | bytes 7380000 | tf_op jit(solution)/shard_map/project/pallas_call | solution.py:238
  42.8 0.7 %collective-permute-start.18 = (bf16[128,512]{1,0:T(8,128)(2,1)S(1)}, bf16[128,512]{1,0:T(8,128)(2,1)S(1)}, u32[]{:S(2)}, u32[]{:S(2)}) collective-permute-start(bf16[128,512]{1,0:T(8,128)(2,1)S(1)} %get-tuple-element.45), channel_id=1, source_target_pairs={{0,1},{1,0},{2,3},{3,2},{4,5},{5,4},{6,7},{7,6},{8,9},{9,8},{10,11... | collective-permute-start | bytes 393224 | tf_op jit(solution)/shard_map/out_sibling/ppermute | solution.py:84
  43.5 1.4 %multiply_subtract_fusion = (f32[1,256,512]{2,1,0:T(8,128)}, f32[1,256,512]{2,1,0:T(8,128)}, f32[1,256,512]{2,1,0:T(8,128)}) fusion(f32[1,256,512]{2,1,0:T(8,128)S(1)} %copy-done, f32[1,256,512]{2,1,0:T(8,128)S(1)} %copy-done.4, f32[1,256,512]{2,1,0:T(8,128)S(1)} %copy-done.1, f32[1,256,512]{2,1,0:T(8,128)S(1)} %copy-done.2), kind=kLoop, calls=%fused_computation.2 | loop fusion | flops 1966080 | bytes 3670016 | tf_op jit(solution)/shard_map/sub | solution.py:26
  45.0 0.5 %collective-permute-done.19.refs_2_ = bf16[128,512]{1,0:T(8,128)(2,1)S(1)} collective-permute-done((bf16[128,512]{1,0:T(8,128)(2,1)S(1)}, bf16[128,512]{1,0:T(8,128)(2,1)S(1)}, u32[]{:S(2)}, u32[]{:S(2)}) %collective-permute-start.19) | collective-permute-done | bytes 131104 | tf_op jit(solution)/shard_map/out1_same/ppermute | solution.py:84
  45.5 1.7 %collective-permute-done.20.refs_3_ = bf16[128,512]{1,0:T(8,128)(2,1)S(1)} collective-permute-done((bf16[128,512]{1,0:T(8,128)(2,1)S(1)}, bf16[128,512]{1,0:T(8,128)(2,1)S(1)}, u32[]{:S(2)}, u32[]{:S(2)}) %collective-permute-start.20) | collective-permute-done | bytes 131104 | tf_op jit(solution)/shard_map/out1_cross/ppermute | solution.py:84
  47.3 0.8 %place.1 = bf16[128,2048]{1,0:T(8,128)(2,1)} custom-call(bf16[128,512]{1,0:T(8,128)(2,1)S(1)} %get-tuple-element.44.refs_0_, bf16[128,512]{1,0:T(8,128)(2,1)S(1)} %collective-permute-done.18.refs_1_, bf16[128,512]{1,0:T(8,128)(2,1)S(1)} %collective-permute-done.19.refs_2_, bf16[128,512]{1,0:T(8,128)(2,1)S(1)} %collective-permute-done.20.refs_3_), custom_call_target="tpu_custom_call" | custom-call | bytes 3690000 | tf_op jit(solution)/shard_map/place/pallas_call | solution.py:261
  (28 shorter events, 0.1 us)
Async XLA Ops:
  0.6 4.9 %copy-start = (f32[1,256,512]{2,1,0:T(8,128)S(1)}, f32[1,256,512]{2,1,0:T(8,128)}, u32[]{:S(2)}) copy-start(f32[1,256,512]{2,1,0:T(8,128)} %param.13) | copy-start | bytes 1572868
  0.6 4.9 %copy-start.1 = (f32[1,256,512]{2,1,0:T(8,128)S(1)}, f32[1,256,512]{2,1,0:T(8,128)}, u32[]{:S(2)}) copy-start(f32[1,256,512]{2,1,0:T(8,128)} %param.14) | copy-start | bytes 1572868
  0.7 4.9 %copy-start.2 = (f32[1,256,512]{2,1,0:T(8,128)S(1)}, f32[1,256,512]{2,1,0:T(8,128)}, u32[]{:S(2)}) copy-start(f32[1,256,512]{2,1,0:T(8,128)} %param.15) | copy-start | bytes 1572868
  2.5 10.2 %collective-permute-start.3 = (bf16[2,128,512]{2,1,0:T(8,128)(2,1)S(1)}, bf16[2,128,512]{2,1,0:T(8,128)(2,1)S(1)}, u32[]{:S(2)}, u32[]{:S(2)}) collective-permute-start(bf16[2,128,512]{2,1,0:T(8,128)(2,1)S(1)} %get-tuple-element.31), channel_id=1, source_target_pairs={{0,2},{1,3},{2,0},{3,1},{4,6},{5,7},{6,4},{7,5},{8,10},{9,11},{10,... | collective-permute-start | bytes 786440 | tf_op jit(solution)/shard_map/pairs1_same/ppermute | solution.py:84
  6.0 10.8 %collective-permute-start.11 = (bf16[256,512]{1,0:T(8,128)(2,1)S(1)}, bf16[256,512]{1,0:T(8,128)(2,1)S(1)}, u32[]{:S(2)}, u32[]{:S(2)}) collective-permute-start(bf16[256,512]{1,0:T(8,128)(2,1)S(1)} %half.1.refs_4_), channel_id=1, source_target_pairs={{0,8},{4,12},{8,16},{12,20},{16,24},{20,28},{24,0},{28,4},{1,9},{5... | collective-permute-start | bytes 786440 | tf_op jit(solution)/shard_map/ahead1/ppermute | solution.py:84
  7.6 14.2 %collective-permute-start.2 = (bf16[3,128,512]{2,1,0:T(8,128)(2,1)S(1)}, bf16[3,128,512]{2,1,0:T(8,128)(2,1)S(1)}, u32[]{:S(2)}, u32[]{:S(2)}) collective-permute-start(bf16[3,128,512]{2,1,0:T(8,128)(2,1)S(1)} %get-tuple-element.30), channel_id=1, source_target_pairs={{0,1},{1,0},{2,3},{3,2},{4,5},{5,4},{6,7},{7,6},{8,9},{9,8},{10,11... | collective-permute-start | bytes 1179656 | tf_op jit(solution)/shard_map/sibling/ppermute | solution.py:84
  7.6 10.7 %collective-permute-start.4 = (bf16[2,128,512]{2,1,0:T(8,128)(2,1)S(1)}, bf16[2,128,512]{2,1,0:T(8,128)(2,1)S(1)}, u32[]{:S(2)}, u32[]{:S(2)}) collective-permute-start(bf16[2,128,512]{2,1,0:T(8,128)(2,1)S(1)} %get-tuple-element.32), channel_id=1, source_target_pairs={{0,3},{1,2},{2,1},{3,0},{4,7},{5,6},{6,5},{7,4},{8,11},{9,10},{10,... | collective-permute-start | bytes 786440 | tf_op jit(solution)/shard_map/pairs1_cross/ppermute | solution.py:84
  8.2 11.6 %collective-permute-start = (bf16[256,512]{1,0:T(8,128)(2,1)S(1)}, bf16[256,512]{1,0:T(8,128)(2,1)S(1)}, u32[]{:S(2)}, u32[]{:S(2)}) collective-permute-start(bf16[256,512]{1,0:T(8,128)(2,1)S(1)} %half.1.refs_4_), channel_id=1, source_target_pairs={{0,4},{4,0},{8,12},{12,8},{16,20},{20,16},{24,28},{28,24},{1,5},{5... | collective-permute-start | bytes 786440 | tf_op jit(solution)/shard_map/swap_own/ppermute | solution.py:84
  12.7 8.6 %collective-permute-start.1 = (bf16[256,512]{1,0:T(8,128)(2,1)S(1)}, bf16[256,512]{1,0:T(8,128)(2,1)S(1)}, u32[]{:S(2)}, u32[]{:S(2)}) collective-permute-start(bf16[256,512]{1,0:T(8,128)(2,1)S(1)} %half.1.refs_4_), channel_id=1, source_target_pairs={{0,24},{4,28},{8,0},{12,4},{16,8},{20,12},{24,16},{28,20},{1,25},{... | collective-permute-start | bytes 786440 | tf_op jit(solution)/shard_map/back1/ppermute | solution.py:84
  16.8 12.3 %collective-permute-start.12 = (bf16[256,512]{1,0:T(8,128)(2,1)S(1)}, bf16[256,512]{1,0:T(8,128)(2,1)S(1)}, u32[]{:S(2)}, u32[]{:S(2)}) collective-permute-start(bf16[256,512]{1,0:T(8,128)(2,1)S(1)} %collective-permute-done.11.refs_6_), channel_id=1, source_target_pairs={{0,4},{4,0},{8,12},{12,8},{16,20},{20,16},{24,28},{28,24},{1,5},{5... | collective-permute-start | bytes 786440 | tf_op jit(solution)/shard_map/swap_ahead1/ppermute | solution.py:84
  18.3 7.0 %collective-permute-start.5 = (bf16[1,128,512]{2,1,0:T(8,128)(2,1)S(1)}, bf16[1,128,512]{2,1,0:T(8,128)(2,1)S(1)}, u32[]{:S(2)}, u32[]{:S(2)}) collective-permute-start(bf16[1,128,512]{2,1,0:T(8,128)(2,1)S(1)} %get-tuple-element.34), channel_id=1, source_target_pairs={{0,2},{1,3},{2,0},{3,1},{4,6},{5,7},{6,4},{7,5},{8,10},{9,11},{10,... | collective-permute-start | bytes 393224 | tf_op jit(solution)/shard_map/queries1_same/ppermute | solution.py:84
  19.9 7.0 %collective-permute-start.6 = (bf16[1,128,512]{2,1,0:T(8,128)(2,1)S(1)}, bf16[1,128,512]{2,1,0:T(8,128)(2,1)S(1)}, u32[]{:S(2)}, u32[]{:S(2)}) collective-permute-start(bf16[1,128,512]{2,1,0:T(8,128)(2,1)S(1)} %get-tuple-element.37), channel_id=1, source_target_pairs={{0,3},{1,2},{2,1},{3,0},{4,7},{5,6},{6,5},{7,4},{8,11},{9,10},{10,... | collective-permute-start | bytes 393224 | tf_op jit(solution)/shard_map/queries1_cross/ppermute | solution.py:84
  21.3 9.9 %collective-permute-start.13 = (bf16[256,512]{1,0:T(8,128)(2,1)S(1)}, bf16[256,512]{1,0:T(8,128)(2,1)S(1)}, u32[]{:S(2)}, u32[]{:S(2)}) collective-permute-start(bf16[256,512]{1,0:T(8,128)(2,1)S(1)} %collective-permute-done.11.refs_6_), channel_id=1, source_target_pairs={{0,8},{4,12},{8,16},{12,20},{16,24},{20,28},{24,0},{28,4},{1,9},{5... | collective-permute-start | bytes 786440 | tf_op jit(solution)/shard_map/ahead2/ppermute | solution.py:84
  24.1 14.5 %copy-start.3 = (s32[8]{0:T(128)S(1)}, s32[8]{0:T(128)}, u32[]{:S(2)}) copy-start(s32[8]{0:T(128)} %bucket_ref.3) | copy-start | bytes 100
  24.1 8.5 %collective-permute-start.7 = (bf16[2,128,512]{2,1,0:T(8,128)(2,1)S(1)}, bf16[2,128,512]{2,1,0:T(8,128)(2,1)S(1)}, u32[]{:S(2)}, u32[]{:S(2)}) collective-permute-start(bf16[2,128,512]{2,1,0:T(8,128)(2,1)S(1)} %attend.2.refs_0_), channel_id=1, source_target_pairs={{0,2},{1,3},{2,0},{3,1},{4,6},{5,7},{6,4},{7,5},{8,10},{9,11},{10,... | collective-permute-start | bytes 786440 | tf_op jit(solution)/shard_map/attended0_to1/ppermute | solution.py:84
  25.4 7.8 %collective-permute-start.9 = (bf16[256,512]{1,0:T(8,128)(2,1)S(1)}, bf16[256,512]{1,0:T(8,128)(2,1)S(1)}, u32[]{:S(2)}, u32[]{:S(2)}) collective-permute-start(bf16[256,512]{1,0:T(8,128)(2,1)S(1)} %collective-permute-done.1.refs_8_), channel_id=1, source_target_pairs={{0,4},{4,0},{8,12},{12,8},{16,20},{20,16},{24,28},{28,24},{1,5},{5... | collective-permute-start | bytes 786440 | tf_op jit(solution)/shard_map/swap_back1/ppermute | solution.py:84
  29.1 8.2 %collective-permute-start.16 = (bf16[2,128,512]{2,1,0:T(8,128)(2,1)S(1)}, bf16[2,128,512]{2,1,0:T(8,128)(2,1)S(1)}, u32[]{:S(2)}, u32[]{:S(2)}) collective-permute-start(bf16[2,128,512]{2,1,0:T(8,128)(2,1)S(1)} %attend.3.refs_0_), channel_id=1, source_target_pairs={{0,2},{1,3},{2,0},{3,1},{4,6},{5,7},{6,4},{7,5},{8,10},{9,11},{10,... | collective-permute-start | bytes 786440 | tf_op jit(solution)/shard_map/attended1_to1/ppermute | solution.py:84
  31.2 7.4 %collective-permute-start.14 = (bf16[256,512]{1,0:T(8,128)(2,1)S(1)}, bf16[256,512]{1,0:T(8,128)(2,1)S(1)}, u32[]{:S(2)}, u32[]{:S(2)}) collective-permute-start(bf16[256,512]{1,0:T(8,128)(2,1)S(1)} %collective-permute-done.13.refs_10_), channel_id=1, source_target_pairs={{0,4},{4,0},{8,12},{12,8},{16,20},{20,16},{24,28},{28,24},{1,5},{5... | collective-permute-start | bytes 786440 | tf_op jit(solution)/shard_map/swap_ahead2/ppermute | solution.py:84
  32.6 6.0 %collective-permute-start.8 = (bf16[2,128,512]{2,1,0:T(8,128)(2,1)S(1)}, bf16[2,128,512]{2,1,0:T(8,128)(2,1)S(1)}, u32[]{:S(2)}, u32[]{:S(2)}) collective-permute-start(bf16[2,128,512]{2,1,0:T(8,128)(2,1)S(1)} %attend.3.refs_0_), channel_id=1, source_target_pairs={{0,1},{1,0},{2,3},{3,2},{4,5},{5,4},{6,7},{7,6},{8,9},{9,8},{10,11... | collective-permute-start | bytes 786440 | tf_op jit(solution)/shard_map/sibling0_for1/ppermute | solution.py:84
  33.1 5.5 %collective-permute-start.10 = (bf16[2,128,512]{2,1,0:T(8,128)(2,1)S(1)}, bf16[2,128,512]{2,1,0:T(8,128)(2,1)S(1)}, u32[]{:S(2)}, u32[]{:S(2)}) collective-permute-start(bf16[2,128,512]{2,1,0:T(8,128)(2,1)S(1)} %collective-permute-done.7.refs_2_), channel_id=1, source_target_pairs={{0,1},{1,0},{2,3},{3,2},{4,5},{5,4},{6,7},{7,6},{8,9},{9,8},{10,11... | collective-permute-start | bytes 786440 | tf_op jit(solution)/shard_map/sibling1_for1/ppermute | solution.py:84
  33.1 8.4 %collective-permute-start.15 = (bf16[2,128,512]{2,1,0:T(8,128)(2,1)S(1)}, bf16[2,128,512]{2,1,0:T(8,128)(2,1)S(1)}, u32[]{:S(2)}, u32[]{:S(2)}) collective-permute-start(bf16[2,128,512]{2,1,0:T(8,128)(2,1)S(1)} %attend.2.refs_0_), channel_id=1, source_target_pairs={{0,1},{1,0},{2,3},{3,2},{4,5},{5,4},{6,7},{7,6},{8,9},{9,8},{10,11... | collective-permute-start | bytes 786440 | tf_op jit(solution)/shard_map/sibling0_for0/ppermute | solution.py:84
  37.4 4.1 %collective-permute-start.17 = (bf16[2,128,512]{2,1,0:T(8,128)(2,1)S(1)}, bf16[2,128,512]{2,1,0:T(8,128)(2,1)S(1)}, u32[]{:S(2)}, u32[]{:S(2)}) collective-permute-start(bf16[2,128,512]{2,1,0:T(8,128)(2,1)S(1)} %collective-permute-done.16.refs_2_), channel_id=1, source_target_pairs={{0,1},{1,0},{2,3},{3,2},{4,5},{5,4},{6,7},{7,6},{8,9},{9,8},{10,11... | collective-permute-start | bytes 786440 | tf_op jit(solution)/shard_map/sibling1_for0/ppermute | solution.py:84
  40.0 5.6 %collective-permute-start.19 = (bf16[128,512]{1,0:T(8,128)(2,1)S(1)}, bf16[128,512]{1,0:T(8,128)(2,1)S(1)}, u32[]{:S(2)}, u32[]{:S(2)}) collective-permute-start(bf16[128,512]{1,0:T(8,128)(2,1)S(1)} %get-tuple-element.40), channel_id=1, source_target_pairs={{0,2},{1,3},{2,0},{3,1},{4,6},{5,7},{6,4},{7,5},{8,10},{9,11},{10,... | collective-permute-start | bytes 393224 | tf_op jit(solution)/shard_map/out1_same/ppermute | solution.py:84
  41.5 2.1 %copy-start.4 = (f32[1,256,512]{2,1,0:T(8,128)S(1)}, f32[1,256,512]{2,1,0:T(8,128)}, u32[]{:S(2)}) copy-start(f32[1,256,512]{2,1,0:T(8,128)} %param.16) | copy-start | bytes 1572868
  41.5 5.8 %collective-permute-start.20 = (bf16[128,512]{1,0:T(8,128)(2,1)S(1)}, bf16[128,512]{1,0:T(8,128)(2,1)S(1)}, u32[]{:S(2)}, u32[]{:S(2)}) collective-permute-start(bf16[128,512]{1,0:T(8,128)(2,1)S(1)} %get-tuple-element.46), channel_id=1, source_target_pairs={{0,3},{1,2},{2,1},{3,0},{4,7},{5,6},{6,5},{7,4},{8,11},{9,10},{10,... | collective-permute-start | bytes 393224 | tf_op jit(solution)/shard_map/out1_cross/ppermute | solution.py:84
  42.8 4.5 %collective-permute-start.18 = (bf16[128,512]{1,0:T(8,128)(2,1)S(1)}, bf16[128,512]{1,0:T(8,128)(2,1)S(1)}, u32[]{:S(2)}, u32[]{:S(2)}) collective-permute-start(bf16[128,512]{1,0:T(8,128)(2,1)S(1)} %get-tuple-element.45), channel_id=1, source_target_pairs={{0,1},{1,0},{2,3},{3,2},{4,5},{5,4},{6,7},{7,6},{8,9},{9,8},{10,11... | collective-permute-start | bytes 393224 | tf_op jit(solution)/shard_map/out_sibling/ppermute | solution.py:84
